TPU v7x, 32 devices: a whole 2x2x4 slice. The times are simulated.
32 devices in a mesh: grp: 4 (over y, x), inner: 8 (over z, core).
Axes of the slice: x: 2, y: 2, z: 4, core: 2. Of those that a mesh axis runs over, the one named last changes fastest.
Arguments:
- tokens: bfloat16 [512, 8192], P('inner', 'grp'), may hold values from -170 to 170
- norm_gain: bfloat16 [8192], P('grp'), may hold values from 0.5 to 2
- gate_up_weight: bfloat16 [2, 8192, 28672], P(None, 'grp', 'inner'), may hold values from -0.0625 to 0.0625
- down_weight: bfloat16 [28672, 8192], P('inner', 'grp'), may hold values from -0.03125 to 0.03125
- student_in: bfloat16 [512, 1024], P('grp'), may hold values from -6 to 6
- student_proj: bfloat16 [1024, 8192], P(None, 'inner'), may hold values from -0.1875 to 0.1875
Outputs:
- teacher_out: bfloat16 [512, 8192], P('inner', 'grp')
- grad_student: float32 [512, 1024], P('grp')
- grad_proj: float32 [1024, 8192], P(None, 'inner')
All inputs are finite; a program needn't handle non-finite values.
Results may differ from a plain program's by a relative error of at most 0.025.
Values may be sent and summed in bfloat16 or wider, within the bound.
No kernel may reach another device: no remote copies, remote signals or barrier semaphores. Data moves between devices by JAX's collectives and lax.ppermute only.
A program may use at most 128 MiB of HBM per device.

v0:
```python
import functools

import jax
import jax.numpy as jnp
from jax import lax
from jax.experimental import pallas as pl
from jax.experimental.pallas import tpu as pltpu
from jax.sharding import PartitionSpec as P


D = 8192
AXES = ("grp", "inner")
BF16 = jnp.bfloat16
F32 = jnp.float32
ROW_SHARES = (1, 2, 1)
COL_CHUNKS = 2
WEIGHT_PARTS = 2


def tile_of(extent, limit=1024):
    for tile in range(limit, 0, -128):
        if extent % tile == 0:
            return tile
    return extent


def cost(flops, nbytes):
    return pl.CostEstimate(flops=int(flops), bytes_accessed=int(nbytes), transcendentals=0)


def room(mebibytes):
    return pltpu.CompilerParams(vmem_limit_bytes=mebibytes << 20)


def whole_block(shape):
    return pl.BlockSpec(shape, lambda *at: (0,) * len(shape))


def scatter_list(order):
    blocks = [0]
    for bit in reversed(order):
        blocks = blocks + [block | (1 << bit) for block in blocks]
    return blocks


def gather_list(order):
    blocks = [0]
    for bit in order:
        blocks = blocks + [block ^ (1 << bit) for block in blocks]
    return blocks


def prepare_kernel(count, step, at_ref, *refs):
    pieces, gain_ref, out_ref = refs[:count], refs[count], refs[count + 1]
    gain = gain_ref[...].astype(F32)
    for offset in range(count):
        start = pl.multiple_of((at_ref[0] ^ offset) * step, step)
        out_ref[pl.ds(start, step), :] = (pieces[offset][...].astype(F32) * gain).astype(BF16)


def prepare(at, pieces, gain):
    count = len(pieces)
    step, width = pieces[0].shape
    return pl.pallas_call(
        functools.partial(prepare_kernel, count, step),
        grid=(1,),
        out_shape=jax.ShapeDtypeStruct((count * step, width), BF16),
        in_specs=[pl.BlockSpec(memory_space=pltpu.SMEM)]
        + [whole_block((step, width))] * count
        + [whole_block(gain.shape)],
        out_specs=whole_block((count * step, width)),
        cost_estimate=cost(count * step * width, 4 * count * step * width),
        name="prepare",
        compiler_params=room(8),
    )(at, *pieces, gain)


def up_kernel(block, blocks, parts, x_ref, *refs):
    w_refs, outs = refs[:parts], refs[parts:]
    part = w_refs[0].shape[0]
    total = 0.0
    for at, w_ref in enumerate(w_refs):
        total += jnp.dot(
            x_ref[:, at * part : (at + 1) * part], w_ref[...], preferred_element_type=F32
        )
    half = len(blocks) // 2
    for slot, at in enumerate(blocks):
        row = (slot % half) * block
        outs[slot // half][row : row + block, :] = total[at * block : (at + 1) * block, :].astype(
            BF16
        )


def up_product(x, weight, chunk, chunks, blocks):
    rows, depth = x.shape
    block = rows // len(blocks)
    width = weight.shape[2] // chunks
    tile = tile_of(width)
    tiles = width // tile
    half = jax.ShapeDtypeStruct((2, rows // 2, width), BF16)
    return pl.pallas_call(
        functools.partial(up_kernel, block, blocks, WEIGHT_PARTS),
        grid=(2, tiles),
        out_shape=[half] * 2,
        in_specs=[whole_block(x.shape)]
        + [
            pl.BlockSpec(
                (None, depth // WEIGHT_PARTS, tile),
                lambda k, n, at=at: (k, at, chunk * tiles + n),
            )
            for at in range(WEIGHT_PARTS)
        ],
        out_specs=[pl.BlockSpec((None, rows // 2, tile), lambda k, n: (k, 0, n))] * 2,
        cost_estimate=cost(4 * rows * depth * width, 4 * depth * width + 2 * rows * depth),
        name="up_product",
        compiler_params=room(44),
    )(x, *[weight] * WEIGHT_PARTS)


def add_kernel(keep_ref, arrived_ref, kept_ref, send_ref):
    rows = kept_ref.shape[0]
    total = keep_ref[...].astype(F32) + arrived_ref[...].astype(F32)
    kept_ref[...] = total[:rows]
    send_ref[...] = total[rows:].astype(BF16)


def add_halves(keep, arrived):
    _, rows, width = keep.shape
    whole = pl.BlockSpec((None, rows, width), lambda k: (k, 0, 0))
    half = pl.BlockSpec((None, rows // 2, width), lambda k: (k, 0, 0))
    return pl.pallas_call(
        add_kernel,
        grid=(2,),
        out_shape=[
            jax.ShapeDtypeStruct((2, rows // 2, width), F32),
            jax.ShapeDtypeStruct((2, rows // 2, width), BF16),
        ],
        in_specs=[whole] * 2,
        out_specs=[half] * 2,
        cost_estimate=cost(2 * rows * width, 14 * rows * width),
        name="add_halves",
        compiler_params=room(8),
    )(keep, arrived)


def squares_kernel(tokens_ref, out_ref):
    values = tokens_ref[...].astype(F32)
    total = jnp.sum(values * values, axis=1, keepdims=True)
    out_ref[...] = jnp.broadcast_to(total, out_ref.shape)


def row_squares(tokens):
    rows, width = tokens.shape
    return pl.pallas_call(
        squares_kernel,
        grid=(1,),
        out_shape=jax.ShapeDtypeStruct((rows, 128), F32),
        in_specs=[pl.BlockSpec((rows, width), lambda n: (0, 0))],
        out_specs=pl.BlockSpec((rows, 128), lambda n: (0, 0)),
        cost_estimate=cost(2 * rows * width, 2 * rows * width),
        name="row_squares",
        compiler_params=room(8),
    )(tokens)


def activate_kernel(cores, start, width, meta_ref, keep_ref, arrived_ref, *refs):
    squares, out_ref = refs[:cores], refs[cores]
    step = out_ref.shape[0] // cores
    for slot in range(cores):
        total = squares[0][start : start + step, :1]
        for offset in range(1, cores):
            other = squares[offset][start : start + step, :1]
            total = jnp.where((meta_ref[2] ^ slot) == offset, other, total)
        inverse = lax.rsqrt(total / width + 1e-05)
        rows = slice(slot * step, (slot + 1) * step)
        gate = (keep_ref[0, rows, :].astype(F32) + arrived_ref[0, rows, :].astype(F32)) * inverse
        up = (keep_ref[1, rows, :].astype(F32) + arrived_ref[1, rows, :].astype(F32)) * inverse
        out_ref[rows, :] = (jax.nn.silu(gate) * up).astype(BF16)


def activate(meta, keep, arrived, squares, start):
    _, rows, width = keep.shape
    tile = tile_of(width)
    both = pl.BlockSpec((2, rows, tile), lambda n: (0, 0, n))
    return pl.pallas_call(
        functools.partial(activate_kernel, len(squares), start, D),
        grid=(width // tile,),
        out_shape=jax.ShapeDtypeStruct((rows, width), BF16),
        in_specs=[pl.BlockSpec(memory_space=pltpu.SMEM), both, both]
        + [pl.BlockSpec(value.shape, lambda n: (0, 0)) for value in squares],
        out_specs=pl.BlockSpec((rows, tile), lambda n: (0, n)),
        cost_estimate=cost(10 * rows * width, 14 * rows * width),
        name="activate",
        compiler_params=room(8),
    )(meta, keep, arrived, *squares)


def join_kernel(near_ref, far_ref, out_ref):
    rows = near_ref.shape[0]
    out_ref[:rows, :] = near_ref[...]
    out_ref[rows:, :] = far_ref[...]


def join(near, far):
    rows, width = near.shape
    return pl.pallas_call(
        join_kernel,
        grid=(1,),
        out_shape=jax.ShapeDtypeStruct((2 * rows, width), near.dtype),
        in_specs=[pl.BlockSpec((rows, width), lambda n: (0, 0))] * 2,
        out_specs=pl.BlockSpec((2 * rows, width), lambda n: (0, 0)),
        cost_estimate=cost(rows * width, 8 * rows * width),
        name="join",
        compiler_params=room(8),
    )(near, far)


def down_kernel(block, step, blocks, parts, first, last, at_ref, near_ref, far_ref, *refs):
    w_refs, refs = refs[:parts], refs[parts:]
    if not first:
        before_ref, refs = refs[0], refs[1:]
    if last:
        keep_ref, send_ref, lhs_ref, total_ref = refs
    else:
        total_ref, lhs_ref = refs

    @pl.when(pl.program_id(0) == 0)
    def _():
        half = len(blocks) // 2
        for slot, at in enumerate(blocks):
            ref = far_ref if slot >= half else near_ref
            source = (slot % half) * block
            lhs_ref[at * block : (at + 1) * block, :] = ref[source : source + block, :]

    part = w_refs[0].shape[0]
    total = 0.0
    for at, w_ref in enumerate(w_refs):
        total += jnp.dot(
            lhs_ref[:, at * part : (at + 1) * part], w_ref[...], preferred_element_type=F32
        )
    if not first:
        total = total + before_ref[...]
    total_ref[...] = total
    if last:
        for slot in range(total.shape[0] // step):
            start = pl.multiple_of((at_ref[0] ^ slot) * step, step)
            rows = total_ref[pl.ds(start, step), :]
            row = (slot // 2) * step
            if slot % 2 == 0:
                keep_ref[row : row + step, :] = rows
            else:
                send_ref[row : row + step, :] = rows.astype(BF16)


def down_product(at, near, far, weight, chunk, chunks, step, blocks, before, last):
    rows = 2 * near.shape[0]
    depth = weight.shape[0] // chunks
    width = weight.shape[1]
    tile = tile_of(width)
    whole = pl.BlockSpec(near.shape, lambda n: (0, 0))
    full = pl.BlockSpec((rows, tile), lambda n: (0, n))
    half = pl.BlockSpec((rows // 2, tile), lambda n: (0, n))
    in_specs = [pl.BlockSpec(memory_space=pltpu.SMEM), whole, whole]
    parts = WEIGHT_PARTS
    for part in range(parts):
        in_specs.append(
            pl.BlockSpec((depth // parts, tile), lambda n, at=chunk * parts + part: (at, n))
        )
    operands = [at, near, far] + [weight] * parts
    if before is not None:
        in_specs.append(full)
        operands.append(before)
    scratch = [pltpu.VMEM((rows, depth), BF16)]
    if last:
        out_shape = [
            jax.ShapeDtypeStruct((rows // 2, width), F32),
            jax.ShapeDtypeStruct((rows // 2, width), BF16),
        ]
        out_specs = [half, half]
        scratch.append(pltpu.VMEM((rows, tile), F32))
    else:
        out_shape = jax.ShapeDtypeStruct((rows, width), F32)
        out_specs = full
    return pl.pallas_call(
        functools.partial(
            down_kernel, rows // len(blocks), step, blocks, parts, before is None, last
        ),
        grid=(width // tile,),
        out_shape=out_shape,
        in_specs=in_specs,
        out_specs=out_specs,
        scratch_shapes=scratch,
        cost_estimate=cost(2 * rows * depth * width, 2 * depth * width + 2 * rows * depth),
        name="down_product",
        compiler_params=room(14),
    )(*operands)


def split_kernel(count, keep_ref, arrived_ref, own_ref, *refs):
    step = own_ref.shape[0]
    own_ref[...] = keep_ref[:step, :] + arrived_ref[:step, :].astype(F32)
    for far in range(1, count):
        rows = slice(far * step, (far + 1) * step)
        refs[far - 1][...] = (keep_ref[rows, :] + arrived_ref[rows, :].astype(F32)).astype(BF16)


def split(keep, arrived, count):
    rows, width = keep.shape
    step = rows // count
    piece = jax.ShapeDtypeStruct((step, width), BF16)
    return pl.pallas_call(
        functools.partial(split_kernel, count),
        grid=(1,),
        out_shape=[jax.ShapeDtypeStruct((step, width), F32)] + [piece] * (count - 1),
        in_specs=[pl.BlockSpec((rows, width), lambda n: (0, 0))] * 2,
        out_specs=[pl.BlockSpec((step, width), lambda n: (0, 0))] * count,
        cost_estimate=cost(rows * width, 8 * rows * width),
        name="split",
        compiler_params=room(8),
    )(keep, arrived)


def take_kernel(meta_ref, rows_ref, out_ref):
    step = out_ref.shape[0]
    start = pl.multiple_of(meta_ref[2] * step, step)
    out_ref[...] = rows_ref[pl.ds(start, step), :]


def take_rows(meta, rows, step):
    return pl.pallas_call(
        take_kernel,
        grid=(1,),
        out_shape=jax.ShapeDtypeStruct((step, rows.shape[1]), rows.dtype),
        in_specs=[pl.BlockSpec(memory_space=pltpu.SMEM), whole_block(rows.shape)],
        out_specs=whole_block((step, rows.shape[1])),
        cost_estimate=cost(step, 4 * rows.size),
        name="take_rows",
        compiler_params=room(4),
    )(meta, rows)


def turn_kernel(near_ref, far_ref, out_ref):
    rows = near_ref.shape[0]
    out_ref[:, :rows] = near_ref[...].T
    out_ref[:, rows:] = far_ref[...].T


def turn(near, far):
    rows, width = near.shape
    return pl.pallas_call(
        turn_kernel,
        grid=(1,),
        out_shape=jax.ShapeDtypeStruct((width, 2 * rows), near.dtype),
        in_specs=[pl.BlockSpec((rows, width), lambda n: (0, 0))] * 2,
        out_specs=pl.BlockSpec((width, 2 * rows), lambda n: (0, 0)),
        cost_estimate=cost(rows * width, 8 * rows * width),
        name="turn",
        compiler_params=room(8),
    )(near, far)


def sum_kernel(own_ref, *refs):
    total = own_ref[...]
    for ref in refs[:-1]:
        total = total + ref[...].astype(F32)
    refs[-1][...] = total.astype(BF16)


def sum_rows(own, others):
    whole = pl.BlockSpec(own.shape, lambda n: (0, 0))
    return pl.pallas_call(
        sum_kernel,
        grid=(1,),
        out_shape=jax.ShapeDtypeStruct(own.shape, BF16),
        in_specs=[whole] * (1 + len(others)),
        out_specs=whole,
        cost_estimate=cost(own.size * len(others), 12 * own.size),
        name="sum_rows",
        compiler_params=room(8),
    )(own, *others)


def predict_kernel(rows_ref, proj_ref, other_ref, out_own_ref, out_other_ref):
    for weight, out in ((proj_ref, out_own_ref), (other_ref, out_other_ref)):
        out[...] = jnp.tanh(jnp.dot(rows_ref[...], weight[...], preferred_element_type=F32))


def predict(rows, proj, other):
    count, depth = rows.shape
    width = proj.shape[1]
    tile = tile_of(width, 512)
    weight = pl.BlockSpec((depth, tile), lambda n: (0, n))
    out = pl.BlockSpec((count, tile), lambda n: (0, n))
    return pl.pallas_call(
        predict_kernel,
        grid=(width // tile,),
        out_shape=[jax.ShapeDtypeStruct((count, width), F32)] * 2,
        in_specs=[pl.BlockSpec((count, depth), lambda n: (0, 0)), weight, weight],
        out_specs=[out, out],
        cost_estimate=cost(4 * count * depth * width, 4 * depth * width),
        name="predict",
        compiler_params=room(8),
    )(rows, proj, other)


def term_kernel(count, meta_ref, own_ref, other_ref, proj_ref, proj_other_ref, *refs):
    outs, total_ref = refs[:count], refs[count]
    contract = (((1,), (1,)), ((), ()))
    total = lax.dot_general(own_ref[...], proj_ref[...], contract, preferred_element_type=F32)
    total_ref[...] = total + lax.dot_general(
        other_ref[...], proj_other_ref[...], contract, preferred_element_type=F32
    )
    step = outs[0].shape[0]
    for far in range(count):
        start = pl.multiple_of((meta_ref[3] ^ far) * step, step)
        outs[far][...] = total_ref[pl.ds(start, step), :].astype(outs[far].dtype)


def student_term(meta, own, other, proj, proj_other, count):
    rows = own.shape[0]
    width = proj.shape[0]
    step = rows // count
    piece = jax.ShapeDtypeStruct((step, width), BF16)
    return pl.pallas_call(
        functools.partial(term_kernel, count),
        grid=(1,),
        out_shape=[jax.ShapeDtypeStruct((step, width), F32)] + [piece] * (count - 1),
        in_specs=[pl.BlockSpec(memory_space=pltpu.SMEM)]
        + [whole_block(own.shape)] * 2
        + [whole_block(proj.shape)] * 2,
        out_specs=[whole_block((step, width))] * count,
        scratch_shapes=[pltpu.VMEM((rows, width), F32)],
        cost_estimate=cost(4 * rows * proj.size, 4 * proj.size),
        name="student_term",
        compiler_params=room(14),
    )(meta, own, other, proj, proj_other)


def pre_kernel(starts, meta_ref, own_ref, other_ref, *refs):
    targets, out_refs = refs[: len(starts)], refs[len(starts) :]
    half = own_ref.shape[1]
    for offset, predicted_ref in enumerate((own_ref, other_ref)):
        column = pl.multiple_of((meta_ref[2] ^ offset) * half, half)
        for start, target_ref in zip(starts, targets):
            rows = slice(start, start + target_ref.shape[0])
            predicted = predicted_ref[rows, :]
            target = target_ref[:, pl.ds(column, half)].astype(F32)
            out_refs[offset][rows, :] = (
                (predicted - target) * (1.0 - predicted * predicted)
            ).astype(BF16)


def pre_gradient(meta, own, other, targets, starts):
    out = jax.ShapeDtypeStruct(own.shape, BF16)
    whole = pl.BlockSpec(own.shape, lambda n: (0, 0))
    return pl.pallas_call(
        functools.partial(pre_kernel, tuple(starts)),
        grid=(1,),
        out_shape=[out, out],
        in_specs=[pl.BlockSpec(memory_space=pltpu.SMEM), whole, whole]
        + [pl.BlockSpec(target.shape, lambda n: (0, 0)) for target in targets],
        out_specs=[whole, whole],
        cost_estimate=cost(8 * own.size, 16 * own.size),
        name="pre_gradient",
        compiler_params=room(8),
    )(meta, own, other, *targets)


def proj_kernel(rows, step, own_ref, other_ref, *refs):
    pieces, out_ref, rhs_ref = refs[: len(rows)], refs[len(rows)], refs[len(rows) + 1]
    for places, ref in zip(rows, pieces):
        for slot, at in enumerate(places):
            rhs_ref[at * step : (at + 1) * step, :] = ref[slot * step : (slot + 1) * step, :]
    half = own_ref.shape[1]
    out_ref[...] = jnp.dot(
        own_ref[...], rhs_ref[:half, :], preferred_element_type=F32
    ) + jnp.dot(other_ref[...], rhs_ref[half:, :], preferred_element_type=F32)


def proj_product(own, other, pieces, places, step):
    rows, depth = own.shape
    width = pieces[0].shape[1]
    tile = tile_of(width, 256)
    lhs = pl.BlockSpec((rows, depth), lambda n: (0, 0))
    return pl.pallas_call(
        functools.partial(proj_kernel, places, step),
        grid=(width // tile,),
        out_shape=jax.ShapeDtypeStruct((rows, width), F32),
        in_specs=[lhs, lhs]
        + [pl.BlockSpec((piece.shape[0], tile), lambda n: (0, n)) for piece in pieces],
        out_specs=pl.BlockSpec((rows, tile), lambda n: (0, n)),
        scratch_shapes=[pltpu.VMEM((2 * depth, tile), BF16)],
        cost_estimate=cost(4 * rows * depth * width, 4 * rows * width + 4 * rows * depth),
        name="proj_product",
        compiler_params=room(8),
    )(own, other, *pieces)


def place_kernel(count, step, cores, at_ref, *refs):
    pieces, out_ref = refs[:count], refs[count]
    for offset in range(count):
        source = at_ref[1] ^ offset
        slot = (source & (cores - 1)) * (count // cores) + (source >> (cores.bit_length() - 1))
        start = pl.multiple_of(slot * step, step)
        out_ref[pl.ds(start, step), :] = pieces[offset][...].astype(F32)


def place(at, pieces, cores):
    count = len(pieces)
    step, width = pieces[0].shape
    return pl.pallas_call(
        functools.partial(place_kernel, count, step, cores),
        grid=(1,),
        out_shape=jax.ShapeDtypeStruct((count * step, width), F32),
        in_specs=[pl.BlockSpec(memory_space=pltpu.SMEM)] + [whole_block((step, width))] * count,
        out_specs=whole_block((count * step, width)),
        cost_estimate=cost(count * step * width, 6 * count * step * width),
        name="place",
        compiler_params=room(4),
    )(at, *pieces)


def shards(tokens, norm_gain, gate_up_weight, down_weight, student_in, student_proj):
    groups = lax.axis_size("grp")
    inner = lax.axis_size("inner")
    cores = inner // groups
    depth = inner // 2
    g = lax.axis_index("grp")
    i = lax.axis_index("inner")
    c = i & (cores - 1)
    b = i >> (cores.bit_length() - 1)
    local_rows = tokens.shape[0]
    meta = jnp.stack([i ^ (cores * g), i, c, b]).astype(jnp.int32)
    meta, tokens = lax.optimization_barrier((meta, tokens))

    places = [(x, y) for x in range(groups) for y in range(inner)]

    def move(value, target):
        pairs = []
        for x, y in places:
            to_x, to_y = target(x, y)
            pairs.append((x * inner + y, to_x * inner + to_y))
        return lax.ppermute(value, AXES, pairs)

    def over_grp(value, mask):
        return move(value, lambda x, y: (x ^ mask, y))

    def over_inner(value, mask):
        return move(value, lambda x, y: (x, y ^ mask))

    def transpose(value):
        return move(value, lambda x, y: (y // cores, x * cores + y % cores))

    bits = list(range(groups.bit_length() - 1))
    orders = (bits, bits[::-1])

    def gather(value, order):
        for bit in order[:-1]:
            arrived = over_grp(value, 1 << bit)
            value = join(value, arrived)
        return value, over_grp(value, 1 << order[-1])

    share_total = sum(ROW_SHARES)
    steps = [local_rows * share // share_total for share in ROW_SHARES]
    starts = [sum(steps[:r]) for r in range(len(steps))]

    total = row_squares(tokens)
    for bit in bits:
        total = total + over_grp(total, 1 << bit)
    total = transpose(total)
    squares = [total] + [over_inner(total, offset) for offset in range(1, cores)]

    gain = norm_gain[None, :]

    def gather_rows(r):
        own = tokens[starts[r] : starts[r] + steps[r]]
        pieces = [None] * inner
        pieces[0] = own
        for far in range(1, depth):
            pieces[2 * far] = over_inner(own, 2 * far)
        for far in range(depth):
            pieces[2 * far + 1] = over_inner(pieces[2 * far], 1)
        return pieces

    proj_other = over_inner(student_proj, 1)
    student_own = take_rows(meta, student_in, local_rows)
    near, far_rows = gather(student_own, bits)
    student_cols = turn(near, far_rows)
    student_cols_other = over_inner(student_cols, 1)
    predicted_own, predicted_other = predict(student_own, student_proj, proj_other)

    teacher_parts = []
    target_parts = []
    for r, step in enumerate(steps):
        x = prepare(meta, gather_rows(r), gain)
        if r == len(steps) - 1:
            x, predicted_own, predicted_other = lax.optimization_barrier(
                (x, predicted_own, predicted_other)
            )
        before = None
        for chunk in range(COL_CHUNKS):
            u = r * COL_CHUNKS + chunk
            order = orders[u % 2]
            keep, send = up_product(
                x, gate_up_weight, chunk, COL_CHUNKS, scatter_list(order)
            )
            for stage, bit in enumerate(order):
                arrived = over_grp(send, 1 << bit)
                if stage < len(order) - 1:
                    keep, send = add_halves(keep, arrived)
            hidden = activate(meta, keep, arrived, squares, starts[r])
            near, far_rows = gather(hidden, order)
            last = chunk == COL_CHUNKS - 1
            before = down_product(
                meta,
                near,
                far_rows,
                down_weight,
                chunk,
                COL_CHUNKS,
                step,
                gather_list(order),
                before,
                last,
            )
        keep, send = before
        result, *sends = split(keep, over_inner(send, 1), depth)
        result = sum_rows(
            result,
            [over_inner(sends[far - 1], 2 * far) for far in range(1, depth)],
        )
        teacher_parts.append(result)
        target_parts.append(transpose(result))

    teacher_out = jnp.concatenate(teacher_parts, axis=0)
    pre_own, pre_other = pre_gradient(meta, predicted_own, predicted_other, target_parts, starts)
    pre_here = over_inner(pre_other, 1)

    own, *sends = student_term(meta, pre_own, pre_other, student_proj, proj_other, depth)
    total = sum_rows(own, [over_inner(sends[far - 1], 2 * far) for far in range(1, depth)])
    pieces = [None] * inner
    pieces[0] = total
    for far in range(1, depth):
        pieces[2 * far] = over_inner(total, 2 * far)
    for far in range(depth):
        pieces[2 * far + 1] = over_inner(pieces[2 * far], 1)
    grad_student = place(meta, pieces, cores)

    pre_pieces = []
    pre_places = []
    for half, value in enumerate((pre_own, pre_here)):
        pre_pieces.extend(gather(value, orders[half]))
        blocks = [half * groups + block for block in gather_list(orders[half])]
        pre_places.extend((blocks[: groups // 2], blocks[groups // 2 :]))
    grad_proj = proj_product(
        student_cols, student_cols_other, pre_pieces, pre_places, local_rows
    )
    return (teacher_out, grad_student, grad_proj)


def solution(mesh):
    return jax.shard_map(
        shards,
        mesh=mesh,
        in_specs=(
            P("inner", "grp"),
            P("grp"),
            P(None, "grp", "inner"),
            P("inner", "grp"),
            P("grp", None),
            P(None, "inner"),
        ),
        out_specs=(P("inner", "grp"), P("grp", None), P(None, "inner")),
        check_vma=False,
    )
```

profile of v0, /device:TPU:0, one launch (start us, length us, event | category | flops | bytes accessed | tf_op | source)
XLA Modules:
  0.0 277.6 jit_solution(2547043721086339566)
XLA Ops:
  1.6 5.1 %collective-permute-start.28 = (bf16[32,2048]{1,0:T(8,128)(2,1)S(1)}, bf16[32,2048]{1,0:T(8,128)(2,1)S(1)}, u32[]{:S(2)}, u32[]{:S(2)}) collective-permute-start(bf16[32,2048]{1,0:T(8,128)(2,1)S(1)} %slice.10.refs_0_), channel_id=1, source_target_pairs={{0,6},{1,7},{2,4},{3,5},{4,2},{5,3},{6,0},{7,1},{8,14},{9,15},{10,... | collective-permute-start | bytes 393224 | tf_op jit(solution)/shard_map/ppermute | solution.py:543
  7.4 3.8 %collective-permute-done.28.refs_6_ = bf16[32,2048]{1,0:T(8,128)(2,1)S(1)} collective-permute-done((bf16[32,2048]{1,0:T(8,128)(2,1)S(1)}, bf16[32,2048]{1,0:T(8,128)(2,1)S(1)}, u32[]{:S(2)}, u32[]{:S(2)}) %collective-permute-start.28) | collective-permute-done | bytes 131104 | tf_op jit(solution)/shard_map/ppermute | solution.py:543
  11.2 6.6 %collective-permute-done.26.refs_4_ = bf16[32,2048]{1,0:T(8,128)(2,1)S(1)} collective-permute-done((bf16[32,2048]{1,0:T(8,128)(2,1)S(1)}, bf16[32,2048]{1,0:T(8,128)(2,1)S(1)}, u32[]{:S(2)}, u32[]{:S(2)}) %collective-permute-start.26) | collective-permute-done | bytes 131104 | tf_op jit(solution)/shard_map/ppermute | solution.py:543
  20.1 8.2 %up_product.8 = (bf16[2,128,1792]{2,1,0:T(8,128)(2,1)S(1)}, bf16[2,128,1792]{2,1,0:T(8,128)(2,1)S(1)}) custom-call(bf16[256,2048]{1,0:T(8,128)(2,1)S(1)} %prepare.4.x_ref, bf16[2,2048,3584]{2,1,0:T(8,128)(2,1)} %refs_1_.21, bf16[2,2048,3584]{2,1,0:T(8,128)(2,1)} %refs_1_.21), custom_call_target="tpu_custom_call" | custom-call | flops 3758096384 | bytes 15728640 | tf_op jit(solution)/shard_map/up_product/pallas_call | solution.py:101
  28.4 1.6 collective-permute-start.30
  30.0 8.2 %up_product.9 = (bf16[2,128,1792]{2,1,0:T(8,128)(2,1)S(1)}, bf16[2,128,1792]{2,1,0:T(8,128)(2,1)S(1)}) custom-call(bf16[256,2048]{1,0:T(8,128)(2,1)S(1)} %prepare.4.x_ref, bf16[2,2048,3584]{2,1,0:T(8,128)(2,1)} %refs_1_.21, bf16[2,2048,3584]{2,1,0:T(8,128)(2,1)} %refs_1_.21), custom_call_target="tpu_custom_call" | custom-call | flops 3758096384 | bytes 15728640 | tf_op jit(solution)/shard_map/up_product/pallas_call | solution.py:101
  38.2 1.6 collective-permute-start.34
  40.4 2.5 collective-permute-start.5
  43.0 18.3 %collective-permute-done.9 = f32[64,128]{1,0:T(8,128)S(1)} collective-permute-done((f32[64,128]{1,0:T(8,128)S(1)}, f32[64,128]{1,0:T(8,128)S(1)}, u32[]{:S(2)}, u32[]{:S(2)}) %collective-permute-start.9) | collective-permute-done | bytes 32800 | tf_op jit(solution)/shard_map/ppermute | solution.py:543
  61.7 3.4 %collective-permute-done.10 = f32[64,128]{1,0:T(8,128)S(1)} collective-permute-done((f32[64,128]{1,0:T(8,128)S(1)}, f32[64,128]{1,0:T(8,128)S(1)}, u32[]{:S(2)}, u32[]{:S(2)}) %collective-permute-start.10) | collective-permute-done | bytes 32800 | tf_op jit(solution)/shard_map/ppermute | solution.py:543
  65.2 3.0 %collective-permute-start.1 = (bf16[16,2048]{1,0:T(8,128)(2,1)S(1)}, bf16[16,2048]{1,0:T(8,128)(2,1)S(1)}, u32[]{:S(2)}, u32[]{:S(2)}) collective-permute-start(bf16[16,2048]{1,0:T(8,128)(2,1)S(1)} %get-tuple-element.113.refs_0_), channel_id=1, source_target_pairs={{0,2},{1,3},{2,0},{3,1},{4,6},{5,7},{6,4},{7,5},{8,10},{9,11},{10,... | collective-permute-start | bytes 196616 | tf_op jit(solution)/shard_map/ppermute | solution.py:543
  68.2 2.5 collective-permute-done.3.refs_4_
  71.1 1.7 collective-permute-start.47
  73.9 3.9 %collective-permute-done.47.refs_6_ = bf16[16,2048]{1,0:T(8,128)(2,1)S(1)} collective-permute-done((bf16[16,2048]{1,0:T(8,128)(2,1)S(1)}, bf16[16,2048]{1,0:T(8,128)(2,1)S(1)}, u32[]{:S(2)}, u32[]{:S(2)}) %collective-permute-start.47) | collective-permute-done | bytes 65568 | tf_op jit(solution)/shard_map/ppermute | solution.py:543
  77.8 2.2 collective-permute-start.43
  83.1 7.0 %collective-permute-start.31 = (bf16[2,64,1792]{2,1,0:T(8,128)(2,1)S(1)}, bf16[2,64,1792]{2,1,0:T(8,128)(2,1)S(1)}, u32[]{:S(2)}, u32[]{:S(2)}) collective-permute-start(bf16[2,64,1792]{2,1,0:T(8,128)(2,1)S(1)} %get-tuple-element.77), channel_id=1, source_target_pairs={{0,8},{1,9},{2,10},{3,11},{4,12},{5,13},{6,14},{7,15},{8,0},{9,1},... | collective-permute-start | bytes 1376264 | tf_op jit(solution)/shard_map/ppermute | solution.py:543
  90.3 2.7 collective-permute-start.35
  94.8 7.7 %up_product.6 = (bf16[2,64,1792]{2,1,0:T(8,128)(2,1)S(1)}, bf16[2,64,1792]{2,1,0:T(8,128)(2,1)}) custom-call(bf16[128,2048]{1,0:T(8,128)(2,1)S(1)} %prepare.3.x_ref, bf16[2,2048,3584]{2,1,0:T(8,128)(2,1)} %refs_1_.21, bf16[2,2048,3584]{2,1,0:T(8,128)(2,1)} %refs_1_.21), custom_call_target="tpu_custom_call" | custom-call | flops 1879048192 | bytes 15204352 | tf_op jit(solution)/shard_map/up_product/pallas_call | solution.py:101
  103.5 7.7 %up_product.7 = (bf16[2,64,1792]{2,1,0:T(8,128)(2,1)S(1)}, bf16[2,64,1792]{2,1,0:T(8,128)(2,1)}) custom-call(bf16[128,2048]{1,0:T(8,128)(2,1)S(1)} %prepare.3.x_ref, bf16[2,2048,3584]{2,1,0:T(8,128)(2,1)} %refs_1_.21, bf16[2,2048,3584]{2,1,0:T(8,128)(2,1)} %refs_1_.21), custom_call_target="tpu_custom_call" | custom-call | flops 1879048192 | bytes 15204352 | tf_op jit(solution)/shard_map/up_product/pallas_call | solution.py:101
  114.1 2.0 collective-permute-start.32
  116.1 1.6 activate.9.near_ref
  117.7 2.0 collective-permute-start.36
  119.7 1.3 predict.1
  122.4 7.6 %up_product.10 = (bf16[2,64,1792]{2,1,0:T(8,128)(2,1)S(1)}, bf16[2,64,1792]{2,1,0:T(8,128)(2,1)}) custom-call(bf16[128,2048]{1,0:T(8,128)(2,1)S(1)} %prepare.5.x_ref, bf16[2,2048,3584]{2,1,0:T(8,128)(2,1)} %refs_1_.21, bf16[2,2048,3584]{2,1,0:T(8,128)(2,1)} %refs_1_.21), custom_call_target="tpu_custom_call" | custom-call | flops 1879048192 | bytes 15204352 | tf_op jit(solution)/shard_map/up_product/pallas_call | solution.py:101
  131.0 8.5 %up_product.11 = (bf16[2,64,1792]{2,1,0:T(8,128)(2,1)S(1)}, bf16[2,64,1792]{2,1,0:T(8,128)(2,1)}) custom-call(bf16[128,2048]{1,0:T(8,128)(2,1)S(1)} %prepare.5.x_ref, bf16[2,2048,3584]{2,1,0:T(8,128)(2,1)} %refs_1_.21, bf16[2,2048,3584]{2,1,0:T(8,128)(2,1)} %refs_1_.21), custom_call_target="tpu_custom_call" | custom-call | flops 1879048192 | bytes 15204352 | tf_op jit(solution)/shard_map/up_product/pallas_call | solution.py:101
  139.5 1.4 copy-done.9
  142.1 1.7 collective-permute-start.8
  144.9 2.7 collective-permute-start.37
  150.8 5.5 %collective-permute-done.8.arrived_ref = bf16[2,32,1792]{2,1,0:T(8,128)(2,1)S(1)} collective-permute-done((bf16[2,32,1792]{2,1,0:T(8,128)(2,1)S(1)}, bf16[2,32,1792]{2,1,0:T(8,128)(2,1)S(1)}, u32[]{:S(2)}, u32[]{:S(2)}) %collective-permute-start.8) | collective-permute-done | bytes 229408 | tf_op jit(solution)/shard_map/ppermute | solution.py:543
  157.4 4.0 %collective-permute-done.16.arrived_ref = bf16[2,32,1792]{2,1,0:T(8,128)(2,1)S(1)} collective-permute-done((bf16[2,32,1792]{2,1,0:T(8,128)(2,1)S(1)}, bf16[2,32,1792]{2,1,0:T(8,128)(2,1)S(1)}, u32[]{:S(2)}, u32[]{:S(2)}) %collective-permute-start.16) | collective-permute-done | bytes 229408 | tf_op jit(solution)/shard_map/ppermute | solution.py:543
  161.4 1.7 collective-permute-start.13
  165.7 1.6 collective-permute-start.51
  167.5 1.1 collective-permute-start.55
  168.6 3.5 %collective-permute-done.17.far_ref = bf16[32,1792]{1,0:T(8,128)(2,1)S(1)} collective-permute-done((bf16[32,1792]{1,0:T(8,128)(2,1)S(1)}, bf16[32,1792]{1,0:T(8,128)(2,1)S(1)}, u32[]{:S(2)}, u32[]{:S(2)}) %collective-permute-start.17) | collective-permute-done | bytes 114720 | tf_op jit(solution)/shard_map/ppermute | solution.py:543
  172.4 2.3 collective-permute-start.18
  174.8 3.5 %down_product.8.refs_2_ = f32[256,2048]{1,0:T(8,128)S(1)} custom-call(s32[4]{0:T(128)S(1)} %pad_add_fusion.at_ref.meta_ref, bf16[128,1792]{1,0:T(8,128)(2,1)S(1)} %join.12.near_ref, bf16[128,1792]{1,0:T(8,128)(2,1)S(1)} %collective-permute-done.37.far_ref, bf16[3584,2048]{1,0:T(8,128)(2,1)S(1)} %bitcast.5, bf16[3584,2048]{1,0:T(8,128)(2,1)S(1)} %bitcast.5), custom_call_target="tpu_custom_call" | custom-call | flops 1879048192 | bytes 8257536 | tf_op jit(solution)/shard_map/down_product/pallas_call | solution.py:284
  180.6 1.3 collective-permute-start.56
  181.9 3.7 %down_product.9 = (f32[128,2048]{1,0:T(8,128)S(1)}, bf16[128,2048]{1,0:T(8,128)(2,1)S(1)}) custom-call(s32[4]{0:T(128)S(1)} %pad_add_fusion.at_ref.meta_ref, bf16[128,1792]{1,0:T(8,128)(2,1)S(1)} %join.11.near_ref, bf16[128,1792]{1,0:T(8,128)(2,1)S(1)} %collective-permute-done.33.far_ref, bf16[3584,2048]{1,0:T(8,128)(2,1)S(1)} %bitcast.5, ...), custom_call_target="tpu_custom_call" | custom-call | flops 1879048192 | bytes 8257536 | tf_op jit(solution)/shard_map/down_product/pallas_call | solution.py:284
  185.7 2.0 collective-permute-start.57
  189.9 2.4 down_product.6.refs_2_
  192.3 2.5 down_product.7
  194.9 2.6 down_product.10.refs_2_
  198.3 2.5 down_product.11
  202.0 3.4 %collective-permute-start.41 = (bf16[32,2048]{1,0:T(8,128)(2,1)S(1)}, bf16[32,2048]{1,0:T(8,128)(2,1)S(1)}, u32[]{:S(2)}, u32[]{:S(2)}) collective-permute-start(bf16[32,2048]{1,0:T(8,128)(2,1)S(1)} %get-tuple-element.87), channel_id=1, source_target_pairs={{0,6},{1,7},{2,4},{3,5},{4,2},{5,3},{6,0},{7,1},{8,14},{9,15},{10,... | collective-permute-start | bytes 393224 | tf_op jit(solution)/shard_map/ppermute | solution.py:543
  206.0 2.1 collective-permute-done.39.refs_0_
  208.1 6.7 %collective-permute-done.40.refs_1_ = bf16[32,2048]{1,0:T(8,128)(2,1)S(1)} collective-permute-done((bf16[32,2048]{1,0:T(8,128)(2,1)S(1)}, bf16[32,2048]{1,0:T(8,128)(2,1)S(1)}, u32[]{:S(2)}, u32[]{:S(2)}) %collective-permute-start.40) | collective-permute-done | bytes 131104 | tf_op jit(solution)/shard_map/ppermute | solution.py:543
  215.7 2.9 %collective-permute-start.59 = (bf16[16,2048]{1,0:T(8,128)(2,1)S(1)}, bf16[16,2048]{1,0:T(8,128)(2,1)S(1)}, u32[]{:S(2)}, u32[]{:S(2)}) collective-permute-start(bf16[16,2048]{1,0:T(8,128)(2,1)S(1)} %get-tuple-element.102), channel_id=1, source_target_pairs={{0,2},{1,3},{2,0},{3,1},{4,6},{5,7},{6,4},{7,5},{8,10},{9,11},{10,... | collective-permute-start | bytes 196616 | tf_op jit(solution)/shard_map/ppermute | solution.py:543
  219.5 1.8 collective-permute-done.21.refs_1_
  221.3 1.2 collective-permute-start.61
  223.9 2.4 collective-permute-done.60.refs_1_
  226.2 1.2 collective-permute-done.61.refs_2_
  229.7 16.4 %collective-permute-start.78 = (bf16[64,1024]{1,0:T(8,128)(2,1)S(1)}, bf16[64,1024]{1,0:T(8,128)(2,1)S(1)}, u32[]{:S(2)}, u32[]{:S(2)}) collective-permute-start(bf16[64,1024]{1,0:T(8,128)(2,1)S(1)} %get-tuple-element.107.own_ref.near_ref), channel_id=1, source_target_pairs={{0,8},{1,9},{2,10},{3,11},{4,12},{5,13},{6,14},{7,15},{8,0},{9,1},... | collective-permute-start | bytes 393224 | tf_op jit(solution)/shard_map/ppermute | solution.py:543
  246.1 1.9 student_term.1
  248.1 2.8 %collective-permute-start.66 = (bf16[16,1024]{1,0:T(8,128)(2,1)S(1)}, bf16[16,1024]{1,0:T(8,128)(2,1)S(1)}, u32[]{:S(2)}, u32[]{:S(2)}) collective-permute-start(bf16[16,1024]{1,0:T(8,128)(2,1)S(1)} %get-tuple-element.111), channel_id=1, source_target_pairs={{0,4},{1,5},{2,6},{3,7},{4,0},{5,1},{6,2},{7,3},{8,12},{9,13},{10,... | collective-permute-start | bytes 98312 | tf_op jit(solution)/shard_map/ppermute | solution.py:543
  251.0 1.2 collective-permute-done.65.refs_0_
  252.2 2.4 collective-permute-start.67
  254.6 3.4 %collective-permute-done.67.refs_2_ = bf16[16,1024]{1,0:T(8,128)(2,1)S(1)} collective-permute-done((bf16[16,1024]{1,0:T(8,128)(2,1)S(1)}, bf16[16,1024]{1,0:T(8,128)(2,1)S(1)}, u32[]{:S(2)}, u32[]{:S(2)}) %collective-permute-start.67) | collective-permute-done | bytes 32800 | tf_op jit(solution)/shard_map/ppermute | solution.py:543
  257.9 2.4 collective-permute-start.73
  260.4 3.6 %collective-permute-done.73.refs_6_ = bf16[16,1024]{1,0:T(8,128)(2,1)S(1)} collective-permute-done((bf16[16,1024]{1,0:T(8,128)(2,1)S(1)}, bf16[16,1024]{1,0:T(8,128)(2,1)S(1)}, u32[]{:S(2)}, u32[]{:S(2)}) %collective-permute-start.73) | collective-permute-done | bytes 32800 | tf_op jit(solution)/shard_map/ppermute | solution.py:543
  266.2 1.6 collective-permute-done.69.refs_2_
  269.6 1.4 place.1
  271.0 1.8 collective-permute-done.79.refs_1_
  272.9 1.4 collective-permute-done.82.refs_3_
  274.2 3.4 %proj_product.1 = f32[1024,1024]{1,0:T(8,128)} custom-call(bf16[1024,256]{1,0:T(8,128)(2,1)S(1)} %turn.1.own_ref, bf16[1024,256]{1,0:T(8,128)(2,1)S(1)} %collective-permute-done.77.other_ref, bf16[128,1024]{1,0:T(8,128)(2,1)S(1)} %join.16.refs_0_, bf16[128,1024]{1,0:T(8,128)(2,1)S(1)} %collective-permute-done.79.refs_1_, ...), custom_call_target="tpu_custom_call" | custom-call | flops 1073741824 | bytes 5242880 | tf_op jit(solution)/shard_map/proj_product/pallas_call | solution.py:485
  (199 shorter events, 44.4 us)
Async XLA Ops:
  1.6 9.6 %collective-permute-start.28 = (bf16[32,2048]{1,0:T(8,128)(2,1)S(1)}, bf16[32,2048]{1,0:T(8,128)(2,1)S(1)}, u32[]{:S(2)}, u32[]{:S(2)}) collective-permute-start(bf16[32,2048]{1,0:T(8,128)(2,1)S(1)} %slice.10.refs_0_), channel_id=1, source_target_pairs={{0,6},{1,7},{2,4},{3,5},{4,2},{5,3},{6,0},{7,1},{8,14},{9,15},{10,... | collective-permute-start | bytes 393224 | tf_op jit(solution)/shard_map/ppermute | solution.py:543
  6.8 11.1 %collective-permute-start.26 = (bf16[32,2048]{1,0:T(8,128)(2,1)S(1)}, bf16[32,2048]{1,0:T(8,128)(2,1)S(1)}, u32[]{:S(2)}, u32[]{:S(2)}) collective-permute-start(bf16[32,2048]{1,0:T(8,128)(2,1)S(1)} %slice.10.refs_0_), channel_id=1, source_target_pairs={{0,4},{1,5},{2,6},{3,7},{4,0},{5,1},{6,2},{7,3},{8,12},{9,13},{10,... | collective-permute-start | bytes 393224 | tf_op jit(solution)/shard_map/ppermute | solution.py:543
  6.8 11.1 %collective-permute-start.24 = (bf16[32,2048]{1,0:T(8,128)(2,1)S(1)}, bf16[32,2048]{1,0:T(8,128)(2,1)S(1)}, u32[]{:S(2)}, u32[]{:S(2)}) collective-permute-start(bf16[32,2048]{1,0:T(8,128)(2,1)S(1)} %slice.10.refs_0_), channel_id=1, source_target_pairs={{0,2},{1,3},{2,0},{3,1},{4,6},{5,7},{6,4},{7,5},{8,10},{9,11},{10,... | collective-permute-start | bytes 393224 | tf_op jit(solution)/shard_map/ppermute | solution.py:543
  7.4 11.6 %collective-permute-start.23 = (bf16[32,2048]{1,0:T(8,128)(2,1)S(1)}, bf16[32,2048]{1,0:T(8,128)(2,1)S(1)}, u32[]{:S(2)}, u32[]{:S(2)}) collective-permute-start(bf16[32,2048]{1,0:T(8,128)(2,1)S(1)} %slice.10.refs_0_), channel_id=1, source_target_pairs={{0,1},{1,0},{2,3},{3,2},{4,5},{5,4},{6,7},{7,6},{8,9},{9,8},{10,11... | collective-permute-start | bytes 393224 | tf_op jit(solution)/shard_map/ppermute | solution.py:543
  11.2 7.8 %collective-permute-start.29 = (bf16[32,2048]{1,0:T(8,128)(2,1)S(1)}, bf16[32,2048]{1,0:T(8,128)(2,1)S(1)}, u32[]{:S(2)}, u32[]{:S(2)}) collective-permute-start(bf16[32,2048]{1,0:T(8,128)(2,1)S(1)} %collective-permute-done.28.refs_6_), channel_id=1, source_target_pairs={{0,1},{1,0},{2,3},{3,2},{4,5},{5,4},{6,7},{7,6},{8,9},{9,8},{10,11... | collective-permute-start | bytes 393224 | tf_op jit(solution)/shard_map/ppermute | solution.py:543
  18.4 101.3 %collective-permute-start.49 = (bf16[1024,1024]{1,0:T(8,128)(2,1)}, bf16[1024,1024]{1,0:T(8,128)(2,1)S(1)}, u32[]{:S(2)}, u32[]{:S(2)}) collective-permute-start(bf16[1024,1024]{1,0:T(8,128)(2,1)} %proj_ref.3), channel_id=1, source_target_pairs={{0,1},{1,0},{2,3},{3,2},{4,5},{5,4},{6,7},{7,6},{8,9},{9,8},{10,11... | collective-permute-start | bytes 6291464 | tf_op jit(solution)/shard_map/ppermute | solution.py:543
  28.4 54.4 %collective-permute-start.30 = (bf16[2,128,1792]{2,1,0:T(8,128)(2,1)S(1)}, bf16[2,128,1792]{2,1,0:T(8,128)(2,1)S(1)}, u32[]{:S(2)}, u32[]{:S(2)}) collective-permute-start(bf16[2,128,1792]{2,1,0:T(8,128)(2,1)S(1)} %get-tuple-element.75), channel_id=1, source_target_pairs={{0,16},{1,17},{2,18},{3,19},{4,20},{5,21},{6,22},{7,23},{8,24},{9,... | collective-permute-start | bytes 2752520 | tf_op jit(solution)/shard_map/ppermute | solution.py:543
  38.2 44.9 %collective-permute-start.34 = (bf16[2,128,1792]{2,1,0:T(8,128)(2,1)S(1)}, bf16[2,128,1792]{2,1,0:T(8,128)(2,1)S(1)}, u32[]{:S(2)}, u32[]{:S(2)}) collective-permute-start(bf16[2,128,1792]{2,1,0:T(8,128)(2,1)S(1)} %get-tuple-element.79), channel_id=1, source_target_pairs={{0,8},{1,9},{2,10},{3,11},{4,12},{5,13},{6,14},{7,15},{8,0},{9,1},... | collective-permute-start | bytes 2752520 | tf_op jit(solution)/shard_map/ppermute | solution.py:543
  39.9 21.4 %collective-permute-start.9 = (f32[64,128]{1,0:T(8,128)S(1)}, f32[64,128]{1,0:T(8,128)S(1)}, u32[]{:S(2)}, u32[]{:S(2)}) collective-permute-start(f32[64,128]{1,0:T(8,128)S(1)} %row_squares.1), channel_id=1, source_target_pairs={{0,8},{1,9},{2,10},{3,11},{4,12},{5,13},{6,14},{7,15},{8,0},{9,1},... | collective-permute-start | bytes 98312 | tf_op jit(solution)/shard_map/ppermute | solution.py:543
  40.4 24.8 %collective-permute-start.5 = (bf16[16,2048]{1,0:T(8,128)(2,1)S(1)}, bf16[16,2048]{1,0:T(8,128)(2,1)S(1)}, u32[]{:S(2)}, u32[]{:S(2)}) collective-permute-start(bf16[16,2048]{1,0:T(8,128)(2,1)S(1)} %get-tuple-element.113.refs_0_), channel_id=1, source_target_pairs={{0,6},{1,7},{2,4},{3,5},{4,2},{5,3},{6,0},{7,1},{8,14},{9,15},{10,... | collective-permute-start | bytes 196616 | tf_op jit(solution)/shard_map/ppermute | solution.py:543
  65.2 5.9 %collective-permute-start.1 = (bf16[16,2048]{1,0:T(8,128)(2,1)S(1)}, bf16[16,2048]{1,0:T(8,128)(2,1)S(1)}, u32[]{:S(2)}, u32[]{:S(2)}) collective-permute-start(bf16[16,2048]{1,0:T(8,128)(2,1)S(1)} %get-tuple-element.113.refs_0_), channel_id=1, source_target_pairs={{0,2},{1,3},{2,0},{3,1},{4,6},{5,7},{6,4},{7,5},{8,10},{9,11},{10,... | collective-permute-start | bytes 196616 | tf_op jit(solution)/shard_map/ppermute | solution.py:543
  71.1 6.7 %collective-permute-start.47 = (bf16[16,2048]{1,0:T(8,128)(2,1)S(1)}, bf16[16,2048]{1,0:T(8,128)(2,1)S(1)}, u32[]{:S(2)}, u32[]{:S(2)}) collective-permute-start(bf16[16,2048]{1,0:T(8,128)(2,1)S(1)} %get-tuple-element.114.refs_0_), channel_id=1, source_target_pairs={{0,6},{1,7},{2,4},{3,5},{4,2},{5,3},{6,0},{7,1},{8,14},{9,15},{10,... | collective-permute-start | bytes 196616 | tf_op jit(solution)/shard_map/ppermute | solution.py:543
  72.8 7.7 %collective-permute-start.45 = (bf16[16,2048]{1,0:T(8,128)(2,1)S(1)}, bf16[16,2048]{1,0:T(8,128)(2,1)S(1)}, u32[]{:S(2)}, u32[]{:S(2)}) collective-permute-start(bf16[16,2048]{1,0:T(8,128)(2,1)S(1)} %get-tuple-element.114.refs_0_), channel_id=1, source_target_pairs={{0,4},{1,5},{2,6},{3,7},{4,0},{5,1},{6,2},{7,3},{8,12},{9,13},{10,... | collective-permute-start | bytes 196616 | tf_op jit(solution)/shard_map/ppermute | solution.py:543
  82.3 8.1 %collective-permute-start.6 = (bf16[16,2048]{1,0:T(8,128)(2,1)S(1)}, bf16[16,2048]{1,0:T(8,128)(2,1)S(1)}, u32[]{:S(2)}, u32[]{:S(2)}) collective-permute-start(bf16[16,2048]{1,0:T(8,128)(2,1)S(1)} %collective-permute-done.5.refs_6_), channel_id=1, source_target_pairs={{0,1},{1,0},{2,3},{3,2},{4,5},{5,4},{6,7},{7,6},{8,9},{9,8},{10,11... | collective-permute-start | bytes 196616 | tf_op jit(solution)/shard_map/ppermute | solution.py:543
  82.3 10.7 %collective-permute-start.4 = (bf16[16,2048]{1,0:T(8,128)(2,1)S(1)}, bf16[16,2048]{1,0:T(8,128)(2,1)S(1)}, u32[]{:S(2)}, u32[]{:S(2)}) collective-permute-start(bf16[16,2048]{1,0:T(8,128)(2,1)S(1)} %collective-permute-done.3.refs_4_), channel_id=1, source_target_pairs={{0,1},{1,0},{2,3},{3,2},{4,5},{5,4},{6,7},{7,6},{8,9},{9,8},{10,11... | collective-permute-start | bytes 196616 | tf_op jit(solution)/shard_map/ppermute | solution.py:543
  82.8 10.2 %collective-permute-start.2 = (bf16[16,2048]{1,0:T(8,128)(2,1)S(1)}, bf16[16,2048]{1,0:T(8,128)(2,1)S(1)}, u32[]{:S(2)}, u32[]{:S(2)}) collective-permute-start(bf16[16,2048]{1,0:T(8,128)(2,1)S(1)} %collective-permute-done.1.refs_2_), channel_id=1, source_target_pairs={{0,1},{1,0},{2,3},{3,2},{4,5},{5,4},{6,7},{7,6},{8,9},{9,8},{10,11... | collective-permute-start | bytes 196616 | tf_op jit(solution)/shard_map/ppermute | solution.py:543
  83.1 30.1 %collective-permute-start.31 = (bf16[2,64,1792]{2,1,0:T(8,128)(2,1)S(1)}, bf16[2,64,1792]{2,1,0:T(8,128)(2,1)S(1)}, u32[]{:S(2)}, u32[]{:S(2)}) collective-permute-start(bf16[2,64,1792]{2,1,0:T(8,128)(2,1)S(1)} %get-tuple-element.77), channel_id=1, source_target_pairs={{0,8},{1,9},{2,10},{3,11},{4,12},{5,13},{6,14},{7,15},{8,0},{9,1},... | collective-permute-start | bytes 1376264 | tf_op jit(solution)/shard_map/ppermute | solution.py:543
  90.3 25.8 %collective-permute-start.35 = (bf16[2,64,1792]{2,1,0:T(8,128)(2,1)S(1)}, bf16[2,64,1792]{2,1,0:T(8,128)(2,1)S(1)}, u32[]{:S(2)}, u32[]{:S(2)}) collective-permute-start(bf16[2,64,1792]{2,1,0:T(8,128)(2,1)S(1)} %get-tuple-element.81), channel_id=1, source_target_pairs={{0,16},{1,17},{2,18},{3,19},{4,20},{5,21},{6,22},{7,23},{8,24},{9,... | collective-permute-start | bytes 1376264 | tf_op jit(solution)/shard_map/ppermute | solution.py:543
  94.3 9.0 %collective-permute-start.48 = (bf16[16,2048]{1,0:T(8,128)(2,1)S(1)}, bf16[16,2048]{1,0:T(8,128)(2,1)S(1)}, u32[]{:S(2)}, u32[]{:S(2)}) collective-permute-start(bf16[16,2048]{1,0:T(8,128)(2,1)S(1)} %collective-permute-done.47.refs_6_), channel_id=1, source_target_pairs={{0,1},{1,0},{2,3},{3,2},{4,5},{5,4},{6,7},{7,6},{8,9},{9,8},{10,11... | collective-permute-start | bytes 196616 | tf_op jit(solution)/shard_map/ppermute | solution.py:543
  94.4 8.9 %collective-permute-start.46 = (bf16[16,2048]{1,0:T(8,128)(2,1)S(1)}, bf16[16,2048]{1,0:T(8,128)(2,1)S(1)}, u32[]{:S(2)}, u32[]{:S(2)}) collective-permute-start(bf16[16,2048]{1,0:T(8,128)(2,1)S(1)} %collective-permute-done.45.refs_4_), channel_id=1, source_target_pairs={{0,1},{1,0},{2,3},{3,2},{4,5},{5,4},{6,7},{7,6},{8,9},{9,8},{10,11... | collective-permute-start | bytes 196616 | tf_op jit(solution)/shard_map/ppermute | solution.py:543
  103.2 8.7 %collective-permute-start.44 = (bf16[16,2048]{1,0:T(8,128)(2,1)S(1)}, bf16[16,2048]{1,0:T(8,128)(2,1)S(1)}, u32[]{:S(2)}, u32[]{:S(2)}) collective-permute-start(bf16[16,2048]{1,0:T(8,128)(2,1)S(1)} %collective-permute-done.43.refs_2_), channel_id=1, source_target_pairs={{0,1},{1,0},{2,3},{3,2},{4,5},{5,4},{6,7},{7,6},{8,9},{9,8},{10,11... | collective-permute-start | bytes 196616 | tf_op jit(solution)/shard_map/ppermute | solution.py:543
  103.4 36.1 %collective-permute-start.7 = (bf16[2,64,1792]{2,1,0:T(8,128)(2,1)}, bf16[2,64,1792]{2,1,0:T(8,128)(2,1)}, u32[]{:S(2)}, u32[]{:S(2)}) collective-permute-start(bf16[2,64,1792]{2,1,0:T(8,128)(2,1)} %get-tuple-element.61), channel_id=1, source_target_pairs={{0,16},{1,17},{2,18},{3,19},{4,20},{5,21},{6,22},{7,23},{8,24},{9,... | collective-permute-start | bytes 1376264 | tf_op jit(solution)/shard_map/ppermute | solution.py:543
  111.9 33.0 %collective-permute-start.15 = (bf16[2,64,1792]{2,1,0:T(8,128)(2,1)}, bf16[2,64,1792]{2,1,0:T(8,128)(2,1)}, u32[]{:S(2)}, u32[]{:S(2)}) collective-permute-start(bf16[2,64,1792]{2,1,0:T(8,128)(2,1)} %get-tuple-element.65), channel_id=1, source_target_pairs={{0,8},{1,9},{2,10},{3,11},{4,12},{5,13},{6,14},{7,15},{8,0},{9,1},... | collective-permute-start | bytes 1376264 | tf_op jit(solution)/shard_map/ppermute | solution.py:543
  114.1 35.6 %collective-permute-start.32 = (bf16[64,1792]{1,0:T(8,128)(2,1)S(1)}, bf16[64,1792]{1,0:T(8,128)(2,1)}, u32[]{:S(2)}, u32[]{:S(2)}) collective-permute-start(bf16[64,1792]{1,0:T(8,128)(2,1)S(1)} %activate.8.near_ref), channel_id=1, source_target_pairs={{0,16},{1,17},{2,18},{3,19},{4,20},{5,21},{6,22},{7,23},{8,24},{9,... | collective-permute-start | bytes 688136 | tf_op jit(solution)/shard_map/ppermute | solution.py:543
  117.7 24.4 %collective-permute-start.36 = (bf16[64,1792]{1,0:T(8,128)(2,1)}, bf16[64,1792]{1,0:T(8,128)(2,1)}, u32[]{:S(2)}, u32[]{:S(2)}) collective-permute-start(bf16[64,1792]{1,0:T(8,128)(2,1)} %activate.9.near_ref), channel_id=1, source_target_pairs={{0,8},{1,9},{2,10},{3,11},{4,12},{5,13},{6,14},{7,15},{8,0},{9,1},... | collective-permute-start | bytes 688136 | tf_op jit(solution)/shard_map/ppermute | solution.py:543
  130.8 33.2 %collective-permute-start.50 = (bf16[2,64,1792]{2,1,0:T(8,128)(2,1)}, bf16[2,64,1792]{2,1,0:T(8,128)(2,1)}, u32[]{:S(2)}, u32[]{:S(2)}) collective-permute-start(bf16[2,64,1792]{2,1,0:T(8,128)(2,1)} %get-tuple-element.92), channel_id=1, source_target_pairs={{0,16},{1,17},{2,18},{3,19},{4,20},{5,21},{6,22},{7,23},{8,24},{9,... | collective-permute-start | bytes 1376264 | tf_op jit(solution)/shard_map/ppermute | solution.py:543
  139.5 26.3 %collective-permute-start.54 = (bf16[2,64,1792]{2,1,0:T(8,128)(2,1)}, bf16[2,64,1792]{2,1,0:T(8,128)(2,1)S(1)}, u32[]{:S(2)}, u32[]{:S(2)}) collective-permute-start(bf16[2,64,1792]{2,1,0:T(8,128)(2,1)} %get-tuple-element.96), channel_id=1, source_target_pairs={{0,8},{1,9},{2,10},{3,11},{4,12},{5,13},{6,14},{7,15},{8,0},{9,1},... | collective-permute-start | bytes 1376264 | tf_op jit(solution)/shard_map/ppermute | solution.py:543
  142.1 14.2 %collective-permute-start.8 = (bf16[2,32,1792]{2,1,0:T(8,128)(2,1)S(1)}, bf16[2,32,1792]{2,1,0:T(8,128)(2,1)S(1)}, u32[]{:S(2)}, u32[]{:S(2)}) collective-permute-start(bf16[2,32,1792]{2,1,0:T(8,128)(2,1)S(1)} %get-tuple-element.63), channel_id=1, source_target_pairs={{0,8},{1,9},{2,10},{3,11},{4,12},{5,13},{6,14},{7,15},{8,0},{9,1},... | collective-permute-start | bytes 688136 | tf_op jit(solution)/shard_map/ppermute | solution.py:543
  144.9 27.6 %collective-permute-start.37 = (bf16[128,1792]{1,0:T(8,128)(2,1)S(1)}, bf16[128,1792]{1,0:T(8,128)(2,1)S(1)}, u32[]{:S(2)}, u32[]{:S(2)}) collective-permute-start(bf16[128,1792]{1,0:T(8,128)(2,1)S(1)} %join.12.near_ref), channel_id=1, source_target_pairs={{0,16},{1,17},{2,18},{3,19},{4,20},{5,21},{6,22},{7,23},{8,24},{9,... | collective-permute-start | bytes 1376264 | tf_op jit(solution)/shard_map/ppermute | solution.py:543
  149.7 11.7 %collective-permute-start.16 = (bf16[2,32,1792]{2,1,0:T(8,128)(2,1)S(1)}, bf16[2,32,1792]{2,1,0:T(8,128)(2,1)S(1)}, u32[]{:S(2)}, u32[]{:S(2)}) collective-permute-start(bf16[2,32,1792]{2,1,0:T(8,128)(2,1)S(1)} %get-tuple-element.67), channel_id=1, source_target_pairs={{0,16},{1,17},{2,18},{3,19},{4,20},{5,21},{6,22},{7,23},{8,24},{9,... | collective-permute-start | bytes 688136 | tf_op jit(solution)/shard_map/ppermute | solution.py:543
  156.3 25.7 %collective-permute-start.33 = (bf16[128,1792]{1,0:T(8,128)(2,1)S(1)}, bf16[128,1792]{1,0:T(8,128)(2,1)S(1)}, u32[]{:S(2)}, u32[]{:S(2)}) collective-permute-start(bf16[128,1792]{1,0:T(8,128)(2,1)S(1)} %join.11.near_ref), channel_id=1, source_target_pairs={{0,8},{1,9},{2,10},{3,11},{4,12},{5,13},{6,14},{7,15},{8,0},{9,1},... | collective-permute-start | bytes 1376264 | tf_op jit(solution)/shard_map/ppermute | solution.py:543
  161.4 6.0 %collective-permute-start.13 = (bf16[32,1792]{1,0:T(8,128)(2,1)S(1)}, bf16[32,1792]{1,0:T(8,128)(2,1)S(1)}, u32[]{:S(2)}, u32[]{:S(2)}) collective-permute-start(bf16[32,1792]{1,0:T(8,128)(2,1)S(1)} %activate.6.near_ref), channel_id=1, source_target_pairs={{0,16},{1,17},{2,18},{3,19},{4,20},{5,21},{6,22},{7,23},{8,24},{9,... | collective-permute-start | bytes 344072 | tf_op jit(solution)/shard_map/ppermute | solution.py:543
  164.0 8.1 %collective-permute-start.17 = (bf16[32,1792]{1,0:T(8,128)(2,1)S(1)}, bf16[32,1792]{1,0:T(8,128)(2,1)S(1)}, u32[]{:S(2)}, u32[]{:S(2)}) collective-permute-start(bf16[32,1792]{1,0:T(8,128)(2,1)S(1)} %activate.7.near_ref), channel_id=1, source_target_pairs={{0,8},{1,9},{2,10},{3,11},{4,12},{5,13},{6,14},{7,15},{8,0},{9,1},... | collective-permute-start | bytes 344072 | tf_op jit(solution)/shard_map/ppermute | solution.py:543
  165.7 12.5 %collective-permute-start.51 = (bf16[2,32,1792]{2,1,0:T(8,128)(2,1)S(1)}, bf16[2,32,1792]{2,1,0:T(8,128)(2,1)S(1)}, u32[]{:S(2)}, u32[]{:S(2)}) collective-permute-start(bf16[2,32,1792]{2,1,0:T(8,128)(2,1)S(1)} %get-tuple-element.94), channel_id=1, source_target_pairs={{0,8},{1,9},{2,10},{3,11},{4,12},{5,13},{6,14},{7,15},{8,0},{9,1},... | collective-permute-start | bytes 688136 | tf_op jit(solution)/shard_map/ppermute | solution.py:543
  167.5 12.3 %collective-permute-start.55 = (bf16[2,32,1792]{2,1,0:T(8,128)(2,1)S(1)}, bf16[2,32,1792]{2,1,0:T(8,128)(2,1)S(1)}, u32[]{:S(2)}, u32[]{:S(2)}) collective-permute-start(bf16[2,32,1792]{2,1,0:T(8,128)(2,1)S(1)} %get-tuple-element.98), channel_id=1, source_target_pairs={{0,16},{1,17},{2,18},{3,19},{4,20},{5,21},{6,22},{7,23},{8,24},{9,... | collective-permute-start | bytes 688136 | tf_op jit(solution)/shard_map/ppermute | solution.py:543
  172.1 20.2 %collective-permute-start.14 = (bf16[64,1792]{1,0:T(8,128)(2,1)S(1)}, bf16[64,1792]{1,0:T(8,128)(2,1)S(1)}, u32[]{:S(2)}, u32[]{:S(2)}) collective-permute-start(bf16[64,1792]{1,0:T(8,128)(2,1)S(1)} %join.9.near_ref), channel_id=1, source_target_pairs={{0,8},{1,9},{2,10},{3,11},{4,12},{5,13},{6,14},{7,15},{8,0},{9,1},... | collective-permute-start | bytes 688136 | tf_op jit(solution)/shard_map/ppermute | solution.py:543
  172.4 16.4 %collective-permute-start.18 = (bf16[64,1792]{1,0:T(8,128)(2,1)S(1)}, bf16[64,1792]{1,0:T(8,128)(2,1)S(1)}, u32[]{:S(2)}, u32[]{:S(2)}) collective-permute-start(bf16[64,1792]{1,0:T(8,128)(2,1)S(1)} %join.10.near_ref), channel_id=1, source_target_pairs={{0,16},{1,17},{2,18},{3,19},{4,20},{5,21},{6,22},{7,23},{8,24},{9,... | collective-permute-start | bytes 688136 | tf_op jit(solution)/shard_map/ppermute | solution.py:543
  179.2 8.6 %collective-permute-start.52 = (bf16[32,1792]{1,0:T(8,128)(2,1)S(1)}, bf16[32,1792]{1,0:T(8,128)(2,1)S(1)}, u32[]{:S(2)}, u32[]{:S(2)}) collective-permute-start(bf16[32,1792]{1,0:T(8,128)(2,1)S(1)} %activate.10.near_ref), channel_id=1, source_target_pairs={{0,16},{1,17},{2,18},{3,19},{4,20},{5,21},{6,22},{7,23},{8,24},{9,... | collective-permute-start | bytes 344072 | tf_op jit(solution)/shard_map/ppermute | solution.py:543
  185.6 15.3 %collective-permute-start.38 = (bf16[128,2048]{1,0:T(8,128)(2,1)S(1)}, bf16[128,2048]{1,0:T(8,128)(2,1)S(1)}, u32[]{:S(2)}, u32[]{:S(2)}) collective-permute-start(bf16[128,2048]{1,0:T(8,128)(2,1)S(1)} %get-tuple-element.83), channel_id=1, source_target_pairs={{0,1},{1,0},{2,3},{3,2},{4,5},{5,4},{6,7},{7,6},{8,9},{9,8},{10,11... | collective-permute-start | bytes 1572872 | tf_op jit(solution)/shard_map/ppermute | solution.py:543
  185.7 9.1 %collective-permute-start.57 = (bf16[64,1792]{1,0:T(8,128)(2,1)S(1)}, bf16[64,1792]{1,0:T(8,128)(2,1)S(1)}, u32[]{:S(2)}, u32[]{:S(2)}) collective-permute-start(bf16[64,1792]{1,0:T(8,128)(2,1)S(1)} %join.14.near_ref), channel_id=1, source_target_pairs={{0,16},{1,17},{2,18},{3,19},{4,20},{5,21},{6,22},{7,23},{8,24},{9,... | collective-permute-start | bytes 688136 | tf_op jit(solution)/shard_map/ppermute | solution.py:543
  187.8 14.2 %collective-permute-start.75 = (bf16[64,1024]{1,0:T(8,128)(2,1)S(1)}, bf16[64,1024]{1,0:T(8,128)(2,1)S(1)}, u32[]{:S(2)}, u32[]{:S(2)}) collective-permute-start(bf16[64,1024]{1,0:T(8,128)(2,1)S(1)} %take_rows.1.rows_ref.near_ref), channel_id=1, source_target_pairs={{0,8},{1,9},{2,10},{3,11},{4,12},{5,13},{6,14},{7,15},{8,0},{9,1},... | collective-permute-start | bytes 393224 | tf_op jit(solution)/shard_map/ppermute | solution.py:543
  188.8 9.5 %collective-permute-start.53 = (bf16[64,1792]{1,0:T(8,128)(2,1)S(1)}, bf16[64,1792]{1,0:T(8,128)(2,1)S(1)}, u32[]{:S(2)}, u32[]{:S(2)}) collective-permute-start(bf16[64,1792]{1,0:T(8,128)(2,1)S(1)} %join.13.near_ref), channel_id=1, source_target_pairs={{0,8},{1,9},{2,10},{3,11},{4,12},{5,13},{6,14},{7,15},{8,0},{9,1},... | collective-permute-start | bytes 688136 | tf_op jit(solution)/shard_map/ppermute | solution.py:543
  194.8 10.7 %collective-permute-start.19 = (bf16[64,2048]{1,0:T(8,128)(2,1)S(1)}, bf16[64,2048]{1,0:T(8,128)(2,1)S(1)}, u32[]{:S(2)}, u32[]{:S(2)}) collective-permute-start(bf16[64,2048]{1,0:T(8,128)(2,1)S(1)} %get-tuple-element.69), channel_id=1, source_target_pairs={{0,1},{1,0},{2,3},{3,2},{4,5},{5,4},{6,7},{7,6},{8,9},{9,8},{10,11... | collective-permute-start | bytes 786440 | tf_op jit(solution)/shard_map/ppermute | solution.py:543
  200.8 14.8 %collective-permute-start.58 = (bf16[64,2048]{1,0:T(8,128)(2,1)S(1)}, bf16[64,2048]{1,0:T(8,128)(2,1)S(1)}, u32[]{:S(2)}, u32[]{:S(2)}) collective-permute-start(bf16[64,2048]{1,0:T(8,128)(2,1)S(1)} %get-tuple-element.100), channel_id=1, source_target_pairs={{0,1},{1,0},{2,3},{3,2},{4,5},{5,4},{6,7},{7,6},{8,9},{9,8},{10,11... | collective-permute-start | bytes 786440 | tf_op jit(solution)/shard_map/ppermute | solution.py:543
  201.0 7.1 %collective-permute-start.39 = (bf16[32,2048]{1,0:T(8,128)(2,1)S(1)}, bf16[32,2048]{1,0:T(8,128)(2,1)S(1)}, u32[]{:S(2)}, u32[]{:S(2)}) collective-permute-start(bf16[32,2048]{1,0:T(8,128)(2,1)S(1)} %get-tuple-element.85), channel_id=1, source_target_pairs={{0,2},{1,3},{2,0},{3,1},{4,6},{5,7},{6,4},{7,5},{8,10},{9,11},{10,... | collective-permute-start | bytes 393224 | tf_op jit(solution)/shard_map/ppermute | solution.py:543
  201.1 13.7 %collective-permute-start.40 = (bf16[32,2048]{1,0:T(8,128)(2,1)S(1)}, bf16[32,2048]{1,0:T(8,128)(2,1)S(1)}, u32[]{:S(2)}, u32[]{:S(2)}) collective-permute-start(bf16[32,2048]{1,0:T(8,128)(2,1)S(1)} %get-tuple-element.86), channel_id=1, source_target_pairs={{0,4},{1,5},{2,6},{3,7},{4,0},{5,1},{6,2},{7,3},{8,12},{9,13},{10,... | collective-permute-start | bytes 393224 | tf_op jit(solution)/shard_map/ppermute | solution.py:543
  202.0 12.8 %collective-permute-start.41 = (bf16[32,2048]{1,0:T(8,128)(2,1)S(1)}, bf16[32,2048]{1,0:T(8,128)(2,1)S(1)}, u32[]{:S(2)}, u32[]{:S(2)}) collective-permute-start(bf16[32,2048]{1,0:T(8,128)(2,1)S(1)} %get-tuple-element.87), channel_id=1, source_target_pairs={{0,6},{1,7},{2,4},{3,5},{4,2},{5,3},{6,0},{7,1},{8,14},{9,15},{10,... | collective-permute-start | bytes 393224 | tf_op jit(solution)/shard_map/ppermute | solution.py:543
  205.5 23.5 %collective-permute-start.76 = (bf16[128,1024]{1,0:T(8,128)(2,1)S(1)}, bf16[128,1024]{1,0:T(8,128)(2,1)S(1)}, u32[]{:S(2)}, u32[]{:S(2)}) collective-permute-start(bf16[128,1024]{1,0:T(8,128)(2,1)S(1)} %join.15.near_ref), channel_id=1, source_target_pairs={{0,16},{1,17},{2,18},{3,19},{4,20},{5,21},{6,22},{7,23},{8,24},{9,... | collective-permute-start | bytes 786440 | tf_op jit(solution)/shard_map/ppermute | solution.py:543
  208.1 10.4 %collective-permute-start.20 = (bf16[16,2048]{1,0:T(8,128)(2,1)S(1)}, bf16[16,2048]{1,0:T(8,128)(2,1)S(1)}, u32[]{:S(2)}, u32[]{:S(2)}) collective-permute-start(bf16[16,2048]{1,0:T(8,128)(2,1)S(1)} %get-tuple-element.71), channel_id=1, source_target_pairs={{0,2},{1,3},{2,0},{3,1},{4,6},{5,7},{6,4},{7,5},{8,10},{9,11},{10,... | collective-permute-start | bytes 196616 | tf_op jit(solution)/shard_map/ppermute | solution.py:543
  214.8 6.5 %collective-permute-start.21 = (bf16[16,2048]{1,0:T(8,128)(2,1)S(1)}, bf16[16,2048]{1,0:T(8,128)(2,1)S(1)}, u32[]{:S(2)}, u32[]{:S(2)}) collective-permute-start(bf16[16,2048]{1,0:T(8,128)(2,1)S(1)} %get-tuple-element.72), channel_id=1, source_target_pairs={{0,4},{1,5},{2,6},{3,7},{4,0},{5,1},{6,2},{7,3},{8,12},{9,13},{10,... | collective-permute-start | bytes 196616 | tf_op jit(solution)/shard_map/ppermute | solution.py:543
  214.8 7.6 %collective-permute-start.22 = (bf16[16,2048]{1,0:T(8,128)(2,1)S(1)}, bf16[16,2048]{1,0:T(8,128)(2,1)S(1)}, u32[]{:S(2)}, u32[]{:S(2)}) collective-permute-start(bf16[16,2048]{1,0:T(8,128)(2,1)S(1)} %get-tuple-element.73), channel_id=1, source_target_pairs={{0,6},{1,7},{2,4},{3,5},{4,2},{5,3},{6,0},{7,1},{8,14},{9,15},{10,... | collective-permute-start | bytes 196616 | tf_op jit(solution)/shard_map/ppermute | solution.py:543
  215.7 7.5 %collective-permute-start.59 = (bf16[16,2048]{1,0:T(8,128)(2,1)S(1)}, bf16[16,2048]{1,0:T(8,128)(2,1)S(1)}, u32[]{:S(2)}, u32[]{:S(2)}) collective-permute-start(bf16[16,2048]{1,0:T(8,128)(2,1)S(1)} %get-tuple-element.102), channel_id=1, source_target_pairs={{0,2},{1,3},{2,0},{3,1},{4,6},{5,7},{6,4},{7,5},{8,10},{9,11},{10,... | collective-permute-start | bytes 196616 | tf_op jit(solution)/shard_map/ppermute | solution.py:543
  218.5 7.7 %collective-permute-start.60 = (bf16[16,2048]{1,0:T(8,128)(2,1)S(1)}, bf16[16,2048]{1,0:T(8,128)(2,1)S(1)}, u32[]{:S(2)}, u32[]{:S(2)}) collective-permute-start(bf16[16,2048]{1,0:T(8,128)(2,1)S(1)} %get-tuple-element.103), channel_id=1, source_target_pairs={{0,4},{1,5},{2,6},{3,7},{4,0},{5,1},{6,2},{7,3},{8,12},{9,13},{10,... | collective-permute-start | bytes 196616 | tf_op jit(solution)/shard_map/ppermute | solution.py:543
  221.3 6.2 %collective-permute-start.61 = (bf16[16,2048]{1,0:T(8,128)(2,1)S(1)}, bf16[16,2048]{1,0:T(8,128)(2,1)S(1)}, u32[]{:S(2)}, u32[]{:S(2)}) collective-permute-start(bf16[16,2048]{1,0:T(8,128)(2,1)S(1)} %get-tuple-element.104), channel_id=1, source_target_pairs={{0,6},{1,7},{2,4},{3,5},{4,2},{5,3},{6,0},{7,1},{8,14},{9,15},{10,... | collective-permute-start | bytes 196616 | tf_op jit(solution)/shard_map/ppermute | solution.py:543
  222.5 5.7 %collective-permute-start.63 = (bf16[32,2048]{1,0:T(8,128)(2,1)S(1)}, bf16[32,2048]{1,0:T(8,128)(2,1)S(1)}, u32[]{:S(2)}, u32[]{:S(2)}) collective-permute-start(bf16[32,2048]{1,0:T(8,128)(2,1)S(1)} %sum_rows.5), channel_id=1, source_target_pairs={{0,0},{1,1},{2,8},{3,9},{4,16},{5,17},{6,24},{7,25},{8,2},{9,3},{1... | collective-permute-start | bytes 393224 | tf_op jit(solution)/shard_map/ppermute | solution.py:543
  228.9 17.2 %collective-permute-start.80 = (bf16[64,1024]{1,0:T(8,128)(2,1)S(1)}, bf16[64,1024]{1,0:T(8,128)(2,1)S(1)}, u32[]{:S(2)}, u32[]{:S(2)}) collective-permute-start(bf16[64,1024]{1,0:T(8,128)(2,1)S(1)} %get-tuple-element.108.other_ref), channel_id=1, source_target_pairs={{0,1},{1,0},{2,3},{3,2},{4,5},{5,4},{6,7},{7,6},{8,9},{9,8},{10,11... | collective-permute-start | bytes 393224 | tf_op jit(solution)/shard_map/ppermute | solution.py:543
  229.2 41.9 %collective-permute-start.77 = (bf16[1024,256]{1,0:T(8,128)(2,1)S(1)}, bf16[1024,256]{1,0:T(8,128)(2,1)S(1)}, u32[]{:S(2)}, u32[]{:S(2)}) collective-permute-start(bf16[1024,256]{1,0:T(8,128)(2,1)S(1)} %turn.1.own_ref), channel_id=1, source_target_pairs={{0,1},{1,0},{2,3},{3,2},{4,5},{5,4},{6,7},{7,6},{8,9},{9,8},{10,11... | collective-permute-start | bytes 1572872 | tf_op jit(solution)/shard_map/ppermute | solution.py:543
  229.7 34.2 %collective-permute-start.78 = (bf16[64,1024]{1,0:T(8,128)(2,1)S(1)}, bf16[64,1024]{1,0:T(8,128)(2,1)S(1)}, u32[]{:S(2)}, u32[]{:S(2)}) collective-permute-start(bf16[64,1024]{1,0:T(8,128)(2,1)S(1)} %get-tuple-element.107.own_ref.near_ref), channel_id=1, source_target_pairs={{0,8},{1,9},{2,10},{3,11},{4,12},{5,13},{6,14},{7,15},{8,0},{9,1},... | collective-permute-start | bytes 393224 | tf_op jit(solution)/shard_map/ppermute | solution.py:543
  246.1 17.8 %collective-permute-start.81 = (bf16[64,1024]{1,0:T(8,128)(2,1)S(1)}, bf16[64,1024]{1,0:T(8,128)(2,1)S(1)}, u32[]{:S(2)}, u32[]{:S(2)}) collective-permute-start(bf16[64,1024]{1,0:T(8,128)(2,1)S(1)} %collective-permute-done.80.near_ref), channel_id=1, source_target_pairs={{0,16},{1,17},{2,18},{3,19},{4,20},{5,21},{6,22},{7,23},{8,24},{9,... | collective-permute-start | bytes 393224 | tf_op jit(solution)/shard_map/ppermute | solution.py:543
  248.1 6.4 %collective-permute-start.66 = (bf16[16,1024]{1,0:T(8,128)(2,1)S(1)}, bf16[16,1024]{1,0:T(8,128)(2,1)S(1)}, u32[]{:S(2)}, u32[]{:S(2)}) collective-permute-start(bf16[16,1024]{1,0:T(8,128)(2,1)S(1)} %get-tuple-element.111), channel_id=1, source_target_pairs={{0,4},{1,5},{2,6},{3,7},{4,0},{5,1},{6,2},{7,3},{8,12},{9,13},{10,... | collective-permute-start | bytes 98312 | tf_op jit(solution)/shard_map/ppermute | solution.py:543
  252.2 5.7 %collective-permute-start.67 = (bf16[16,1024]{1,0:T(8,128)(2,1)S(1)}, bf16[16,1024]{1,0:T(8,128)(2,1)S(1)}, u32[]{:S(2)}, u32[]{:S(2)}) collective-permute-start(bf16[16,1024]{1,0:T(8,128)(2,1)S(1)} %get-tuple-element.112), channel_id=1, source_target_pairs={{0,6},{1,7},{2,4},{3,5},{4,2},{5,3},{6,0},{7,1},{8,14},{9,15},{10,... | collective-permute-start | bytes 98312 | tf_op jit(solution)/shard_map/ppermute | solution.py:543
  257.9 6.0 %collective-permute-start.73 = (bf16[16,1024]{1,0:T(8,128)(2,1)S(1)}, bf16[16,1024]{1,0:T(8,128)(2,1)S(1)}, u32[]{:S(2)}, u32[]{:S(2)}) collective-permute-start(bf16[16,1024]{1,0:T(8,128)(2,1)S(1)} %sum_rows.7.refs_0_), channel_id=1, source_target_pairs={{0,6},{1,7},{2,4},{3,5},{4,2},{5,3},{6,0},{7,1},{8,14},{9,15},{10,... | collective-permute-start | bytes 98312 | tf_op jit(solution)/shard_map/ppermute | solution.py:543
  265.2 7.7 %collective-permute-start.79 = (bf16[128,1024]{1,0:T(8,128)(2,1)S(1)}, bf16[128,1024]{1,0:T(8,128)(2,1)S(1)}, u32[]{:S(2)}, u32[]{:S(2)}) collective-permute-start(bf16[128,1024]{1,0:T(8,128)(2,1)S(1)} %join.16.refs_0_), channel_id=1, source_target_pairs={{0,16},{1,17},{2,18},{3,19},{4,20},{5,21},{6,22},{7,23},{8,24},{9,... | collective-permute-start | bytes 786440 | tf_op jit(solution)/shard_map/ppermute | solution.py:543
  267.8 6.4 %collective-permute-start.82 = (bf16[128,1024]{1,0:T(8,128)(2,1)S(1)}, bf16[128,1024]{1,0:T(8,128)(2,1)S(1)}, u32[]{:S(2)}, u32[]{:S(2)}) collective-permute-start(bf16[128,1024]{1,0:T(8,128)(2,1)S(1)} %join.17.refs_2_), channel_id=1, source_target_pairs={{0,8},{1,9},{2,10},{3,11},{4,12},{5,13},{6,14},{7,15},{8,0},{9,1},... | collective-permute-start | bytes 786440 | tf_op jit(solution)/shard_map/ppermute | solution.py:543
  (38 other events, 375.7 us)
where the time goes:
time: 278 us
  starting transfers between devices  96.1 us (35%)
  Pallas kernels  88.9 us (32%)
  waiting for transfers between devices  82.7 us (30%)
  local copies, waits for them, and re-layouts  7.76 us (3%)
    ppermute x83, starting transfers between devices, move(): return lax.ppermute(value, AXES, pairs)  96.1 us
    ppermute x83, waiting for transfers between devices, move(): return lax.ppermute(value, AXES, pairs)  82.7 us
    pallas_call x6, Pallas kernels, up_product(): pl.pallas_call(functools.partial(up_kernel, block, blocks, WEIGHT_PARTS),...  47.9 us
    pallas_call x6, Pallas kernels, down_product(): pl.pallas_call(functools.partial(down_kernel, rows // len(blocks), step,...  17.1 us
    unnamed x38, local copies, waits for them, and re-layouts  6.14 us
    pallas_call x6, Pallas kernels, activate(): pl.pallas_call(functools.partial(activate_kernel, len(squares), start, D)...  5.95 us
  transfers between devices with their start and end apart: 83, of which 29 were waited for; matrix products, arithmetic and copies ran while one was open for 1% of the time, Pallas kernels for 31%

commit v1 on v0

--- a/solution.py
+++ b/solution.py
@@ -12,7 +12,7 @@
 AXES = ("grp", "inner")
 BF16 = jnp.bfloat16
 F32 = jnp.float32
-ROW_SHARES = (1, 2, 1)
+ROW_SHARES = (1, 1)
 COL_CHUNKS = 2
 WEIGHT_PARTS = 2
 
@@ -593,10 +593,6 @@
     target_parts = []
     for r, step in enumerate(steps):
         x = prepare(meta, gather_rows(r), gain)
-        if r == len(steps) - 1:
-            x, predicted_own, predicted_other = lax.optimization_barrier(
-                (x, predicted_own, predicted_other)
-            )
         before = None
         for chunk in range(COL_CHUNKS):
             u = r * COL_CHUNKS + chunk
@@ -652,9 +648,7 @@
         pre_pieces.extend(gather(value, orders[half]))
         blocks = [half * groups + block for block in gather_list(orders[half])]
         pre_places.extend((blocks[: groups // 2], blocks[groups // 2 :]))
-    grad_proj = proj_product(
-        student_cols, student_cols_other, pre_pieces, pre_places, local_rows
-    )
+    grad_proj = proj_product(student_cols, student_cols_other, pre_pieces, pre_places, local_rows)
     return (teacher_out, grad_student, grad_proj)
 
 

time: 278 us -> 263 us (0.946)
  Pallas kernels: 88.9 us -> 70.7 us
  waiting for transfers between devices: 82.7 us -> 96.8 us
  starting transfers between devices: 96.1 us -> 89.9 us
  local copies, waits for them, and re-layouts: 7.76 us -> 2.9 us
    ppermute x83 -> x63, waiting for transfers between devices: 82.7 us -> 96.8 us  [move(): return lax.ppermute(value, AXES, pairs)]
    pallas_call x6 -> x4, Pallas kernels: 47.9 us -> 37 us  [up_product(): pl.pallas_call(functools.partial(up_kernel, block, blocks, WEIGHT_PARTS),...]
    ppermute x83 -> x63, starting transfers between devices: 96.1 us -> 89.9 us  [move(): return lax.ppermute(value, AXES, pairs)]
    unnamed x38 -> x18, local copies, waits for them, and re-layouts: 6.14 us -> 1.22 us
    pallas_call x6 -> x4, Pallas kernels: 17.1 us -> 14.4 us  [down_product(): pl.pallas_call(functools.partial(down_kernel, rows // len(blocks), step,...]
    pallas_call x6 -> x4, Pallas kernels: 5.95 us -> 3.72 us  [activate(): pl.pallas_call(functools.partial(activate_kernel, len(squares), start, D)...]
  transfers between devices with their start and end apart: 83 -> 63, of which waited for: 29 -> 20; matrix products, arithmetic and copies ran while one was open for 1% -> 1% of each run, Pallas kernels for 31% -> 26%
where the time goes in v1:
time: 263 us; the launch traced here: 262 us
  waiting for transfers between devices  96.8 us (37%)
  starting transfers between devices  89.9 us (34%)
  Pallas kernels  70.7 us (27%)
  local copies, waits for them, and re-layouts  2.9 us (1%)
    ppermute x63, waiting for transfers between devices, move(): return lax.ppermute(value, AXES, pairs)  96.8 us
    ppermute x63, starting transfers between devices, move(): return lax.ppermute(value, AXES, pairs)  89.9 us
    pallas_call x4, Pallas kernels, up_product(): pl.pallas_call(functools.partial(up_kernel, block, blocks, WEIGHT_PARTS),...  37 us
    pallas_call x4, Pallas kernels, down_product(): pl.pallas_call(functools.partial(down_kernel, rows // len(blocks), step,...  14.4 us
  transfers between devices with their start and end apart: 63, of which 20 were waited for; matrix products, arithmetic and copies ran while one was open for 1% of the time, Pallas kernels for 26%

profile of v1, /device:TPU:0, one launch (start us, length us, event | category | flops | bytes accessed | tf_op | source)
XLA Modules:
  0.0 262.3 jit_solution(1847464947793844701)
XLA Ops:
  0.7 1.0 fusion
  1.7 3.1 %collective-permute-start.24 = (bf16[32,2048]{1,0:T(8,128)(2,1)S(1)}, bf16[32,2048]{1,0:T(8,128)(2,1)S(1)}, u32[]{:S(2)}, u32[]{:S(2)}) collective-permute-start(bf16[32,2048]{1,0:T(8,128)(2,1)S(1)} %get-tuple-element.80.refs_0_), channel_id=1, source_target_pairs={{0,2},{1,3},{2,0},{3,1},{4,6},{5,7},{6,4},{7,5},{8,10},{9,11},{10,... | collective-permute-start | bytes 393224 | tf_op jit(solution)/shard_map/ppermute | solution.py:543
  4.8 2.6 collective-permute-start.26
  7.9 3.9 %collective-permute-start.5 = (bf16[32,2048]{1,0:T(8,128)(2,1)S(1)}, bf16[32,2048]{1,0:T(8,128)(2,1)S(1)}, u32[]{:S(2)}, u32[]{:S(2)}) collective-permute-start(bf16[32,2048]{1,0:T(8,128)(2,1)S(1)} %get-tuple-element.79.refs_0_), channel_id=1, source_target_pairs={{0,6},{1,7},{2,4},{3,5},{4,2},{5,3},{6,0},{7,1},{8,14},{9,15},{10,... | collective-permute-start | bytes 393224 | tf_op jit(solution)/shard_map/ppermute | solution.py:543
  11.8 3.8 %collective-permute-start.28 = (bf16[32,2048]{1,0:T(8,128)(2,1)S(1)}, bf16[32,2048]{1,0:T(8,128)(2,1)S(1)}, u32[]{:S(2)}, u32[]{:S(2)}) collective-permute-start(bf16[32,2048]{1,0:T(8,128)(2,1)S(1)} %get-tuple-element.80.refs_0_), channel_id=1, source_target_pairs={{0,6},{1,7},{2,4},{3,5},{4,2},{5,3},{6,0},{7,1},{8,14},{9,15},{10,... | collective-permute-start | bytes 393224 | tf_op jit(solution)/shard_map/ppermute | solution.py:543
  16.2 9.5 %collective-permute-done.3.refs_4_ = bf16[32,2048]{1,0:T(8,128)(2,1)S(1)} collective-permute-done((bf16[32,2048]{1,0:T(8,128)(2,1)S(1)}, bf16[32,2048]{1,0:T(8,128)(2,1)S(1)}, u32[]{:S(2)}, u32[]{:S(2)}) %collective-permute-start.3) | collective-permute-done | bytes 131104 | tf_op jit(solution)/shard_map/ppermute | solution.py:543
  28.7 9.0 %up_product.4 = (bf16[2,128,1792]{2,1,0:T(8,128)(2,1)S(1)}, bf16[2,128,1792]{2,1,0:T(8,128)(2,1)}) custom-call(bf16[256,2048]{1,0:T(8,128)(2,1)S(1)} %prepare.2.x_ref, bf16[2,2048,3584]{2,1,0:T(8,128)(2,1)} %refs_1_.13, bf16[2,2048,3584]{2,1,0:T(8,128)(2,1)} %refs_1_.13), custom_call_target="tpu_custom_call" | custom-call | flops 3758096384 | bytes 15728640 | tf_op jit(solution)/shard_map/up_product/pallas_call | solution.py:101
  37.7 8.9 %up_product.5 = (bf16[2,128,1792]{2,1,0:T(8,128)(2,1)S(1)}, bf16[2,128,1792]{2,1,0:T(8,128)(2,1)}) custom-call(bf16[256,2048]{1,0:T(8,128)(2,1)S(1)} %prepare.2.x_ref, bf16[2,2048,3584]{2,1,0:T(8,128)(2,1)} %refs_1_.13, bf16[2,2048,3584]{2,1,0:T(8,128)(2,1)} %refs_1_.13), custom_call_target="tpu_custom_call" | custom-call | flops 3758096384 | bytes 15728640 | tf_op jit(solution)/shard_map/up_product/pallas_call | solution.py:101
  46.6 1.5 collective-permute-start.15
  48.9 9.8 %up_product.7 = (bf16[2,128,1792]{2,1,0:T(8,128)(2,1)S(1)}, bf16[2,128,1792]{2,1,0:T(8,128)(2,1)}) custom-call(bf16[256,2048]{1,0:T(8,128)(2,1)S(1)} %prepare.3.x_ref, bf16[2,2048,3584]{2,1,0:T(8,128)(2,1)} %refs_1_.13, bf16[2,2048,3584]{2,1,0:T(8,128)(2,1)} %refs_1_.13), custom_call_target="tpu_custom_call" | custom-call | flops 3758096384 | bytes 15728640 | tf_op jit(solution)/shard_map/up_product/pallas_call | solution.py:101
  59.2 1.5 collective-permute-start.7
  60.7 9.3 %up_product.6 = (bf16[2,128,1792]{2,1,0:T(8,128)(2,1)S(1)}, bf16[2,128,1792]{2,1,0:T(8,128)(2,1)}) custom-call(bf16[256,2048]{1,0:T(8,128)(2,1)S(1)} %prepare.3.x_ref, bf16[2,2048,3584]{2,1,0:T(8,128)(2,1)} %refs_1_.13, bf16[2,2048,3584]{2,1,0:T(8,128)(2,1)} %refs_1_.13), custom_call_target="tpu_custom_call" | custom-call | flops 3758096384 | bytes 15728640 | tf_op jit(solution)/shard_map/up_product/pallas_call | solution.py:101
  70.4 1.2 copy-done.3
  71.6 1.3 add_halves.5
  72.9 1.7 collective-permute-start.16
  74.5 8.2 %collective-permute-done.7.arrived_ref = bf16[2,128,1792]{2,1,0:T(8,128)(2,1)} collective-permute-done((bf16[2,128,1792]{2,1,0:T(8,128)(2,1)}, bf16[2,128,1792]{2,1,0:T(8,128)(2,1)}, u32[]{:S(2)}, u32[]{:S(2)}) %collective-permute-start.7) | collective-permute-done | bytes 917536 | tf_op jit(solution)/shard_map/ppermute | solution.py:543
  82.7 1.3 add_halves.4
  84.0 1.6 collective-permute-start.8
  86.3 3.6 %collective-permute-done.34.arrived_ref = bf16[2,128,1792]{2,1,0:T(8,128)(2,1)} collective-permute-done((bf16[2,128,1792]{2,1,0:T(8,128)(2,1)}, bf16[2,128,1792]{2,1,0:T(8,128)(2,1)}, u32[]{:S(2)}, u32[]{:S(2)}) %collective-permute-start.34) | collective-permute-done | bytes 917536 | tf_op jit(solution)/shard_map/ppermute | solution.py:543
  89.8 1.3 add_halves.7
  91.1 1.6 collective-permute-start.35
  92.7 6.7 %collective-permute-done.9 = f32[64,128]{1,0:T(8,128)S(1)} collective-permute-done((f32[64,128]{1,0:T(8,128)S(1)}, f32[64,128]{1,0:T(8,128)S(1)}, u32[]{:S(2)}, u32[]{:S(2)}) %collective-permute-start.9) | collective-permute-done | bytes 32800 | tf_op jit(solution)/shard_map/ppermute | solution.py:543
  99.4 1.5 collective-permute-start.10
  100.9 20.3 %collective-permute-done.10 = f32[64,128]{1,0:T(8,128)S(1)} collective-permute-done((f32[64,128]{1,0:T(8,128)S(1)}, f32[64,128]{1,0:T(8,128)S(1)}, u32[]{:S(2)}, u32[]{:S(2)}) %collective-permute-start.10) | collective-permute-done | bytes 32800 | tf_op jit(solution)/shard_map/ppermute | solution.py:543
  122.4 8.4 %collective-permute-start.31 = (bf16[2,64,1792]{2,1,0:T(8,128)(2,1)S(1)}, bf16[2,64,1792]{2,1,0:T(8,128)(2,1)S(1)}, u32[]{:S(2)}, u32[]{:S(2)}) collective-permute-start(bf16[2,64,1792]{2,1,0:T(8,128)(2,1)S(1)} %get-tuple-element.60), channel_id=1, source_target_pairs={{0,8},{1,9},{2,10},{3,11},{4,12},{5,13},{6,14},{7,15},{8,0},{9,1},... | collective-permute-start | bytes 1376264 | tf_op jit(solution)/shard_map/ppermute | solution.py:543
  130.8 0.9 activate.5.near_ref
  131.7 1.0 collective-permute-start.17
  132.7 0.9 activate.4.near_ref
  133.7 3.2 %collective-permute-start.13 = (bf16[64,1792]{1,0:T(8,128)(2,1)S(1)}, bf16[64,1792]{1,0:T(8,128)(2,1)S(1)}, u32[]{:S(2)}, u32[]{:S(2)}) collective-permute-start(bf16[64,1792]{1,0:T(8,128)(2,1)S(1)} %activate.4.near_ref), channel_id=1, source_target_pairs={{0,16},{1,17},{2,18},{3,19},{4,20},{5,21},{6,22},{7,23},{8,24},{9,... | collective-permute-start | bytes 688136 | tf_op jit(solution)/shard_map/ppermute | solution.py:543
  136.9 10.0 %collective-permute-done.17.far_ref = bf16[64,1792]{1,0:T(8,128)(2,1)S(1)} collective-permute-done((bf16[64,1792]{1,0:T(8,128)(2,1)S(1)}, bf16[64,1792]{1,0:T(8,128)(2,1)S(1)}, u32[]{:S(2)}, u32[]{:S(2)}) %collective-permute-start.17) | collective-permute-done | bytes 229408 | tf_op jit(solution)/shard_map/ppermute | solution.py:543
  146.9 3.2 %collective-permute-start.18 = (bf16[128,1792]{1,0:T(8,128)(2,1)S(1)}, bf16[128,1792]{1,0:T(8,128)(2,1)S(1)}, u32[]{:S(2)}, u32[]{:S(2)}) collective-permute-start(bf16[128,1792]{1,0:T(8,128)(2,1)S(1)} %join.8.near_ref), channel_id=1, source_target_pairs={{0,16},{1,17},{2,18},{3,19},{4,20},{5,21},{6,22},{7,23},{8,24},{9,... | collective-permute-start | bytes 1376264 | tf_op jit(solution)/shard_map/ppermute | solution.py:543
  151.1 1.8 collective-permute-start.36
  154.3 5.3 %collective-permute-done.36.far_ref = bf16[64,1792]{1,0:T(8,128)(2,1)S(1)} collective-permute-done((bf16[64,1792]{1,0:T(8,128)(2,1)S(1)}, bf16[64,1792]{1,0:T(8,128)(2,1)S(1)}, u32[]{:S(2)}, u32[]{:S(2)}) %collective-permute-start.36) | collective-permute-done | bytes 229408 | tf_op jit(solution)/shard_map/ppermute | solution.py:543
  159.8 6.7 %collective-permute-done.32.far_ref = bf16[64,1792]{1,0:T(8,128)(2,1)S(1)} collective-permute-done((bf16[64,1792]{1,0:T(8,128)(2,1)S(1)}, bf16[64,1792]{1,0:T(8,128)(2,1)S(1)}, u32[]{:S(2)}, u32[]{:S(2)}) %collective-permute-start.32) | collective-permute-done | bytes 229408 | tf_op jit(solution)/shard_map/ppermute | solution.py:543
  166.5 1.8 collective-permute-start.33
  168.3 3.5 %down_product.4.refs_2_ = f32[256,2048]{1,0:T(8,128)S(1)} custom-call(s32[4]{0:T(128)S(1)} %pad_add_fusion.at_ref.meta_ref, bf16[128,1792]{1,0:T(8,128)(2,1)S(1)} %join.8.near_ref, bf16[128,1792]{1,0:T(8,128)(2,1)S(1)} %collective-permute-done.18.far_ref, bf16[3584,2048]{1,0:T(8,128)(2,1)S(1)} %bitcast.5, bf16[3584,2048]{1,0:T(8,128)(2,1)S(1)} %bitcast.5), custom_call_target="tpu_custom_call" | custom-call | flops 1879048192 | bytes 8257536 | tf_op jit(solution)/shard_map/down_product/pallas_call | solution.py:284
  171.8 3.7 %down_product.5 = (f32[128,2048]{1,0:T(8,128)S(1)}, bf16[128,2048]{1,0:T(8,128)(2,1)S(1)}) custom-call(s32[4]{0:T(128)S(1)} %pad_add_fusion.at_ref.meta_ref, bf16[128,1792]{1,0:T(8,128)(2,1)S(1)} %join.7.near_ref, bf16[128,1792]{1,0:T(8,128)(2,1)S(1)} %collective-permute-done.14.far_ref, bf16[3584,2048]{1,0:T(8,128)(2,1)S(1)} %bitcast.5, ...), custom_call_target="tpu_custom_call" | custom-call | flops 1879048192 | bytes 8257536 | tf_op jit(solution)/shard_map/down_product/pallas_call | solution.py:284
  175.6 3.5 %down_product.6.refs_2_ = f32[256,2048]{1,0:T(8,128)S(1)} custom-call(s32[4]{0:T(128)S(1)} %pad_add_fusion.at_ref.meta_ref, bf16[128,1792]{1,0:T(8,128)(2,1)S(1)} %join.10.near_ref, bf16[128,1792]{1,0:T(8,128)(2,1)S(1)} %collective-permute-done.37.far_ref, bf16[3584,2048]{1,0:T(8,128)(2,1)S(1)} %bitcast.5, bf16[3584,2048]{1,0:T(8,128)(2,1)S(1)} %bitcast.5), custom_call_target="tpu_custom_call" | custom-call | flops 1879048192 | bytes 8257536 | tf_op jit(solution)/shard_map/down_product/pallas_call | solution.py:284
  179.2 3.7 %down_product.7 = (f32[128,2048]{1,0:T(8,128)S(1)}, bf16[128,2048]{1,0:T(8,128)(2,1)S(1)}) custom-call(s32[4]{0:T(128)S(1)} %pad_add_fusion.at_ref.meta_ref, bf16[128,1792]{1,0:T(8,128)(2,1)S(1)} %join.9.near_ref, bf16[128,1792]{1,0:T(8,128)(2,1)S(1)} %collective-permute-done.33.far_ref, bf16[3584,2048]{1,0:T(8,128)(2,1)S(1)} %bitcast.5, ...), custom_call_target="tpu_custom_call" | custom-call | flops 1879048192 | bytes 8257536 | tf_op jit(solution)/shard_map/down_product/pallas_call | solution.py:284
  185.0 2.3 collective-permute-start.20
  187.3 1.7 collective-permute-start.21
  189.1 1.4 collective-permute-start.22
  190.6 1.2 collective-permute-start.39
  191.7 2.1 collective-permute-done.20.refs_0_
  193.8 1.5 collective-permute-start.40
  195.3 4.4 %collective-permute-done.21.refs_1_ = bf16[32,2048]{1,0:T(8,128)(2,1)S(1)} collective-permute-done((bf16[32,2048]{1,0:T(8,128)(2,1)S(1)}, bf16[32,2048]{1,0:T(8,128)(2,1)S(1)}, u32[]{:S(2)}, u32[]{:S(2)}) %collective-permute-start.21) | collective-permute-done | bytes 131104 | tf_op jit(solution)/shard_map/ppermute | solution.py:543
  199.7 3.6 %collective-permute-start.41 = (bf16[32,2048]{1,0:T(8,128)(2,1)S(1)}, bf16[32,2048]{1,0:T(8,128)(2,1)S(1)}, u32[]{:S(2)}, u32[]{:S(2)}) collective-permute-start(bf16[32,2048]{1,0:T(8,128)(2,1)S(1)} %get-tuple-element.70), channel_id=1, source_target_pairs={{0,6},{1,7},{2,4},{3,5},{4,2},{5,3},{6,0},{7,1},{8,14},{9,15},{10,... | collective-permute-start | bytes 393224 | tf_op jit(solution)/shard_map/ppermute | solution.py:543
  204.5 8.3 %collective-permute-done.40.refs_1_ = bf16[32,2048]{1,0:T(8,128)(2,1)S(1)} collective-permute-done((bf16[32,2048]{1,0:T(8,128)(2,1)S(1)}, bf16[32,2048]{1,0:T(8,128)(2,1)S(1)}, u32[]{:S(2)}, u32[]{:S(2)}) %collective-permute-start.40) | collective-permute-done | bytes 131104 | tf_op jit(solution)/shard_map/ppermute | solution.py:543
  213.5 1.3 predict.1
  216.4 13.9 %collective-permute-start.58 = (bf16[64,1024]{1,0:T(8,128)(2,1)S(1)}, bf16[64,1024]{1,0:T(8,128)(2,1)S(1)}, u32[]{:S(2)}, u32[]{:S(2)}) collective-permute-start(bf16[64,1024]{1,0:T(8,128)(2,1)S(1)} %get-tuple-element.73.own_ref.near_ref), channel_id=1, source_target_pairs={{0,8},{1,9},{2,10},{3,11},{4,12},{5,13},{6,14},{7,15},{8,0},{9,1},... | collective-permute-start | bytes 393224 | tf_op jit(solution)/shard_map/ppermute | solution.py:543
  230.3 1.9 student_term.1
  232.3 3.5 %collective-permute-start.46 = (bf16[16,1024]{1,0:T(8,128)(2,1)S(1)}, bf16[16,1024]{1,0:T(8,128)(2,1)S(1)}, u32[]{:S(2)}, u32[]{:S(2)}) collective-permute-start(bf16[16,1024]{1,0:T(8,128)(2,1)S(1)} %get-tuple-element.77), channel_id=1, source_target_pairs={{0,4},{1,5},{2,6},{3,7},{4,0},{5,1},{6,2},{7,3},{8,12},{9,13},{10,... | collective-permute-start | bytes 98312 | tf_op jit(solution)/shard_map/ppermute | solution.py:543
  236.2 3.2 %collective-permute-start.47 = (bf16[16,1024]{1,0:T(8,128)(2,1)S(1)}, bf16[16,1024]{1,0:T(8,128)(2,1)S(1)}, u32[]{:S(2)}, u32[]{:S(2)}) collective-permute-start(bf16[16,1024]{1,0:T(8,128)(2,1)S(1)} %get-tuple-element.78), channel_id=1, source_target_pairs={{0,6},{1,7},{2,4},{3,5},{4,2},{5,3},{6,0},{7,1},{8,14},{9,15},{10,... | collective-permute-start | bytes 98312 | tf_op jit(solution)/shard_map/ppermute | solution.py:543
  239.4 2.6 collective-permute-done.47.refs_2_
  242.1 3.8 %collective-permute-done.49.refs_2_ = bf16[16,1024]{1,0:T(8,128)(2,1)S(1)} collective-permute-done((bf16[16,1024]{1,0:T(8,128)(2,1)S(1)}, bf16[16,1024]{1,0:T(8,128)(2,1)S(1)}, u32[]{:S(2)}, u32[]{:S(2)}) %collective-permute-start.49) | collective-permute-done | bytes 32800 | tf_op jit(solution)/shard_map/ppermute | solution.py:543
  245.9 1.8 collective-permute-start.51
  247.8 1.5 collective-permute-start.53
  249.3 1.2 collective-permute-start.59
  250.5 1.0 collective-permute-done.51.refs_4_
  251.4 1.0 collective-permute-start.62
  252.5 1.0 collective-permute-done.53.refs_6_
  254.9 1.4 place.1
  256.3 1.8 collective-permute-done.59.refs_1_
  258.9 3.4 %proj_product.1 = f32[1024,1024]{1,0:T(8,128)} custom-call(bf16[1024,256]{1,0:T(8,128)(2,1)S(1)} %turn.1.own_ref, bf16[1024,256]{1,0:T(8,128)(2,1)S(1)} %collective-permute-done.57.other_ref, bf16[128,1024]{1,0:T(8,128)(2,1)S(1)} %join.12.refs_0_, bf16[128,1024]{1,0:T(8,128)(2,1)S(1)} %collective-permute-done.59.refs_1_, ...), custom_call_target="tpu_custom_call" | custom-call | flops 1073741824 | bytes 5242880 | tf_op jit(solution)/shard_map/proj_product/pallas_call | solution.py:485
  (125 shorter events, 18.7 us)
Async XLA Ops:
  1.7 10.1 %collective-permute-start.24 = (bf16[32,2048]{1,0:T(8,128)(2,1)S(1)}, bf16[32,2048]{1,0:T(8,128)(2,1)S(1)}, u32[]{:S(2)}, u32[]{:S(2)}) collective-permute-start(bf16[32,2048]{1,0:T(8,128)(2,1)S(1)} %get-tuple-element.80.refs_0_), channel_id=1, source_target_pairs={{0,2},{1,3},{2,0},{3,1},{4,6},{5,7},{6,4},{7,5},{8,10},{9,11},{10,... | collective-permute-start | bytes 393224 | tf_op jit(solution)/shard_map/ppermute | solution.py:543
  4.8 10.8 %collective-permute-start.26 = (bf16[32,2048]{1,0:T(8,128)(2,1)S(1)}, bf16[32,2048]{1,0:T(8,128)(2,1)S(1)}, u32[]{:S(2)}, u32[]{:S(2)}) collective-permute-start(bf16[32,2048]{1,0:T(8,128)(2,1)S(1)} %get-tuple-element.80.refs_0_), channel_id=1, source_target_pairs={{0,4},{1,5},{2,6},{3,7},{4,0},{5,1},{6,2},{7,3},{8,12},{9,13},{10,... | collective-permute-start | bytes 393224 | tf_op jit(solution)/shard_map/ppermute | solution.py:543
  7.4 8.4 %collective-permute-start.1 = (bf16[32,2048]{1,0:T(8,128)(2,1)S(1)}, bf16[32,2048]{1,0:T(8,128)(2,1)S(1)}, u32[]{:S(2)}, u32[]{:S(2)}) collective-permute-start(bf16[32,2048]{1,0:T(8,128)(2,1)S(1)} %get-tuple-element.79.refs_0_), channel_id=1, source_target_pairs={{0,2},{1,3},{2,0},{3,1},{4,6},{5,7},{6,4},{7,5},{8,10},{9,11},{10,... | collective-permute-start | bytes 393224 | tf_op jit(solution)/shard_map/ppermute | solution.py:543
  7.9 17.8 %collective-permute-start.3 = (bf16[32,2048]{1,0:T(8,128)(2,1)S(1)}, bf16[32,2048]{1,0:T(8,128)(2,1)S(1)}, u32[]{:S(2)}, u32[]{:S(2)}) collective-permute-start(bf16[32,2048]{1,0:T(8,128)(2,1)S(1)} %get-tuple-element.79.refs_0_), channel_id=1, source_target_pairs={{0,4},{1,5},{2,6},{3,7},{4,0},{5,1},{6,2},{7,3},{8,12},{9,13},{10,... | collective-permute-start | bytes 393224 | tf_op jit(solution)/shard_map/ppermute | solution.py:543
  7.9 17.8 %collective-permute-start.5 = (bf16[32,2048]{1,0:T(8,128)(2,1)S(1)}, bf16[32,2048]{1,0:T(8,128)(2,1)S(1)}, u32[]{:S(2)}, u32[]{:S(2)}) collective-permute-start(bf16[32,2048]{1,0:T(8,128)(2,1)S(1)} %get-tuple-element.79.refs_0_), channel_id=1, source_target_pairs={{0,6},{1,7},{2,4},{3,5},{4,2},{5,3},{6,0},{7,1},{8,14},{9,15},{10,... | collective-permute-start | bytes 393224 | tf_op jit(solution)/shard_map/ppermute | solution.py:543
  11.8 15.0 %collective-permute-start.28 = (bf16[32,2048]{1,0:T(8,128)(2,1)S(1)}, bf16[32,2048]{1,0:T(8,128)(2,1)S(1)}, u32[]{:S(2)}, u32[]{:S(2)}) collective-permute-start(bf16[32,2048]{1,0:T(8,128)(2,1)S(1)} %get-tuple-element.80.refs_0_), channel_id=1, source_target_pairs={{0,6},{1,7},{2,4},{3,5},{4,2},{5,3},{6,0},{7,1},{8,14},{9,15},{10,... | collective-permute-start | bytes 393224 | tf_op jit(solution)/shard_map/ppermute | solution.py:543
  15.6 11.3 %collective-permute-start = (bf16[32,2048]{1,0:T(8,128)(2,1)S(1)}, bf16[32,2048]{1,0:T(8,128)(2,1)S(1)}, u32[]{:S(2)}, u32[]{:S(2)}) collective-permute-start(bf16[32,2048]{1,0:T(8,128)(2,1)S(1)} %get-tuple-element.79.refs_0_), channel_id=1, source_target_pairs={{0,1},{1,0},{2,3},{3,2},{4,5},{5,4},{6,7},{7,6},{8,9},{9,8},{10,11... | collective-permute-start | bytes 393224 | tf_op jit(solution)/shard_map/ppermute | solution.py:543
  15.8 11.6 %collective-permute-start.2 = (bf16[32,2048]{1,0:T(8,128)(2,1)S(1)}, bf16[32,2048]{1,0:T(8,128)(2,1)S(1)}, u32[]{:S(2)}, u32[]{:S(2)}) collective-permute-start(bf16[32,2048]{1,0:T(8,128)(2,1)S(1)} %collective-permute-done.1.refs_2_), channel_id=1, source_target_pairs={{0,1},{1,0},{2,3},{3,2},{4,5},{5,4},{6,7},{7,6},{8,9},{9,8},{10,11... | collective-permute-start | bytes 393224 | tf_op jit(solution)/shard_map/ppermute | solution.py:543
  25.6 1.9 collective-permute-start.4
  25.6 2.3 collective-permute-start.6
  26.8 21.3 %collective-permute-start.23 = (bf16[32,2048]{1,0:T(8,128)(2,1)S(1)}, bf16[32,2048]{1,0:T(8,128)(2,1)S(1)}, u32[]{:S(2)}, u32[]{:S(2)}) collective-permute-start(bf16[32,2048]{1,0:T(8,128)(2,1)S(1)} %get-tuple-element.80.refs_0_), channel_id=1, source_target_pairs={{0,1},{1,0},{2,3},{3,2},{4,5},{5,4},{6,7},{7,6},{8,9},{9,8},{10,11... | collective-permute-start | bytes 393224 | tf_op jit(solution)/shard_map/ppermute | solution.py:543
  26.9 21.2 %collective-permute-start.25 = (bf16[32,2048]{1,0:T(8,128)(2,1)S(1)}, bf16[32,2048]{1,0:T(8,128)(2,1)S(1)}, u32[]{:S(2)}, u32[]{:S(2)}) collective-permute-start(bf16[32,2048]{1,0:T(8,128)(2,1)S(1)} %collective-permute-done.24.refs_2_), channel_id=1, source_target_pairs={{0,1},{1,0},{2,3},{3,2},{4,5},{5,4},{6,7},{7,6},{8,9},{9,8},{10,11... | collective-permute-start | bytes 393224 | tf_op jit(solution)/shard_map/ppermute | solution.py:543
  27.4 20.7 %collective-permute-start.27 = (bf16[32,2048]{1,0:T(8,128)(2,1)S(1)}, bf16[32,2048]{1,0:T(8,128)(2,1)S(1)}, u32[]{:S(2)}, u32[]{:S(2)}) collective-permute-start(bf16[32,2048]{1,0:T(8,128)(2,1)S(1)} %collective-permute-done.26.refs_4_), channel_id=1, source_target_pairs={{0,1},{1,0},{2,3},{3,2},{4,5},{5,4},{6,7},{7,6},{8,9},{9,8},{10,11... | collective-permute-start | bytes 393224 | tf_op jit(solution)/shard_map/ppermute | solution.py:543
  27.5 20.6 %collective-permute-start.29 = (bf16[32,2048]{1,0:T(8,128)(2,1)S(1)}, bf16[32,2048]{1,0:T(8,128)(2,1)S(1)}, u32[]{:S(2)}, u32[]{:S(2)}) collective-permute-start(bf16[32,2048]{1,0:T(8,128)(2,1)S(1)} %collective-permute-done.28.refs_6_), channel_id=1, source_target_pairs={{0,1},{1,0},{2,3},{3,2},{4,5},{5,4},{6,7},{7,6},{8,9},{9,8},{10,11... | collective-permute-start | bytes 393224 | tf_op jit(solution)/shard_map/ppermute | solution.py:543
  46.6 23.8 %collective-permute-start.15 = (bf16[2,128,1792]{2,1,0:T(8,128)(2,1)}, bf16[2,128,1792]{2,1,0:T(8,128)(2,1)}, u32[]{:S(2)}, u32[]{:S(2)}) collective-permute-start(bf16[2,128,1792]{2,1,0:T(8,128)(2,1)} %get-tuple-element.48), channel_id=1, source_target_pairs={{0,8},{1,9},{2,10},{3,11},{4,12},{5,13},{6,14},{7,15},{8,0},{9,1},... | collective-permute-start | bytes 2752520 | tf_op jit(solution)/shard_map/ppermute | solution.py:543
  48.9 119.4 %slice-start = ((s8[14680064]{0:T(1024)(128)(4,1)}), s8[4194304]{0:T(1024)(128)(4,1)S(1)}, s32[]{:S(2)}) async-start(s8[14680064]{0:T(1024)(128)(4,1)} %bitcast.4), calls=%async_computation | async-start | bytes 8388608
  58.7 31.2 %collective-permute-start.34 = (bf16[2,128,1792]{2,1,0:T(8,128)(2,1)}, bf16[2,128,1792]{2,1,0:T(8,128)(2,1)}, u32[]{:S(2)}, u32[]{:S(2)}) collective-permute-start(bf16[2,128,1792]{2,1,0:T(8,128)(2,1)} %get-tuple-element.62), channel_id=1, source_target_pairs={{0,8},{1,9},{2,10},{3,11},{4,12},{5,13},{6,14},{7,15},{8,0},{9,1},... | collective-permute-start | bytes 2752520 | tf_op jit(solution)/shard_map/ppermute | solution.py:543
  59.2 23.5 %collective-permute-start.7 = (bf16[2,128,1792]{2,1,0:T(8,128)(2,1)}, bf16[2,128,1792]{2,1,0:T(8,128)(2,1)}, u32[]{:S(2)}, u32[]{:S(2)}) collective-permute-start(bf16[2,128,1792]{2,1,0:T(8,128)(2,1)} %get-tuple-element.44), channel_id=1, source_target_pairs={{0,16},{1,17},{2,18},{3,19},{4,20},{5,21},{6,22},{7,23},{8,24},{9,... | collective-permute-start | bytes 2752520 | tf_op jit(solution)/shard_map/ppermute | solution.py:543
  70.0 52.2 %collective-permute-start.30 = (bf16[2,128,1792]{2,1,0:T(8,128)(2,1)}, bf16[2,128,1792]{2,1,0:T(8,128)(2,1)S(1)}, u32[]{:S(2)}, u32[]{:S(2)}) collective-permute-start(bf16[2,128,1792]{2,1,0:T(8,128)(2,1)} %get-tuple-element.58), channel_id=1, source_target_pairs={{0,16},{1,17},{2,18},{3,19},{4,20},{5,21},{6,22},{7,23},{8,24},{9,... | collective-permute-start | bytes 2752520 | tf_op jit(solution)/shard_map/ppermute | solution.py:543
  72.9 57.9 %collective-permute-start.16 = (bf16[2,64,1792]{2,1,0:T(8,128)(2,1)S(1)}, bf16[2,64,1792]{2,1,0:T(8,128)(2,1)S(1)}, u32[]{:S(2)}, u32[]{:S(2)}) collective-permute-start(bf16[2,64,1792]{2,1,0:T(8,128)(2,1)S(1)} %get-tuple-element.50), channel_id=1, source_target_pairs={{0,16},{1,17},{2,18},{3,19},{4,20},{5,21},{6,22},{7,23},{8,24},{9,... | collective-permute-start | bytes 1376264 | tf_op jit(solution)/shard_map/ppermute | solution.py:543
  84.0 48.7 %collective-permute-start.8 = (bf16[2,64,1792]{2,1,0:T(8,128)(2,1)S(1)}, bf16[2,64,1792]{2,1,0:T(8,128)(2,1)S(1)}, u32[]{:S(2)}, u32[]{:S(2)}) collective-permute-start(bf16[2,64,1792]{2,1,0:T(8,128)(2,1)S(1)} %get-tuple-element.46), channel_id=1, source_target_pairs={{0,8},{1,9},{2,10},{3,11},{4,12},{5,13},{6,14},{7,15},{8,0},{9,1},... | collective-permute-start | bytes 1376264 | tf_op jit(solution)/shard_map/ppermute | solution.py:543
  85.7 13.7 %collective-permute-start.9 = (f32[64,128]{1,0:T(8,128)S(1)}, f32[64,128]{1,0:T(8,128)S(1)}, u32[]{:S(2)}, u32[]{:S(2)}) collective-permute-start(f32[64,128]{1,0:T(8,128)S(1)} %row_squares.1), channel_id=1, source_target_pairs={{0,8},{1,9},{2,10},{3,11},{4,12},{5,13},{6,14},{7,15},{8,0},{9,1},... | collective-permute-start | bytes 98312 | tf_op jit(solution)/shard_map/ppermute | solution.py:543
  91.1 59.0 %collective-permute-start.35 = (bf16[2,64,1792]{2,1,0:T(8,128)(2,1)S(1)}, bf16[2,64,1792]{2,1,0:T(8,128)(2,1)S(1)}, u32[]{:S(2)}, u32[]{:S(2)}) collective-permute-start(bf16[2,64,1792]{2,1,0:T(8,128)(2,1)S(1)} %get-tuple-element.64), channel_id=1, source_target_pairs={{0,16},{1,17},{2,18},{3,19},{4,20},{5,21},{6,22},{7,23},{8,24},{9,... | collective-permute-start | bytes 1376264 | tf_op jit(solution)/shard_map/ppermute | solution.py:543
  99.4 21.8 %collective-permute-start.10 = (f32[64,128]{1,0:T(8,128)S(1)}, f32[64,128]{1,0:T(8,128)S(1)}, u32[]{:S(2)}, u32[]{:S(2)}) collective-permute-start(f32[64,128]{1,0:T(8,128)S(1)} %add.6), channel_id=1, source_target_pairs={{0,16},{1,17},{2,18},{3,19},{4,20},{5,21},{6,22},{7,23},{8,24},{9,... | collective-permute-start | bytes 98312 | tf_op jit(solution)/shard_map/ppermute | solution.py:543
  121.2 0.8 collective-permute-start.11
  122.1 8.7 %collective-permute-start.12 = (f32[64,128]{1,0:T(8,128)S(1)}, f32[64,128]{1,0:T(8,128)S(1)}, u32[]{:S(2)}, u32[]{:S(2)}) collective-permute-start(f32[64,128]{1,0:T(8,128)S(1)} %collective-permute-done.11.refs_0_), channel_id=1, source_target_pairs={{0,1},{1,0},{2,3},{3,2},{4,5},{5,4},{6,7},{7,6},{8,9},{9,8},{10,11... | collective-permute-start | bytes 98312 | tf_op jit(solution)/shard_map/ppermute | solution.py:543
  122.4 30.9 %collective-permute-start.31 = (bf16[2,64,1792]{2,1,0:T(8,128)(2,1)S(1)}, bf16[2,64,1792]{2,1,0:T(8,128)(2,1)S(1)}, u32[]{:S(2)}, u32[]{:S(2)}) collective-permute-start(bf16[2,64,1792]{2,1,0:T(8,128)(2,1)S(1)} %get-tuple-element.60), channel_id=1, source_target_pairs={{0,8},{1,9},{2,10},{3,11},{4,12},{5,13},{6,14},{7,15},{8,0},{9,1},... | collective-permute-start | bytes 1376264 | tf_op jit(solution)/shard_map/ppermute | solution.py:543
  131.7 15.2 %collective-permute-start.17 = (bf16[64,1792]{1,0:T(8,128)(2,1)S(1)}, bf16[64,1792]{1,0:T(8,128)(2,1)S(1)}, u32[]{:S(2)}, u32[]{:S(2)}) collective-permute-start(bf16[64,1792]{1,0:T(8,128)(2,1)S(1)} %activate.5.near_ref), channel_id=1, source_target_pairs={{0,8},{1,9},{2,10},{3,11},{4,12},{5,13},{6,14},{7,15},{8,0},{9,1},... | collective-permute-start | bytes 688136 | tf_op jit(solution)/shard_map/ppermute | solution.py:543
  132.7 80.8 %collective-permute-start.42 = (bf16[1024,1024]{1,0:T(8,128)(2,1)S(1)}, bf16[1024,1024]{1,0:T(8,128)(2,1)S(1)}, u32[]{:S(2)}, u32[]{:S(2)}) collective-permute-start(bf16[1024,1024]{1,0:T(8,128)(2,1)S(1)} %copy-done), channel_id=1, source_target_pairs={{0,1},{1,0},{2,3},{3,2},{4,5},{5,4},{6,7},{7,6},{8,9},{9,8},{10,11... | collective-permute-start | bytes 6291464 | tf_op jit(solution)/shard_map/ppermute | solution.py:543
  133.7 19.2 %collective-permute-start.13 = (bf16[64,1792]{1,0:T(8,128)(2,1)S(1)}, bf16[64,1792]{1,0:T(8,128)(2,1)S(1)}, u32[]{:S(2)}, u32[]{:S(2)}) collective-permute-start(bf16[64,1792]{1,0:T(8,128)(2,1)S(1)} %activate.4.near_ref), channel_id=1, source_target_pairs={{0,16},{1,17},{2,18},{3,19},{4,20},{5,21},{6,22},{7,23},{8,24},{9,... | collective-permute-start | bytes 688136 | tf_op jit(solution)/shard_map/ppermute | solution.py:543
  146.9 21.3 %collective-permute-start.18 = (bf16[128,1792]{1,0:T(8,128)(2,1)S(1)}, bf16[128,1792]{1,0:T(8,128)(2,1)S(1)}, u32[]{:S(2)}, u32[]{:S(2)}) collective-permute-start(bf16[128,1792]{1,0:T(8,128)(2,1)S(1)} %join.8.near_ref), channel_id=1, source_target_pairs={{0,16},{1,17},{2,18},{3,19},{4,20},{5,21},{6,22},{7,23},{8,24},{9,... | collective-permute-start | bytes 1376264 | tf_op jit(solution)/shard_map/ppermute | solution.py:543
  151.1 8.5 %collective-permute-start.36 = (bf16[64,1792]{1,0:T(8,128)(2,1)S(1)}, bf16[64,1792]{1,0:T(8,128)(2,1)S(1)}, u32[]{:S(2)}, u32[]{:S(2)}) collective-permute-start(bf16[64,1792]{1,0:T(8,128)(2,1)S(1)} %activate.7.near_ref), channel_id=1, source_target_pairs={{0,8},{1,9},{2,10},{3,11},{4,12},{5,13},{6,14},{7,15},{8,0},{9,1},... | collective-permute-start | bytes 688136 | tf_op jit(solution)/shard_map/ppermute | solution.py:543
  152.9 18.9 %collective-permute-start.14 = (bf16[128,1792]{1,0:T(8,128)(2,1)S(1)}, bf16[128,1792]{1,0:T(8,128)(2,1)S(1)}, u32[]{:S(2)}, u32[]{:S(2)}) collective-permute-start(bf16[128,1792]{1,0:T(8,128)(2,1)S(1)} %join.7.near_ref), channel_id=1, source_target_pairs={{0,8},{1,9},{2,10},{3,11},{4,12},{5,13},{6,14},{7,15},{8,0},{9,1},... | collective-permute-start | bytes 1376264 | tf_op jit(solution)/shard_map/ppermute | solution.py:543
  154.2 12.2 %collective-permute-start.32 = (bf16[64,1792]{1,0:T(8,128)(2,1)S(1)}, bf16[64,1792]{1,0:T(8,128)(2,1)S(1)}, u32[]{:S(2)}, u32[]{:S(2)}) collective-permute-start(bf16[64,1792]{1,0:T(8,128)(2,1)S(1)} %activate.6.near_ref), channel_id=1, source_target_pairs={{0,16},{1,17},{2,18},{3,19},{4,20},{5,21},{6,22},{7,23},{8,24},{9,... | collective-permute-start | bytes 688136 | tf_op jit(solution)/shard_map/ppermute | solution.py:543
  159.7 16.0 %collective-permute-start.37 = (bf16[128,1792]{1,0:T(8,128)(2,1)S(1)}, bf16[128,1792]{1,0:T(8,128)(2,1)S(1)}, u32[]{:S(2)}, u32[]{:S(2)}) collective-permute-start(bf16[128,1792]{1,0:T(8,128)(2,1)S(1)} %join.10.near_ref), channel_id=1, source_target_pairs={{0,16},{1,17},{2,18},{3,19},{4,20},{5,21},{6,22},{7,23},{8,24},{9,... | collective-permute-start | bytes 1376264 | tf_op jit(solution)/shard_map/ppermute | solution.py:543
  166.5 12.7 %collective-permute-start.33 = (bf16[128,1792]{1,0:T(8,128)(2,1)S(1)}, bf16[128,1792]{1,0:T(8,128)(2,1)S(1)}, u32[]{:S(2)}, u32[]{:S(2)}) collective-permute-start(bf16[128,1792]{1,0:T(8,128)(2,1)S(1)} %join.9.near_ref), channel_id=1, source_target_pairs={{0,8},{1,9},{2,10},{3,11},{4,12},{5,13},{6,14},{7,15},{8,0},{9,1},... | collective-permute-start | bytes 1376264 | tf_op jit(solution)/shard_map/ppermute | solution.py:543
  175.5 9.4 %collective-permute-start.19 = (bf16[128,2048]{1,0:T(8,128)(2,1)S(1)}, bf16[128,2048]{1,0:T(8,128)(2,1)S(1)}, u32[]{:S(2)}, u32[]{:S(2)}) collective-permute-start(bf16[128,2048]{1,0:T(8,128)(2,1)S(1)} %get-tuple-element.52), channel_id=1, source_target_pairs={{0,1},{1,0},{2,3},{3,2},{4,5},{5,4},{6,7},{7,6},{8,9},{9,8},{10,11... | collective-permute-start | bytes 1572872 | tf_op jit(solution)/shard_map/ppermute | solution.py:543
  182.9 6.2 %collective-permute-start.38 = (bf16[128,2048]{1,0:T(8,128)(2,1)S(1)}, bf16[128,2048]{1,0:T(8,128)(2,1)S(1)}, u32[]{:S(2)}, u32[]{:S(2)}) collective-permute-start(bf16[128,2048]{1,0:T(8,128)(2,1)S(1)} %get-tuple-element.66), channel_id=1, source_target_pairs={{0,1},{1,0},{2,3},{3,2},{4,5},{5,4},{6,7},{7,6},{8,9},{9,8},{10,11... | collective-permute-start | bytes 1572872 | tf_op jit(solution)/shard_map/ppermute | solution.py:543
  184.0 6.6 %collective-permute-start.55 = (bf16[64,1024]{1,0:T(8,128)(2,1)S(1)}, bf16[64,1024]{1,0:T(8,128)(2,1)S(1)}, u32[]{:S(2)}, u32[]{:S(2)}) collective-permute-start(bf16[64,1024]{1,0:T(8,128)(2,1)S(1)} %take_rows.1.rows_ref.near_ref), channel_id=1, source_target_pairs={{0,8},{1,9},{2,10},{3,11},{4,12},{5,13},{6,14},{7,15},{8,0},{9,1},... | collective-permute-start | bytes 393224 | tf_op jit(solution)/shard_map/ppermute | solution.py:543
  185.0 8.8 %collective-permute-start.20 = (bf16[32,2048]{1,0:T(8,128)(2,1)S(1)}, bf16[32,2048]{1,0:T(8,128)(2,1)S(1)}, u32[]{:S(2)}, u32[]{:S(2)}) collective-permute-start(bf16[32,2048]{1,0:T(8,128)(2,1)S(1)} %get-tuple-element.54), channel_id=1, source_target_pairs={{0,2},{1,3},{2,0},{3,1},{4,6},{5,7},{6,4},{7,5},{8,10},{9,11},{10,... | collective-permute-start | bytes 393224 | tf_op jit(solution)/shard_map/ppermute | solution.py:543
  187.3 12.4 %collective-permute-start.21 = (bf16[32,2048]{1,0:T(8,128)(2,1)S(1)}, bf16[32,2048]{1,0:T(8,128)(2,1)S(1)}, u32[]{:S(2)}, u32[]{:S(2)}) collective-permute-start(bf16[32,2048]{1,0:T(8,128)(2,1)S(1)} %get-tuple-element.55), channel_id=1, source_target_pairs={{0,4},{1,5},{2,6},{3,7},{4,0},{5,1},{6,2},{7,3},{8,12},{9,13},{10,... | collective-permute-start | bytes 393224 | tf_op jit(solution)/shard_map/ppermute | solution.py:543
  189.1 14.3 %collective-permute-start.22 = (bf16[32,2048]{1,0:T(8,128)(2,1)S(1)}, bf16[32,2048]{1,0:T(8,128)(2,1)S(1)}, u32[]{:S(2)}, u32[]{:S(2)}) collective-permute-start(bf16[32,2048]{1,0:T(8,128)(2,1)S(1)} %get-tuple-element.56), channel_id=1, source_target_pairs={{0,6},{1,7},{2,4},{3,5},{4,2},{5,3},{6,0},{7,1},{8,14},{9,15},{10,... | collective-permute-start | bytes 393224 | tf_op jit(solution)/shard_map/ppermute | solution.py:543
  190.6 13.3 %collective-permute-start.39 = (bf16[32,2048]{1,0:T(8,128)(2,1)S(1)}, bf16[32,2048]{1,0:T(8,128)(2,1)S(1)}, u32[]{:S(2)}, u32[]{:S(2)}) collective-permute-start(bf16[32,2048]{1,0:T(8,128)(2,1)S(1)} %get-tuple-element.68), channel_id=1, source_target_pairs={{0,2},{1,3},{2,0},{3,1},{4,6},{5,7},{6,4},{7,5},{8,10},{9,11},{10,... | collective-permute-start | bytes 393224 | tf_op jit(solution)/shard_map/ppermute | solution.py:543
  193.8 19.0 %collective-permute-start.40 = (bf16[32,2048]{1,0:T(8,128)(2,1)S(1)}, bf16[32,2048]{1,0:T(8,128)(2,1)S(1)}, u32[]{:S(2)}, u32[]{:S(2)}) collective-permute-start(bf16[32,2048]{1,0:T(8,128)(2,1)S(1)} %get-tuple-element.69), channel_id=1, source_target_pairs={{0,4},{1,5},{2,6},{3,7},{4,0},{5,1},{6,2},{7,3},{8,12},{9,13},{10,... | collective-permute-start | bytes 393224 | tf_op jit(solution)/shard_map/ppermute | solution.py:543
  199.7 13.0 %collective-permute-start.41 = (bf16[32,2048]{1,0:T(8,128)(2,1)S(1)}, bf16[32,2048]{1,0:T(8,128)(2,1)S(1)}, u32[]{:S(2)}, u32[]{:S(2)}) collective-permute-start(bf16[32,2048]{1,0:T(8,128)(2,1)S(1)} %get-tuple-element.70), channel_id=1, source_target_pairs={{0,6},{1,7},{2,4},{3,5},{4,2},{5,3},{6,0},{7,1},{8,14},{9,15},{10,... | collective-permute-start | bytes 393224 | tf_op jit(solution)/shard_map/ppermute | solution.py:543
  203.4 12.2 %collective-permute-start.56 = (bf16[128,1024]{1,0:T(8,128)(2,1)S(1)}, bf16[128,1024]{1,0:T(8,128)(2,1)S(1)}, u32[]{:S(2)}, u32[]{:S(2)}) collective-permute-start(bf16[128,1024]{1,0:T(8,128)(2,1)S(1)} %join.11.near_ref), channel_id=1, source_target_pairs={{0,16},{1,17},{2,18},{3,19},{4,20},{5,21},{6,22},{7,23},{8,24},{9,... | collective-permute-start | bytes 786440 | tf_op jit(solution)/shard_map/ppermute | solution.py:543
  203.8 11.0 %collective-permute-start.43 = (bf16[32,2048]{1,0:T(8,128)(2,1)S(1)}, bf16[32,2048]{1,0:T(8,128)(2,1)S(1)}, u32[]{:S(2)}, u32[]{:S(2)}) collective-permute-start(bf16[32,2048]{1,0:T(8,128)(2,1)S(1)} %sum_rows.3), channel_id=1, source_target_pairs={{0,0},{1,1},{2,8},{3,9},{4,16},{5,17},{6,24},{7,25},{8,2},{9,3},{1... | collective-permute-start | bytes 393224 | tf_op jit(solution)/shard_map/ppermute | solution.py:543
  212.9 2.0 collective-permute-start.44
  215.5 14.7 %collective-permute-start.60 = (bf16[64,1024]{1,0:T(8,128)(2,1)S(1)}, bf16[64,1024]{1,0:T(8,128)(2,1)S(1)}, u32[]{:S(2)}, u32[]{:S(2)}) collective-permute-start(bf16[64,1024]{1,0:T(8,128)(2,1)S(1)} %get-tuple-element.74.other_ref), channel_id=1, source_target_pairs={{0,1},{1,0},{2,3},{3,2},{4,5},{5,4},{6,7},{7,6},{8,9},{9,8},{10,11... | collective-permute-start | bytes 393224 | tf_op jit(solution)/shard_map/ppermute | solution.py:543
  215.8 40.4 %collective-permute-start.57 = (bf16[1024,256]{1,0:T(8,128)(2,1)S(1)}, bf16[1024,256]{1,0:T(8,128)(2,1)S(1)}, u32[]{:S(2)}, u32[]{:S(2)}) collective-permute-start(bf16[1024,256]{1,0:T(8,128)(2,1)S(1)} %turn.1.own_ref), channel_id=1, source_target_pairs={{0,1},{1,0},{2,3},{3,2},{4,5},{5,4},{6,7},{7,6},{8,9},{9,8},{10,11... | collective-permute-start | bytes 1572872 | tf_op jit(solution)/shard_map/ppermute | solution.py:543
  216.4 31.4 %collective-permute-start.58 = (bf16[64,1024]{1,0:T(8,128)(2,1)S(1)}, bf16[64,1024]{1,0:T(8,128)(2,1)S(1)}, u32[]{:S(2)}, u32[]{:S(2)}) collective-permute-start(bf16[64,1024]{1,0:T(8,128)(2,1)S(1)} %get-tuple-element.73.own_ref.near_ref), channel_id=1, source_target_pairs={{0,8},{1,9},{2,10},{3,11},{4,12},{5,13},{6,14},{7,15},{8,0},{9,1},... | collective-permute-start | bytes 393224 | tf_op jit(solution)/shard_map/ppermute | solution.py:543
  230.3 19.0 %collective-permute-start.61 = (bf16[64,1024]{1,0:T(8,128)(2,1)S(1)}, bf16[64,1024]{1,0:T(8,128)(2,1)S(1)}, u32[]{:S(2)}, u32[]{:S(2)}) collective-permute-start(bf16[64,1024]{1,0:T(8,128)(2,1)S(1)} %collective-permute-done.60.near_ref), channel_id=1, source_target_pairs={{0,16},{1,17},{2,18},{3,19},{4,20},{5,21},{6,22},{7,23},{8,24},{9,... | collective-permute-start | bytes 393224 | tf_op jit(solution)/shard_map/ppermute | solution.py:543
  232.2 4.0 %collective-permute-start.45 = (bf16[16,1024]{1,0:T(8,128)(2,1)S(1)}, bf16[16,1024]{1,0:T(8,128)(2,1)S(1)}, u32[]{:S(2)}, u32[]{:S(2)}) collective-permute-start(bf16[16,1024]{1,0:T(8,128)(2,1)S(1)} %get-tuple-element.76), channel_id=1, source_target_pairs={{0,2},{1,3},{2,0},{3,1},{4,6},{5,7},{6,4},{7,5},{8,10},{9,11},{10,... | collective-permute-start | bytes 98312 | tf_op jit(solution)/shard_map/ppermute | solution.py:543
  232.3 7.1 %collective-permute-start.46 = (bf16[16,1024]{1,0:T(8,128)(2,1)S(1)}, bf16[16,1024]{1,0:T(8,128)(2,1)S(1)}, u32[]{:S(2)}, u32[]{:S(2)}) collective-permute-start(bf16[16,1024]{1,0:T(8,128)(2,1)S(1)} %get-tuple-element.77), channel_id=1, source_target_pairs={{0,4},{1,5},{2,6},{3,7},{4,0},{5,1},{6,2},{7,3},{8,12},{9,13},{10,... | collective-permute-start | bytes 98312 | tf_op jit(solution)/shard_map/ppermute | solution.py:543
  236.2 5.7 %collective-permute-start.47 = (bf16[16,1024]{1,0:T(8,128)(2,1)S(1)}, bf16[16,1024]{1,0:T(8,128)(2,1)S(1)}, u32[]{:S(2)}, u32[]{:S(2)}) collective-permute-start(bf16[16,1024]{1,0:T(8,128)(2,1)S(1)} %get-tuple-element.78), channel_id=1, source_target_pairs={{0,6},{1,7},{2,4},{3,5},{4,2},{5,3},{6,0},{7,1},{8,14},{9,15},{10,... | collective-permute-start | bytes 98312 | tf_op jit(solution)/shard_map/ppermute | solution.py:543
  241.9 4.0 %collective-permute-start.49 = (bf16[16,1024]{1,0:T(8,128)(2,1)S(1)}, bf16[16,1024]{1,0:T(8,128)(2,1)S(1)}, u32[]{:S(2)}, u32[]{:S(2)}) collective-permute-start(bf16[16,1024]{1,0:T(8,128)(2,1)S(1)} %sum_rows.5.refs_0_), channel_id=1, source_target_pairs={{0,2},{1,3},{2,0},{3,1},{4,6},{5,7},{6,4},{7,5},{8,10},{9,11},{10,... | collective-permute-start | bytes 98312 | tf_op jit(solution)/shard_map/ppermute | solution.py:543
  242.0 7.3 %collective-permute-start.48 = (bf16[16,1024]{1,0:T(8,128)(2,1)S(1)}, bf16[16,1024]{1,0:T(8,128)(2,1)S(1)}, u32[]{:S(2)}, u32[]{:S(2)}) collective-permute-start(bf16[16,1024]{1,0:T(8,128)(2,1)S(1)} %sum_rows.5.refs_0_), channel_id=1, source_target_pairs={{0,1},{1,0},{2,3},{3,2},{4,5},{5,4},{6,7},{7,6},{8,9},{9,8},{10,11... | collective-permute-start | bytes 98312 | tf_op jit(solution)/shard_map/ppermute | solution.py:543
  245.9 5.5 %collective-permute-start.51 = (bf16[16,1024]{1,0:T(8,128)(2,1)S(1)}, bf16[16,1024]{1,0:T(8,128)(2,1)S(1)}, u32[]{:S(2)}, u32[]{:S(2)}) collective-permute-start(bf16[16,1024]{1,0:T(8,128)(2,1)S(1)} %sum_rows.5.refs_0_), channel_id=1, source_target_pairs={{0,4},{1,5},{2,6},{3,7},{4,0},{5,1},{6,2},{7,3},{8,12},{9,13},{10,... | collective-permute-start | bytes 98312 | tf_op jit(solution)/shard_map/ppermute | solution.py:543
  247.8 5.7 %collective-permute-start.53 = (bf16[16,1024]{1,0:T(8,128)(2,1)S(1)}, bf16[16,1024]{1,0:T(8,128)(2,1)S(1)}, u32[]{:S(2)}, u32[]{:S(2)}) collective-permute-start(bf16[16,1024]{1,0:T(8,128)(2,1)S(1)} %sum_rows.5.refs_0_), channel_id=1, source_target_pairs={{0,6},{1,7},{2,4},{3,5},{4,2},{5,3},{6,0},{7,1},{8,14},{9,15},{10,... | collective-permute-start | bytes 98312 | tf_op jit(solution)/shard_map/ppermute | solution.py:543
  249.2 4.3 %collective-permute-start.50 = (bf16[16,1024]{1,0:T(8,128)(2,1)S(1)}, bf16[16,1024]{1,0:T(8,128)(2,1)S(1)}, u32[]{:S(2)}, u32[]{:S(2)}) collective-permute-start(bf16[16,1024]{1,0:T(8,128)(2,1)S(1)} %collective-permute-done.49.refs_2_), channel_id=1, source_target_pairs={{0,1},{1,0},{2,3},{3,2},{4,5},{5,4},{6,7},{7,6},{8,9},{9,8},{10,11... | collective-permute-start | bytes 98312 | tf_op jit(solution)/shard_map/ppermute | solution.py:543
  249.3 8.8 %collective-permute-start.59 = (bf16[128,1024]{1,0:T(8,128)(2,1)S(1)}, bf16[128,1024]{1,0:T(8,128)(2,1)S(1)}, u32[]{:S(2)}, u32[]{:S(2)}) collective-permute-start(bf16[128,1024]{1,0:T(8,128)(2,1)S(1)} %join.12.refs_0_), channel_id=1, source_target_pairs={{0,16},{1,17},{2,18},{3,19},{4,20},{5,21},{6,22},{7,23},{8,24},{9,... | collective-permute-start | bytes 786440 | tf_op jit(solution)/shard_map/ppermute | solution.py:543
  251.4 7.5 %collective-permute-start.62 = (bf16[128,1024]{1,0:T(8,128)(2,1)S(1)}, bf16[128,1024]{1,0:T(8,128)(2,1)S(1)}, u32[]{:S(2)}, u32[]{:S(2)}) collective-permute-start(bf16[128,1024]{1,0:T(8,128)(2,1)S(1)} %join.13.refs_2_), channel_id=1, source_target_pairs={{0,8},{1,9},{2,10},{3,11},{4,12},{5,13},{6,14},{7,15},{8,0},{9,1},... | collective-permute-start | bytes 786440 | tf_op jit(solution)/shard_map/ppermute | solution.py:543
  253.5 1.2 collective-permute-start.52
  253.5 1.4 collective-permute-start.54
  (8 other events, 412.2 us)

commit v2 on v1

--- a/solution.py
+++ b/solution.py
@@ -51,11 +51,14 @@
 
 
 def prepare_kernel(count, step, at_ref, *refs):
-    pieces, gain_ref, out_ref = refs[:count], refs[count], refs[count + 1]
+    pieces, gain_ref, out_ref, squares_ref = refs[:count], *refs[count:]
     gain = gain_ref[...].astype(F32)
     for offset in range(count):
         start = pl.multiple_of((at_ref[0] ^ offset) * step, step)
-        out_ref[pl.ds(start, step), :] = (pieces[offset][...].astype(F32) * gain).astype(BF16)
+        values = pieces[offset][...].astype(F32)
+        out_ref[pl.ds(start, step), :] = (values * gain).astype(BF16)
+        total = jnp.sum(values * values, axis=1, keepdims=True)
+        squares_ref[pl.ds(start, step), :] = jnp.broadcast_to(total, (step, 128))
 
 
 def prepare(at, pieces, gain):
@@ -64,57 +67,69 @@
     return pl.pallas_call(
         functools.partial(prepare_kernel, count, step),
         grid=(1,),
-        out_shape=jax.ShapeDtypeStruct((count * step, width), BF16),
+        out_shape=[
+            jax.ShapeDtypeStruct((count * step, width), BF16),
+            jax.ShapeDtypeStruct((count * step, 128), F32),
+        ],
         in_specs=[pl.BlockSpec(memory_space=pltpu.SMEM)]
         + [whole_block((step, width))] * count
         + [whole_block(gain.shape)],
-        out_specs=whole_block((count * step, width)),
-        cost_estimate=cost(count * step * width, 4 * count * step * width),
+        out_specs=[whole_block((count * step, width)), whole_block((count * step, 128))],
+        cost_estimate=cost(3 * count * step * width, 4 * count * step * width),
         name="prepare",
         compiler_params=room(8),
     )(at, *pieces, gain)
 
 
-def up_kernel(block, blocks, parts, x_ref, *refs):
-    w_refs, outs = refs[:parts], refs[parts:]
-    part = w_refs[0].shape[0]
-    total = 0.0
-    for at, w_ref in enumerate(w_refs):
-        total += jnp.dot(
-            x_ref[:, at * part : (at + 1) * part], w_ref[...], preferred_element_type=F32
+def up_kernel(block, blocks, start, tile, x_ref, source_ref, keep_ref, send_ref, w_ref, sems):
+    tiles = w_ref.shape[2] // tile
+    half = len(blocks) // 2
+
+    def copy(k, n):
+        column = pl.multiple_of(n * tile, tile)
+        return pltpu.make_async_copy(
+            source_ref.at[k, :, pl.ds(start + column, tile)],
+            w_ref.at[k, :, pl.ds(column, tile)],
+            sems.at[k, n],
         )
-    half = len(blocks) // 2
-    for slot, at in enumerate(blocks):
-        row = (slot % half) * block
-        outs[slot // half][row : row + block, :] = total[at * block : (at + 1) * block, :].astype(
-            BF16
-        )
+
+    for k in range(2):
+        for n in range(tiles):
+            copy(k, n).start()
+    for k in range(2):
+
+        @pl.loop(0, tiles)
+        def _(n):
+            copy(k, n).wait()
+            columns = pl.ds(pl.multiple_of(n * tile, tile), tile)
+            total = jnp.dot(x_ref[...], w_ref[k, :, columns], preferred_element_type=F32)
+            for slot, at in enumerate(blocks):
+                ref = send_ref if slot >= half else keep_ref
+                row = (slot % half) * block
+                ref[k, row : row + block, columns] = total[
+                    at * block : (at + 1) * block, :
+                ].astype(BF16)
 
 
 def up_product(x, weight, chunk, chunks, blocks):
     rows, depth = x.shape
-    block = rows // len(blocks)
     width = weight.shape[2] // chunks
-    tile = tile_of(width)
-    tiles = width // tile
+    tile = tile_of(width, 256)
     half = jax.ShapeDtypeStruct((2, rows // 2, width), BF16)
     return pl.pallas_call(
-        functools.partial(up_kernel, block, blocks, WEIGHT_PARTS),
-        grid=(2, tiles),
+        functools.partial(up_kernel, rows // len(blocks), blocks, chunk * width, tile),
+        grid=(1,),
         out_shape=[half] * 2,
-        in_specs=[whole_block(x.shape)]
-        + [
-            pl.BlockSpec(
-                (None, depth // WEIGHT_PARTS, tile),
-                lambda k, n, at=at: (k, at, chunk * tiles + n),
-            )
-            for at in range(WEIGHT_PARTS)
+        in_specs=[whole_block(x.shape), pl.BlockSpec(memory_space=pltpu.HBM)],
+        out_specs=[whole_block(half.shape)] * 2,
+        scratch_shapes=[
+            pltpu.VMEM((2, depth, width), BF16),
+            pltpu.SemaphoreType.DMA((2, width // tile)),
         ],
-        out_specs=[pl.BlockSpec((None, rows // 2, tile), lambda k, n: (k, 0, n))] * 2,
         cost_estimate=cost(4 * rows * depth * width, 4 * depth * width + 2 * rows * depth),
         name="up_product",
-        compiler_params=room(44),
-    )(x, *[weight] * WEIGHT_PARTS)
+        compiler_params=room(32),
+    )(x, weight)
 
 
 def add_kernel(keep_ref, arrived_ref, kept_ref, send_ref):
@@ -143,56 +158,27 @@
     )(keep, arrived)
 
 
-def squares_kernel(tokens_ref, out_ref):
-    values = tokens_ref[...].astype(F32)
-    total = jnp.sum(values * values, axis=1, keepdims=True)
-    out_ref[...] = jnp.broadcast_to(total, out_ref.shape)
-
-
-def row_squares(tokens):
-    rows, width = tokens.shape
-    return pl.pallas_call(
-        squares_kernel,
-        grid=(1,),
-        out_shape=jax.ShapeDtypeStruct((rows, 128), F32),
-        in_specs=[pl.BlockSpec((rows, width), lambda n: (0, 0))],
-        out_specs=pl.BlockSpec((rows, 128), lambda n: (0, 0)),
-        cost_estimate=cost(2 * rows * width, 2 * rows * width),
-        name="row_squares",
-        compiler_params=room(8),
-    )(tokens)
-
-
-def activate_kernel(cores, start, width, meta_ref, keep_ref, arrived_ref, *refs):
-    squares, out_ref = refs[:cores], refs[cores]
-    step = out_ref.shape[0] // cores
-    for slot in range(cores):
-        total = squares[0][start : start + step, :1]
-        for offset in range(1, cores):
-            other = squares[offset][start : start + step, :1]
-            total = jnp.where((meta_ref[2] ^ slot) == offset, other, total)
-        inverse = lax.rsqrt(total / width + 1e-05)
-        rows = slice(slot * step, (slot + 1) * step)
-        gate = (keep_ref[0, rows, :].astype(F32) + arrived_ref[0, rows, :].astype(F32)) * inverse
-        up = (keep_ref[1, rows, :].astype(F32) + arrived_ref[1, rows, :].astype(F32)) * inverse
-        out_ref[rows, :] = (jax.nn.silu(gate) * up).astype(BF16)
-
-
-def activate(meta, keep, arrived, squares, start):
+def activate_kernel(depth, keep_ref, arrived_ref, squares_ref, out_ref):
+    inverse = lax.rsqrt(squares_ref[:, :1] / depth + 1e-05)
+    gate = (keep_ref[0].astype(F32) + arrived_ref[0].astype(F32)) * inverse
+    up = (keep_ref[1].astype(F32) + arrived_ref[1].astype(F32)) * inverse
+    out_ref[...] = (jax.nn.silu(gate) * up).astype(BF16)
+
+
+def activate(keep, arrived, squares):
     _, rows, width = keep.shape
     tile = tile_of(width)
     both = pl.BlockSpec((2, rows, tile), lambda n: (0, 0, n))
     return pl.pallas_call(
-        functools.partial(activate_kernel, len(squares), start, D),
+        functools.partial(activate_kernel, D),
         grid=(width // tile,),
         out_shape=jax.ShapeDtypeStruct((rows, width), BF16),
-        in_specs=[pl.BlockSpec(memory_space=pltpu.SMEM), both, both]
-        + [pl.BlockSpec(value.shape, lambda n: (0, 0)) for value in squares],
+        in_specs=[both, both, whole_block(squares.shape)],
         out_specs=pl.BlockSpec((rows, tile), lambda n: (0, n)),
         cost_estimate=cost(10 * rows * width, 14 * rows * width),
         name="activate",
         compiler_params=room(8),
-    )(meta, keep, arrived, *squares)
+    )(keep, arrived, squares)
 
 
 def join_kernel(near_ref, far_ref, out_ref):
@@ -359,25 +345,37 @@
     )(near, far)
 
 
-def sum_kernel(own_ref, *refs):
-    total = own_ref[...]
-    for ref in refs[:-1]:
+def sum_kernel(count, own_ref, *refs):
+    others, before, outs = refs[: count[0]], refs[count[0] : sum(count)], refs[sum(count) :]
+    total = own_ref[...].astype(F32)
+    for ref in others:
         total = total + ref[...].astype(F32)
-    refs[-1][...] = total.astype(BF16)
-
-
-def sum_rows(own, others):
-    whole = pl.BlockSpec(own.shape, lambda n: (0, 0))
-    return pl.pallas_call(
-        sum_kernel,
-        grid=(1,),
-        out_shape=jax.ShapeDtypeStruct(own.shape, BF16),
-        in_specs=[whole] * (1 + len(others)),
-        out_specs=whole,
+    outs[0][...] = total.astype(BF16)
+    row = 0
+    for ref in before:
+        outs[1][row : row + ref.shape[0], :] = ref[...]
+        row += ref.shape[0]
+    if before:
+        outs[1][row:, :] = total.astype(BF16)
+
+
+def sum_rows(own, others, before=()):
+    rows, width = own.shape
+    out_shape = [jax.ShapeDtypeStruct(own.shape, BF16)]
+    if before:
+        rows += sum(value.shape[0] for value in before)
+        out_shape.append(jax.ShapeDtypeStruct((rows, width), BF16))
+    operands = [own, *others, *before]
+    return pl.pallas_call(
+        functools.partial(sum_kernel, (len(others), len(before))),
+        grid=(1,),
+        out_shape=out_shape,
+        in_specs=[whole_block(value.shape) for value in operands],
+        out_specs=[whole_block(value.shape) for value in out_shape],
         cost_estimate=cost(own.size * len(others), 12 * own.size),
         name="sum_rows",
         compiler_params=room(8),
-    )(own, *others)
+    )(*operands)
 
 
 def predict_kernel(rows_ref, proj_ref, other_ref, out_own_ref, out_other_ref):
@@ -403,37 +401,30 @@
     )(rows, proj, other)
 
 
-def term_kernel(count, meta_ref, own_ref, other_ref, proj_ref, proj_other_ref, *refs):
-    outs, total_ref = refs[:count], refs[count]
+def term_kernel(own_ref, other_ref, proj_ref, proj_other_ref, out_ref):
     contract = (((1,), (1,)), ((), ()))
     total = lax.dot_general(own_ref[...], proj_ref[...], contract, preferred_element_type=F32)
-    total_ref[...] = total + lax.dot_general(
+    total = total + lax.dot_general(
         other_ref[...], proj_other_ref[...], contract, preferred_element_type=F32
     )
-    step = outs[0].shape[0]
-    for far in range(count):
-        start = pl.multiple_of((meta_ref[3] ^ far) * step, step)
-        outs[far][...] = total_ref[pl.ds(start, step), :].astype(outs[far].dtype)
-
-
-def student_term(meta, own, other, proj, proj_other, count):
-    rows = own.shape[0]
+    out_ref[...] = total.astype(BF16)
+
+
+def student_term(own, other, proj, proj_other):
+    rows, depth = own.shape
     width = proj.shape[0]
-    step = rows // count
-    piece = jax.ShapeDtypeStruct((step, width), BF16)
-    return pl.pallas_call(
-        functools.partial(term_kernel, count),
-        grid=(1,),
-        out_shape=[jax.ShapeDtypeStruct((step, width), F32)] + [piece] * (count - 1),
-        in_specs=[pl.BlockSpec(memory_space=pltpu.SMEM)]
-        + [whole_block(own.shape)] * 2
-        + [whole_block(proj.shape)] * 2,
-        out_specs=[whole_block((step, width))] * count,
-        scratch_shapes=[pltpu.VMEM((rows, width), F32)],
+    tile = tile_of(width, 512)
+    weight = pl.BlockSpec((tile, depth), lambda n: (n, 0))
+    return pl.pallas_call(
+        term_kernel,
+        grid=(width // tile,),
+        out_shape=jax.ShapeDtypeStruct((rows, width), BF16),
+        in_specs=[whole_block(own.shape)] * 2 + [weight] * 2,
+        out_specs=pl.BlockSpec((rows, tile), lambda n: (0, n)),
         cost_estimate=cost(4 * rows * proj.size, 4 * proj.size),
         name="student_term",
         compiler_params=room(14),
-    )(meta, own, other, proj, proj_other)
+    )(own, other, proj, proj_other)
 
 
 def pre_kernel(starts, meta_ref, own_ref, other_ref, *refs):
@@ -496,28 +487,25 @@
     )(own, other, *pieces)
 
 
-def place_kernel(count, step, cores, at_ref, *refs):
-    pieces, out_ref = refs[:count], refs[count]
-    for offset in range(count):
-        source = at_ref[1] ^ offset
-        slot = (source & (cores - 1)) * (count // cores) + (source >> (cores.bit_length() - 1))
-        start = pl.multiple_of(slot * step, step)
-        out_ref[pl.ds(start, step), :] = pieces[offset][...].astype(F32)
-
-
-def place(at, pieces, cores):
-    count = len(pieces)
-    step, width = pieces[0].shape
-    return pl.pallas_call(
-        functools.partial(place_kernel, count, step, cores),
-        grid=(1,),
-        out_shape=jax.ShapeDtypeStruct((count * step, width), F32),
-        in_specs=[pl.BlockSpec(memory_space=pltpu.SMEM)] + [whole_block((step, width))] * count,
-        out_specs=whole_block((count * step, width)),
-        cost_estimate=cost(count * step * width, 6 * count * step * width),
+def place_kernel(meta_ref, own_ref, other_ref, out_ref):
+    step = own_ref.shape[0]
+    for offset, ref in enumerate((own_ref, other_ref)):
+        start = pl.multiple_of((meta_ref[2] ^ offset) * step, step)
+        out_ref[pl.ds(start, step), :] = ref[...].astype(F32)
+
+
+def place(meta, own, other):
+    step, width = own.shape
+    return pl.pallas_call(
+        place_kernel,
+        grid=(1,),
+        out_shape=jax.ShapeDtypeStruct((2 * step, width), F32),
+        in_specs=[pl.BlockSpec(memory_space=pltpu.SMEM)] + [whole_block(own.shape)] * 2,
+        out_specs=whole_block((2 * step, width)),
+        cost_estimate=cost(own.size, 12 * own.size),
         name="place",
         compiler_params=room(4),
-    )(at, *pieces)
+    )(meta, own, other)
 
 
 def shards(tokens, norm_gain, gate_up_weight, down_weight, student_in, student_proj):
@@ -564,12 +552,6 @@
     steps = [local_rows * share // share_total for share in ROW_SHARES]
     starts = [sum(steps[:r]) for r in range(len(steps))]
 
-    total = row_squares(tokens)
-    for bit in bits:
-        total = total + over_grp(total, 1 << bit)
-    total = transpose(total)
-    squares = [total] + [over_inner(total, offset) for offset in range(1, cores)]
-
     gain = norm_gain[None, :]
 
     def gather_rows(r):
@@ -592,7 +574,10 @@
     teacher_parts = []
     target_parts = []
     for r, step in enumerate(steps):
-        x = prepare(meta, gather_rows(r), gain)
+        x, squares = prepare(meta, gather_rows(r), gain)
+        for bit in bits[::-1]:
+            half = squares.shape[0] // 2
+            squares = squares[:half] + over_grp(squares[half:], 1 << bit)
         before = None
         for chunk in range(COL_CHUNKS):
             u = r * COL_CHUNKS + chunk
@@ -604,7 +589,7 @@
                 arrived = over_grp(send, 1 << bit)
                 if stage < len(order) - 1:
                     keep, send = add_halves(keep, arrived)
-            hidden = activate(meta, keep, arrived, squares, starts[r])
+            hidden = activate(keep, arrived, squares)
             near, far_rows = gather(hidden, order)
             last = chunk == COL_CHUNKS - 1
             before = down_product(
@@ -621,26 +606,19 @@
             )
         keep, send = before
         result, *sends = split(keep, over_inner(send, 1), depth)
-        result = sum_rows(
-            result,
-            [over_inner(sends[far - 1], 2 * far) for far in range(1, depth)],
-        )
+        others = [over_inner(sends[far - 1], 2 * far) for far in range(1, depth)]
+        result, *teacher_out = sum_rows(result, others, teacher_parts)
         teacher_parts.append(result)
         target_parts.append(transpose(result))
 
-    teacher_out = jnp.concatenate(teacher_parts, axis=0)
+    teacher_out = teacher_out[0]
     pre_own, pre_other = pre_gradient(meta, predicted_own, predicted_other, target_parts, starts)
     pre_here = over_inner(pre_other, 1)
 
-    own, *sends = student_term(meta, pre_own, pre_other, student_proj, proj_other, depth)
-    total = sum_rows(own, [over_inner(sends[far - 1], 2 * far) for far in range(1, depth)])
-    pieces = [None] * inner
-    pieces[0] = total
-    for far in range(1, depth):
-        pieces[2 * far] = over_inner(total, 2 * far)
-    for far in range(depth):
-        pieces[2 * far + 1] = over_inner(pieces[2 * far], 1)
-    grad_student = place(meta, pieces, cores)
+    total = student_term(pre_own, pre_other, student_proj, proj_other)
+    for bit in range(1, inner.bit_length() - 1):
+        total = sum_rows(total, [over_inner(total, 1 << bit)])[0]
+    grad_student = place(meta, total, over_inner(total, 1))
 
     pre_pieces = []
     pre_places = []

time: 263 us -> 235 us (0.89)
  starting transfers between devices: 89.9 us -> 71 us
  Pallas kernels: 70.7 us -> 60.5 us
  waiting for transfers between devices: 96.8 us -> 100 us
    ppermute x63 -> x56, starting transfers between devices: 89.9 us -> 71 us  [move(): return lax.ppermute(value, AXES, pairs)]
    pallas_call x14, Pallas kernels: 44.3 us -> 36.4 us  [the longest x4 30.9 us: up_product(): pl.pallas_call(functools.partial(up_kernel, rows // len(blocks), blocks,...]
    ppermute x63 -> x56, waiting for transfers between devices: 96.8 us -> 100 us  [move(): return lax.ppermute(value, AXES, pairs)]
    pallas_call x4, Pallas kernels: 4.06 us -> 0.97 us  [add_halves(): pl.pallas_call(add_kernel, grid=(2,), out_shape=[jax.ShapeDtypeStruct((2,...]
  transfers between devices with their start and end apart: 63 -> 56, of which waited for: 20 -> 17; matrix products, arithmetic and copies ran while one was open for 1% -> 0% of each run, Pallas kernels for 26% -> 24%
where the time goes in v2:
time: 235 us
  waiting for transfers between devices  100 us (43%)
  starting transfers between devices  71 us (30%)
  Pallas kernels  60.5 us (26%)
    ppermute x56, waiting for transfers between devices, move(): return lax.ppermute(value, AXES, pairs)  100 us
    ppermute x56, starting transfers between devices, move(): return lax.ppermute(value, AXES, pairs)  71 us
    pallas_call x4, Pallas kernels, up_product(): pl.pallas_call(functools.partial(up_kernel, rows // len(blocks), blocks,...  30.9 us
    pallas_call x4, Pallas kernels, down_product(): pl.pallas_call(functools.partial(down_kernel, rows // len(blocks), step,...  14.6 us
  transfers between devices with their start and end apart: 56, of which 17 were waited for; matrix products, arithmetic and copies ran while one was open for 0% of the time, Pallas kernels for 24%

profile of v2, /device:TPU:0, one launch (start us, length us, event | category | flops | bytes accessed | tf_op | source)
XLA Modules:
  0.0 234.9 jit_solution(10512052299113930196)
XLA Ops:
  0.7 1.0 fusion
  1.7 3.1 %collective-permute-start.1 = (bf16[32,2048]{1,0:T(8,128)(2,1)S(1)}, bf16[32,2048]{1,0:T(8,128)(2,1)S(1)}, u32[]{:S(2)}, u32[]{:S(2)}) collective-permute-start(bf16[32,2048]{1,0:T(8,128)(2,1)S(1)} %get-tuple-element.84.refs_0_), channel_id=1, source_target_pairs={{0,2},{1,3},{2,0},{3,1},{4,6},{5,7},{6,4},{7,5},{8,10},{9,11},{10,... | collective-permute-start | bytes 393224 | tf_op jit(solution)/shard_map/ppermute | solution.py:531
  4.8 2.6 %collective-permute-start.3 = (bf16[32,2048]{1,0:T(8,128)(2,1)S(1)}, bf16[32,2048]{1,0:T(8,128)(2,1)S(1)}, u32[]{:S(2)}, u32[]{:S(2)}) collective-permute-start(bf16[32,2048]{1,0:T(8,128)(2,1)S(1)} %get-tuple-element.84.refs_0_), channel_id=1, source_target_pairs={{0,4},{1,5},{2,6},{3,7},{4,0},{5,1},{6,2},{7,3},{8,12},{9,13},{10,... | collective-permute-start | bytes 393224 | tf_op jit(solution)/shard_map/ppermute | solution.py:531
  7.9 3.9 %collective-permute-start.26 = (bf16[32,2048]{1,0:T(8,128)(2,1)S(1)}, bf16[32,2048]{1,0:T(8,128)(2,1)S(1)}, u32[]{:S(2)}, u32[]{:S(2)}) collective-permute-start(bf16[32,2048]{1,0:T(8,128)(2,1)S(1)} %get-tuple-element.83.refs_0_), channel_id=1, source_target_pairs={{0,6},{1,7},{2,4},{3,5},{4,2},{5,3},{6,0},{7,1},{8,14},{9,15},{10,... | collective-permute-start | bytes 393224 | tf_op jit(solution)/shard_map/ppermute | solution.py:531
  11.8 3.8 %collective-permute-start.5 = (bf16[32,2048]{1,0:T(8,128)(2,1)S(1)}, bf16[32,2048]{1,0:T(8,128)(2,1)S(1)}, u32[]{:S(2)}, u32[]{:S(2)}) collective-permute-start(bf16[32,2048]{1,0:T(8,128)(2,1)S(1)} %get-tuple-element.84.refs_0_), channel_id=1, source_target_pairs={{0,6},{1,7},{2,4},{3,5},{4,2},{5,3},{6,0},{7,1},{8,14},{9,15},{10,... | collective-permute-start | bytes 393224 | tf_op jit(solution)/shard_map/ppermute | solution.py:531
  16.2 9.5 %collective-permute-done.24.refs_4_ = bf16[32,2048]{1,0:T(8,128)(2,1)S(1)} collective-permute-done((bf16[32,2048]{1,0:T(8,128)(2,1)S(1)}, bf16[32,2048]{1,0:T(8,128)(2,1)S(1)}, u32[]{:S(2)}, u32[]{:S(2)}) %collective-permute-start.24) | collective-permute-done | bytes 131104 | tf_op jit(solution)/shard_map/ppermute | solution.py:531
  26.1 0.7 broadcast_in_dim.3.refs_8_
  27.9 1.0 prepare.3
  28.9 7.7 %up_product.6 = (bf16[2,128,1792]{2,1,0:T(8,128)(2,1)S(1)}, bf16[2,128,1792]{2,1,0:T(8,128)(2,1)S(1)}) custom-call(bf16[256,2048]{1,0:T(8,128)(2,1)S(1)} %get-tuple-element.61.x_ref, bf16[2,2048,3584]{2,1,0:T(8,128)(2,1)} %source_ref.7), custom_call_target="tpu_custom_call" | custom-call | flops 3758096384 | bytes 15728640 | tf_op jit(solution)/shard_map/up_product/pallas_call | solution.py:119
  36.6 7.7 %up_product.7 = (bf16[2,128,1792]{2,1,0:T(8,128)(2,1)S(1)}, bf16[2,128,1792]{2,1,0:T(8,128)(2,1)S(1)}) custom-call(bf16[256,2048]{1,0:T(8,128)(2,1)S(1)} %get-tuple-element.61.x_ref, bf16[2,2048,3584]{2,1,0:T(8,128)(2,1)} %source_ref.7), custom_call_target="tpu_custom_call" | custom-call | flops 3758096384 | bytes 15728640 | tf_op jit(solution)/shard_map/up_product/pallas_call | solution.py:119
  44.3 1.6 collective-permute-start.34
  45.9 1.0 prepare.2
  46.9 7.7 %up_product.4 = (bf16[2,128,1792]{2,1,0:T(8,128)(2,1)S(1)}, bf16[2,128,1792]{2,1,0:T(8,128)(2,1)S(1)}) custom-call(bf16[256,2048]{1,0:T(8,128)(2,1)S(1)} %get-tuple-element.45.x_ref, bf16[2,2048,3584]{2,1,0:T(8,128)(2,1)} %source_ref.7), custom_call_target="tpu_custom_call" | custom-call | flops 3758096384 | bytes 15728640 | tf_op jit(solution)/shard_map/up_product/pallas_call | solution.py:119
  54.6 1.6 collective-permute-start.7
  56.7 7.8 %up_product.5 = (bf16[2,128,1792]{2,1,0:T(8,128)(2,1)S(1)}, bf16[2,128,1792]{2,1,0:T(8,128)(2,1)S(1)}) custom-call(bf16[256,2048]{1,0:T(8,128)(2,1)S(1)} %get-tuple-element.45.x_ref, bf16[2,2048,3584]{2,1,0:T(8,128)(2,1)} %source_ref.7), custom_call_target="tpu_custom_call" | custom-call | flops 3758096384 | bytes 15728640 | tf_op jit(solution)/shard_map/up_product/pallas_call | solution.py:119
  64.5 0.6 collective-permute-start.13
  65.1 1.5 collective-permute-start.30
  67.3 1.6 collective-permute-start.35
  68.8 30.1 %collective-permute-done.30 = f32[128,128]{1,0:T(8,128)S(1)} collective-permute-done((f32[128,128]{1,0:T(8,128)S(1)}, f32[128,128]{1,0:T(8,128)S(1)}, u32[]{:S(2)}, u32[]{:S(2)}) %collective-permute-start.30) | collective-permute-done | bytes 65568 | tf_op jit(solution)/shard_map/ppermute | solution.py:531
  99.0 0.6 collective-permute-start.31
  99.6 1.6 collective-permute-start.9
  101.4 1.9 collective-permute-done.31
  104.1 1.6 collective-permute-start.8
  105.9 1.6 collective-permute-start.14
  107.5 1.3 collective-permute-done.35.arrived_ref
  109.2 0.6 collective-permute-start.36
  110.2 1.2 collective-permute-start.10
  111.4 5.3 %collective-permute-done.29.arrived_ref = bf16[2,64,1792]{2,1,0:T(8,128)(2,1)S(1)} collective-permute-done((bf16[2,64,1792]{2,1,0:T(8,128)(2,1)S(1)}, bf16[2,64,1792]{2,1,0:T(8,128)(2,1)S(1)}, u32[]{:S(2)}, u32[]{:S(2)}) %collective-permute-start.29) | collective-permute-done | bytes 458784 | tf_op jit(solution)/shard_map/ppermute | solution.py:531
  117.1 10.6 %collective-permute-done.36.far_ref = bf16[64,1792]{1,0:T(8,128)(2,1)S(1)} collective-permute-done((bf16[64,1792]{1,0:T(8,128)(2,1)S(1)}, bf16[64,1792]{1,0:T(8,128)(2,1)S(1)}, u32[]{:S(2)}, u32[]{:S(2)}) %collective-permute-start.36) | collective-permute-done | bytes 229408 | tf_op jit(solution)/shard_map/ppermute | solution.py:531
  127.7 1.5 collective-permute-start.32
  130.9 5.3 %collective-permute-done.32.far_ref = bf16[64,1792]{1,0:T(8,128)(2,1)S(1)} collective-permute-done((bf16[64,1792]{1,0:T(8,128)(2,1)S(1)}, bf16[64,1792]{1,0:T(8,128)(2,1)S(1)}, u32[]{:S(2)}, u32[]{:S(2)}) %collective-permute-start.32) | collective-permute-done | bytes 229408 | tf_op jit(solution)/shard_map/ppermute | solution.py:531
  137.3 1.6 collective-permute-start.11
  138.9 1.1 collective-permute-start.16
  140.0 10.6 %collective-permute-done.11.far_ref = bf16[64,1792]{1,0:T(8,128)(2,1)S(1)} collective-permute-done((bf16[64,1792]{1,0:T(8,128)(2,1)S(1)}, bf16[64,1792]{1,0:T(8,128)(2,1)S(1)}, u32[]{:S(2)}, u32[]{:S(2)}) %collective-permute-start.11) | collective-permute-done | bytes 229408 | tf_op jit(solution)/shard_map/ppermute | solution.py:531
  151.3 3.5 %down_product.6.refs_2_ = f32[256,2048]{1,0:T(8,128)S(1)} custom-call(s32[4]{0:T(128)S(1)} %pad_add_fusion.at_ref.meta_ref, bf16[128,1792]{1,0:T(8,128)(2,1)S(1)} %join.10.near_ref, bf16[128,1792]{1,0:T(8,128)(2,1)S(1)} %collective-permute-done.37.far_ref, bf16[3584,2048]{1,0:T(8,128)(2,1)S(1)} %bitcast.5, bf16[3584,2048]{1,0:T(8,128)(2,1)S(1)} %bitcast.5), custom_call_target="tpu_custom_call" | custom-call | flops 1879048192 | bytes 8257536 | tf_op jit(solution)/shard_map/down_product/pallas_call | solution.py:270
  154.8 3.7 %down_product.7 = (f32[128,2048]{1,0:T(8,128)S(1)}, bf16[128,2048]{1,0:T(8,128)(2,1)S(1)}) custom-call(s32[4]{0:T(128)S(1)} %pad_add_fusion.at_ref.meta_ref, bf16[128,1792]{1,0:T(8,128)(2,1)S(1)} %join.9.near_ref, bf16[128,1792]{1,0:T(8,128)(2,1)S(1)} %collective-permute-done.33.far_ref, bf16[3584,2048]{1,0:T(8,128)(2,1)S(1)} %bitcast.5, ...), custom_call_target="tpu_custom_call" | custom-call | flops 1879048192 | bytes 8257536 | tf_op jit(solution)/shard_map/down_product/pallas_call | solution.py:270
  158.6 3.5 %down_product.4.refs_2_ = f32[256,2048]{1,0:T(8,128)S(1)} custom-call(s32[4]{0:T(128)S(1)} %pad_add_fusion.at_ref.meta_ref, bf16[128,1792]{1,0:T(8,128)(2,1)S(1)} %join.8.near_ref, bf16[128,1792]{1,0:T(8,128)(2,1)S(1)} %collective-permute-done.16.far_ref, bf16[3584,2048]{1,0:T(8,128)(2,1)S(1)} %bitcast.5, bf16[3584,2048]{1,0:T(8,128)(2,1)S(1)} %bitcast.5), custom_call_target="tpu_custom_call" | custom-call | flops 1879048192 | bytes 8257536 | tf_op jit(solution)/shard_map/down_product/pallas_call | solution.py:270
  162.2 3.9 %down_product.5 = (f32[128,2048]{1,0:T(8,128)S(1)}, bf16[128,2048]{1,0:T(8,128)(2,1)S(1)}) custom-call(s32[4]{0:T(128)S(1)} %pad_add_fusion.at_ref.meta_ref, bf16[128,1792]{1,0:T(8,128)(2,1)S(1)} %join.7.near_ref, bf16[128,1792]{1,0:T(8,128)(2,1)S(1)} %collective-permute-done.12.far_ref, bf16[3584,2048]{1,0:T(8,128)(2,1)S(1)} %bitcast.5, ...), custom_call_target="tpu_custom_call" | custom-call | flops 1879048192 | bytes 8257536 | tf_op jit(solution)/shard_map/down_product/pallas_call | solution.py:270
  167.1 1.6 collective-permute-start.48
  168.9 4.1 %collective-permute-start.39 = (bf16[32,2048]{1,0:T(8,128)(2,1)S(1)}, bf16[32,2048]{1,0:T(8,128)(2,1)S(1)}, u32[]{:S(2)}, u32[]{:S(2)}) collective-permute-start(bf16[32,2048]{1,0:T(8,128)(2,1)S(1)} %get-tuple-element.74), channel_id=1, source_target_pairs={{0,2},{1,3},{2,0},{3,1},{4,6},{5,7},{6,4},{7,5},{8,10},{9,11},{10,... | collective-permute-start | bytes 393224 | tf_op jit(solution)/shard_map/ppermute | solution.py:531
  172.9 1.1 collective-permute-start.40
  174.0 1.4 collective-permute-start.41
  175.5 1.1 collective-permute-start.18
  176.7 1.7 collective-permute-done.39.refs_0_
  178.3 2.0 collective-permute-start.19
  180.3 5.5 %collective-permute-done.40.refs_1_ = bf16[32,2048]{1,0:T(8,128)(2,1)S(1)} collective-permute-done((bf16[32,2048]{1,0:T(8,128)(2,1)S(1)}, bf16[32,2048]{1,0:T(8,128)(2,1)S(1)}, u32[]{:S(2)}, u32[]{:S(2)}) %collective-permute-start.40) | collective-permute-done | bytes 131104 | tf_op jit(solution)/shard_map/ppermute | solution.py:531
  185.8 2.5 %collective-permute-start.20 = (bf16[32,2048]{1,0:T(8,128)(2,1)S(1)}, bf16[32,2048]{1,0:T(8,128)(2,1)S(1)}, u32[]{:S(2)}, u32[]{:S(2)}) collective-permute-start(bf16[32,2048]{1,0:T(8,128)(2,1)S(1)} %get-tuple-element.60), channel_id=1, source_target_pairs={{0,6},{1,7},{2,4},{3,5},{4,2},{5,3},{6,0},{7,1},{8,14},{9,15},{10,... | collective-permute-start | bytes 393224 | tf_op jit(solution)/shard_map/ppermute | solution.py:531
  188.3 1.6 collective-permute-start.49
  189.9 0.7 collective-permute-start.43
  190.6 9.2 %collective-permute-done.19.refs_1_ = bf16[32,2048]{1,0:T(8,128)(2,1)S(1)} collective-permute-done((bf16[32,2048]{1,0:T(8,128)(2,1)S(1)}, bf16[32,2048]{1,0:T(8,128)(2,1)S(1)}, u32[]{:S(2)}, u32[]{:S(2)}) %collective-permute-start.19) | collective-permute-done | bytes 131104 | tf_op jit(solution)/shard_map/ppermute | solution.py:531
  199.8 0.8 sum_rows.5
  200.6 0.7 collective-permute-start.44
  201.3 1.3 predict.1
  202.6 0.6 pre_gradient.1
  204.1 1.5 student_term.1.own_ref
  205.7 10.6 %collective-permute-start.45 = (bf16[64,1024]{1,0:T(8,128)(2,1)S(1)}, bf16[64,1024]{1,0:T(8,128)(2,1)S(1)}, u32[]{:S(2)}, u32[]{:S(2)}) collective-permute-start(bf16[64,1024]{1,0:T(8,128)(2,1)S(1)} %student_term.1.own_ref), channel_id=1, source_target_pairs={{0,2},{1,3},{2,0},{3,1},{4,6},{5,7},{6,4},{7,5},{8,10},{9,11},{10,... | collective-permute-start | bytes 393224 | tf_op jit(solution)/shard_map/ppermute | solution.py:531
  216.2 0.9 collective-permute-start.51
  217.1 2.8 %collective-permute-done.45.refs_0_ = bf16[64,1024]{1,0:T(8,128)(2,1)S(1)} collective-permute-done((bf16[64,1024]{1,0:T(8,128)(2,1)S(1)}, bf16[64,1024]{1,0:T(8,128)(2,1)S(1)}, u32[]{:S(2)}, u32[]{:S(2)}) %collective-permute-start.45) | collective-permute-done | bytes 131104 | tf_op jit(solution)/shard_map/ppermute | solution.py:531
  220.0 1.6 collective-permute-start.46
  221.6 2.3 collective-permute-start.52
  224.2 4.4 %collective-permute-done.46.refs_0_ = bf16[64,1024]{1,0:T(8,128)(2,1)S(1)} collective-permute-done((bf16[64,1024]{1,0:T(8,128)(2,1)S(1)}, bf16[64,1024]{1,0:T(8,128)(2,1)S(1)}, u32[]{:S(2)}, u32[]{:S(2)}) %collective-permute-start.46) | collective-permute-done | bytes 131104 | tf_op jit(solution)/shard_map/ppermute | solution.py:531
  228.7 1.3 collective-permute-done.47.other_ref
  230.1 1.4 place.1
  231.4 3.4 %proj_product.1 = f32[1024,1024]{1,0:T(8,128)} custom-call(bf16[1024,256]{1,0:T(8,128)(2,1)S(1)} %turn.1.own_ref, bf16[1024,256]{1,0:T(8,128)(2,1)S(1)} %collective-permute-done.50.other_ref, bf16[128,1024]{1,0:T(8,128)(2,1)S(1)} %join.12.refs_0_, bf16[128,1024]{1,0:T(8,128)(2,1)S(1)} %collective-permute-done.52.refs_1_, ...), custom_call_target="tpu_custom_call" | custom-call | flops 1073741824 | bytes 5242880 | tf_op jit(solution)/shard_map/proj_product/pallas_call | solution.py:476
  (110 shorter events, 12.4 us)
Async XLA Ops:
  1.7 10.1 %collective-permute-start.1 = (bf16[32,2048]{1,0:T(8,128)(2,1)S(1)}, bf16[32,2048]{1,0:T(8,128)(2,1)S(1)}, u32[]{:S(2)}, u32[]{:S(2)}) collective-permute-start(bf16[32,2048]{1,0:T(8,128)(2,1)S(1)} %get-tuple-element.84.refs_0_), channel_id=1, source_target_pairs={{0,2},{1,3},{2,0},{3,1},{4,6},{5,7},{6,4},{7,5},{8,10},{9,11},{10,... | collective-permute-start | bytes 393224 | tf_op jit(solution)/shard_map/ppermute | solution.py:531
  4.8 10.8 %collective-permute-start.3 = (bf16[32,2048]{1,0:T(8,128)(2,1)S(1)}, bf16[32,2048]{1,0:T(8,128)(2,1)S(1)}, u32[]{:S(2)}, u32[]{:S(2)}) collective-permute-start(bf16[32,2048]{1,0:T(8,128)(2,1)S(1)} %get-tuple-element.84.refs_0_), channel_id=1, source_target_pairs={{0,4},{1,5},{2,6},{3,7},{4,0},{5,1},{6,2},{7,3},{8,12},{9,13},{10,... | collective-permute-start | bytes 393224 | tf_op jit(solution)/shard_map/ppermute | solution.py:531
  7.4 8.4 %collective-permute-start.22 = (bf16[32,2048]{1,0:T(8,128)(2,1)S(1)}, bf16[32,2048]{1,0:T(8,128)(2,1)S(1)}, u32[]{:S(2)}, u32[]{:S(2)}) collective-permute-start(bf16[32,2048]{1,0:T(8,128)(2,1)S(1)} %get-tuple-element.83.refs_0_), channel_id=1, source_target_pairs={{0,2},{1,3},{2,0},{3,1},{4,6},{5,7},{6,4},{7,5},{8,10},{9,11},{10,... | collective-permute-start | bytes 393224 | tf_op jit(solution)/shard_map/ppermute | solution.py:531
  7.9 17.8 %collective-permute-start.24 = (bf16[32,2048]{1,0:T(8,128)(2,1)S(1)}, bf16[32,2048]{1,0:T(8,128)(2,1)S(1)}, u32[]{:S(2)}, u32[]{:S(2)}) collective-permute-start(bf16[32,2048]{1,0:T(8,128)(2,1)S(1)} %get-tuple-element.83.refs_0_), channel_id=1, source_target_pairs={{0,4},{1,5},{2,6},{3,7},{4,0},{5,1},{6,2},{7,3},{8,12},{9,13},{10,... | collective-permute-start | bytes 393224 | tf_op jit(solution)/shard_map/ppermute | solution.py:531
  7.9 17.8 %collective-permute-start.26 = (bf16[32,2048]{1,0:T(8,128)(2,1)S(1)}, bf16[32,2048]{1,0:T(8,128)(2,1)S(1)}, u32[]{:S(2)}, u32[]{:S(2)}) collective-permute-start(bf16[32,2048]{1,0:T(8,128)(2,1)S(1)} %get-tuple-element.83.refs_0_), channel_id=1, source_target_pairs={{0,6},{1,7},{2,4},{3,5},{4,2},{5,3},{6,0},{7,1},{8,14},{9,15},{10,... | collective-permute-start | bytes 393224 | tf_op jit(solution)/shard_map/ppermute | solution.py:531
  11.8 15.0 %collective-permute-start.5 = (bf16[32,2048]{1,0:T(8,128)(2,1)S(1)}, bf16[32,2048]{1,0:T(8,128)(2,1)S(1)}, u32[]{:S(2)}, u32[]{:S(2)}) collective-permute-start(bf16[32,2048]{1,0:T(8,128)(2,1)S(1)} %get-tuple-element.84.refs_0_), channel_id=1, source_target_pairs={{0,6},{1,7},{2,4},{3,5},{4,2},{5,3},{6,0},{7,1},{8,14},{9,15},{10,... | collective-permute-start | bytes 393224 | tf_op jit(solution)/shard_map/ppermute | solution.py:531
  15.6 11.3 %collective-permute-start.21 = (bf16[32,2048]{1,0:T(8,128)(2,1)S(1)}, bf16[32,2048]{1,0:T(8,128)(2,1)S(1)}, u32[]{:S(2)}, u32[]{:S(2)}) collective-permute-start(bf16[32,2048]{1,0:T(8,128)(2,1)S(1)} %get-tuple-element.83.refs_0_), channel_id=1, source_target_pairs={{0,1},{1,0},{2,3},{3,2},{4,5},{5,4},{6,7},{7,6},{8,9},{9,8},{10,11... | collective-permute-start | bytes 393224 | tf_op jit(solution)/shard_map/ppermute | solution.py:531
  15.8 11.6 %collective-permute-start.23 = (bf16[32,2048]{1,0:T(8,128)(2,1)S(1)}, bf16[32,2048]{1,0:T(8,128)(2,1)S(1)}, u32[]{:S(2)}, u32[]{:S(2)}) collective-permute-start(bf16[32,2048]{1,0:T(8,128)(2,1)S(1)} %collective-permute-done.22.refs_2_), channel_id=1, source_target_pairs={{0,1},{1,0},{2,3},{3,2},{4,5},{5,4},{6,7},{7,6},{8,9},{9,8},{10,11... | collective-permute-start | bytes 393224 | tf_op jit(solution)/shard_map/ppermute | solution.py:531
  25.6 1.9 collective-permute-start.25
  25.6 2.3 collective-permute-start.27
  26.8 19.0 %collective-permute-start = (bf16[32,2048]{1,0:T(8,128)(2,1)S(1)}, bf16[32,2048]{1,0:T(8,128)(2,1)S(1)}, u32[]{:S(2)}, u32[]{:S(2)}) collective-permute-start(bf16[32,2048]{1,0:T(8,128)(2,1)S(1)} %get-tuple-element.84.refs_0_), channel_id=1, source_target_pairs={{0,1},{1,0},{2,3},{3,2},{4,5},{5,4},{6,7},{7,6},{8,9},{9,8},{10,11... | collective-permute-start | bytes 393224 | tf_op jit(solution)/shard_map/ppermute | solution.py:531
  26.9 18.9 %collective-permute-start.2 = (bf16[32,2048]{1,0:T(8,128)(2,1)S(1)}, bf16[32,2048]{1,0:T(8,128)(2,1)S(1)}, u32[]{:S(2)}, u32[]{:S(2)}) collective-permute-start(bf16[32,2048]{1,0:T(8,128)(2,1)S(1)} %collective-permute-done.1.refs_2_), channel_id=1, source_target_pairs={{0,1},{1,0},{2,3},{3,2},{4,5},{5,4},{6,7},{7,6},{8,9},{9,8},{10,11... | collective-permute-start | bytes 393224 | tf_op jit(solution)/shard_map/ppermute | solution.py:531
  27.4 18.5 %collective-permute-start.4 = (bf16[32,2048]{1,0:T(8,128)(2,1)S(1)}, bf16[32,2048]{1,0:T(8,128)(2,1)S(1)}, u32[]{:S(2)}, u32[]{:S(2)}) collective-permute-start(bf16[32,2048]{1,0:T(8,128)(2,1)S(1)} %collective-permute-done.3.refs_4_), channel_id=1, source_target_pairs={{0,1},{1,0},{2,3},{3,2},{4,5},{5,4},{6,7},{7,6},{8,9},{9,8},{10,11... | collective-permute-start | bytes 393224 | tf_op jit(solution)/shard_map/ppermute | solution.py:531
  27.5 18.4 %collective-permute-start.6 = (bf16[32,2048]{1,0:T(8,128)(2,1)S(1)}, bf16[32,2048]{1,0:T(8,128)(2,1)S(1)}, u32[]{:S(2)}, u32[]{:S(2)}) collective-permute-start(bf16[32,2048]{1,0:T(8,128)(2,1)S(1)} %collective-permute-done.5.refs_6_), channel_id=1, source_target_pairs={{0,1},{1,0},{2,3},{3,2},{4,5},{5,4},{6,7},{7,6},{8,9},{9,8},{10,11... | collective-permute-start | bytes 393224 | tf_op jit(solution)/shard_map/ppermute | solution.py:531
  44.3 22.7 %collective-permute-start.34 = (bf16[2,128,1792]{2,1,0:T(8,128)(2,1)S(1)}, bf16[2,128,1792]{2,1,0:T(8,128)(2,1)S(1)}, u32[]{:S(2)}, u32[]{:S(2)}) collective-permute-start(bf16[2,128,1792]{2,1,0:T(8,128)(2,1)S(1)} %get-tuple-element.68), channel_id=1, source_target_pairs={{0,8},{1,9},{2,10},{3,11},{4,12},{5,13},{6,14},{7,15},{8,0},{9,1},... | collective-permute-start | bytes 2752520 | tf_op jit(solution)/shard_map/ppermute | solution.py:531
  54.6 49.3 %collective-permute-start.7 = (bf16[2,128,1792]{2,1,0:T(8,128)(2,1)S(1)}, bf16[2,128,1792]{2,1,0:T(8,128)(2,1)S(1)}, u32[]{:S(2)}, u32[]{:S(2)}) collective-permute-start(bf16[2,128,1792]{2,1,0:T(8,128)(2,1)S(1)} %get-tuple-element.47), channel_id=1, source_target_pairs={{0,16},{1,17},{2,18},{3,19},{4,20},{5,21},{6,22},{7,23},{8,24},{9,... | collective-permute-start | bytes 2752520 | tf_op jit(solution)/shard_map/ppermute | solution.py:531
  56.2 43.4 %collective-permute-start.28 = (bf16[2,128,1792]{2,1,0:T(8,128)(2,1)S(1)}, bf16[2,128,1792]{2,1,0:T(8,128)(2,1)S(1)}, u32[]{:S(2)}, u32[]{:S(2)}) collective-permute-start(bf16[2,128,1792]{2,1,0:T(8,128)(2,1)S(1)} %get-tuple-element.63), channel_id=1, source_target_pairs={{0,16},{1,17},{2,18},{3,19},{4,20},{5,21},{6,22},{7,23},{8,24},{9,... | collective-permute-start | bytes 2752520 | tf_op jit(solution)/shard_map/ppermute | solution.py:531
  56.7 94.6 %slice-start = ((s8[14680064]{0:T(1024)(128)(4,1)}), s8[2097152]{0:T(1024)(128)(4,1)S(1)}, s32[]{:S(2)}) async-start(s8[14680064]{0:T(1024)(128)(4,1)} %bitcast.4), calls=%async_computation | async-start | bytes 4194304
  56.7 94.6 %slice-start.1 = ((s8[14680064]{0:T(1024)(128)(4,1)}), s8[4194304]{0:T(1024)(128)(4,1)S(1)}, s32[]{:S(2)}) async-start(s8[14680064]{0:T(1024)(128)(4,1)} %bitcast.4), calls=%async_computation.1 | async-start | bytes 8388608
  56.7 94.6 %slice-start.2 = ((s8[14680064]{0:T(1024)(128)(4,1)}), s8[4194304]{0:T(1024)(128)(4,1)S(1)}, s32[]{:S(2)}) async-start(s8[14680064]{0:T(1024)(128)(4,1)} %bitcast.4), calls=%async_computation.2 | async-start | bytes 8388608
  64.5 41.2 %collective-permute-start.13 = (bf16[2,128,1792]{2,1,0:T(8,128)(2,1)S(1)}, bf16[2,128,1792]{2,1,0:T(8,128)(2,1)S(1)}, u32[]{:S(2)}, u32[]{:S(2)}) collective-permute-start(bf16[2,128,1792]{2,1,0:T(8,128)(2,1)S(1)} %get-tuple-element.52), channel_id=1, source_target_pairs={{0,8},{1,9},{2,10},{3,11},{4,12},{5,13},{6,14},{7,15},{8,0},{9,1},... | collective-permute-start | bytes 2752520 | tf_op jit(solution)/shard_map/ppermute | solution.py:531
  65.1 33.8 %collective-permute-start.30 = (f32[128,128]{1,0:T(8,128)S(1)}, f32[128,128]{1,0:T(8,128)S(1)}, u32[]{:S(2)}, u32[]{:S(2)}) collective-permute-start(f32[128,128]{1,0:T(8,128)S(1)} %slice.37), channel_id=1, source_target_pairs={{0,16},{1,17},{2,18},{3,19},{4,20},{5,21},{6,22},{7,23},{8,24},{9,... | collective-permute-start | bytes 196616 | tf_op jit(solution)/shard_map/ppermute | solution.py:531
  67.3 41.5 %collective-permute-start.35 = (bf16[2,64,1792]{2,1,0:T(8,128)(2,1)S(1)}, bf16[2,64,1792]{2,1,0:T(8,128)(2,1)S(1)}, u32[]{:S(2)}, u32[]{:S(2)}) collective-permute-start(bf16[2,64,1792]{2,1,0:T(8,128)(2,1)S(1)} %get-tuple-element.70), channel_id=1, source_target_pairs={{0,16},{1,17},{2,18},{3,19},{4,20},{5,21},{6,22},{7,23},{8,24},{9,... | collective-permute-start | bytes 1376264 | tf_op jit(solution)/shard_map/ppermute | solution.py:531
  99.0 4.3 %collective-permute-start.31 = (f32[64,128]{1,0:T(8,128)S(1)}, f32[64,128]{1,0:T(8,128)S(1)}, u32[]{:S(2)}, u32[]{:S(2)}) collective-permute-start(f32[64,128]{1,0:T(8,128)S(1)} %slice.43), channel_id=1, source_target_pairs={{0,8},{1,9},{2,10},{3,11},{4,12},{5,13},{6,14},{7,15},{8,0},{9,1},... | collective-permute-start | bytes 98312 | tf_op jit(solution)/shard_map/ppermute | solution.py:531
  99.6 10.6 %collective-permute-start.9 = (f32[128,128]{1,0:T(8,128)S(1)}, f32[128,128]{1,0:T(8,128)S(1)}, u32[]{:S(2)}, u32[]{:S(2)}) collective-permute-start(f32[128,128]{1,0:T(8,128)S(1)} %slice.32), channel_id=1, source_target_pairs={{0,16},{1,17},{2,18},{3,19},{4,20},{5,21},{6,22},{7,23},{8,24},{9,... | collective-permute-start | bytes 196616 | tf_op jit(solution)/shard_map/ppermute | solution.py:531
  103.3 13.4 %collective-permute-start.29 = (bf16[2,64,1792]{2,1,0:T(8,128)(2,1)S(1)}, bf16[2,64,1792]{2,1,0:T(8,128)(2,1)S(1)}, u32[]{:S(2)}, u32[]{:S(2)}) collective-permute-start(bf16[2,64,1792]{2,1,0:T(8,128)(2,1)S(1)} %get-tuple-element.65), channel_id=1, source_target_pairs={{0,8},{1,9},{2,10},{3,11},{4,12},{5,13},{6,14},{7,15},{8,0},{9,1},... | collective-permute-start | bytes 1376264 | tf_op jit(solution)/shard_map/ppermute | solution.py:531
  104.1 12.6 %copy-start = (bf16[1024,1024]{1,0:T(8,128)(2,1)S(1)}, bf16[1024,1024]{1,0:T(8,128)(2,1)}, u32[]{:S(2)}) copy-start(bf16[1024,1024]{1,0:T(8,128)(2,1)} %proj_ref.3) | copy-start | bytes 6291460
  104.1 32.7 %collective-permute-start.8 = (bf16[2,64,1792]{2,1,0:T(8,128)(2,1)S(1)}, bf16[2,64,1792]{2,1,0:T(8,128)(2,1)S(1)}, u32[]{:S(2)}, u32[]{:S(2)}) collective-permute-start(bf16[2,64,1792]{2,1,0:T(8,128)(2,1)S(1)} %get-tuple-element.49), channel_id=1, source_target_pairs={{0,8},{1,9},{2,10},{3,11},{4,12},{5,13},{6,14},{7,15},{8,0},{9,1},... | collective-permute-start | bytes 1376264 | tf_op jit(solution)/shard_map/ppermute | solution.py:531
  105.7 45.6 %slice-start.3 = ((s8[14680064]{0:T(1024)(128)(4,1)}), s8[4194304]{0:T(1024)(128)(4,1)S(1)}, s32[]{:S(2)}) async-start(s8[14680064]{0:T(1024)(128)(4,1)} %bitcast.4), calls=%async_computation.3 | async-start | bytes 8388608
  105.9 24.0 %collective-permute-start.14 = (bf16[2,64,1792]{2,1,0:T(8,128)(2,1)S(1)}, bf16[2,64,1792]{2,1,0:T(8,128)(2,1)S(1)}, u32[]{:S(2)}, u32[]{:S(2)}) collective-permute-start(bf16[2,64,1792]{2,1,0:T(8,128)(2,1)S(1)} %get-tuple-element.54), channel_id=1, source_target_pairs={{0,16},{1,17},{2,18},{3,19},{4,20},{5,21},{6,22},{7,23},{8,24},{9,... | collective-permute-start | bytes 1376264 | tf_op jit(solution)/shard_map/ppermute | solution.py:531
  109.2 18.5 %collective-permute-start.36 = (bf16[64,1792]{1,0:T(8,128)(2,1)S(1)}, bf16[64,1792]{1,0:T(8,128)(2,1)S(1)}, u32[]{:S(2)}, u32[]{:S(2)}) collective-permute-start(bf16[64,1792]{1,0:T(8,128)(2,1)S(1)} %activate.7.near_ref), channel_id=1, source_target_pairs={{0,8},{1,9},{2,10},{3,11},{4,12},{5,13},{6,14},{7,15},{8,0},{9,1},... | collective-permute-start | bytes 688136 | tf_op jit(solution)/shard_map/ppermute | solution.py:531
  110.2 19.1 %collective-permute-start.10 = (f32[64,128]{1,0:T(8,128)S(1)}, f32[64,128]{1,0:T(8,128)S(1)}, u32[]{:S(2)}, u32[]{:S(2)}) collective-permute-start(f32[64,128]{1,0:T(8,128)S(1)} %slice.41), channel_id=1, source_target_pairs={{0,8},{1,9},{2,10},{3,11},{4,12},{5,13},{6,14},{7,15},{8,0},{9,1},... | collective-permute-start | bytes 98312 | tf_op jit(solution)/shard_map/ppermute | solution.py:531
  116.7 84.6 %collective-permute-start.42 = (bf16[1024,1024]{1,0:T(8,128)(2,1)S(1)}, bf16[1024,1024]{1,0:T(8,128)(2,1)S(1)}, u32[]{:S(2)}, u32[]{:S(2)}) collective-permute-start(bf16[1024,1024]{1,0:T(8,128)(2,1)S(1)} %copy-done), channel_id=1, source_target_pairs={{0,1},{1,0},{2,3},{3,2},{4,5},{5,4},{6,7},{7,6},{8,9},{9,8},{10,11... | collective-permute-start | bytes 6291464 | tf_op jit(solution)/shard_map/ppermute | solution.py:531
  127.7 8.5 %collective-permute-start.32 = (bf16[64,1792]{1,0:T(8,128)(2,1)S(1)}, bf16[64,1792]{1,0:T(8,128)(2,1)S(1)}, u32[]{:S(2)}, u32[]{:S(2)}) collective-permute-start(bf16[64,1792]{1,0:T(8,128)(2,1)S(1)} %activate.6.near_ref), channel_id=1, source_target_pairs={{0,16},{1,17},{2,18},{3,19},{4,20},{5,21},{6,22},{7,23},{8,24},{9,... | collective-permute-start | bytes 688136 | tf_op jit(solution)/shard_map/ppermute | solution.py:531
  129.3 21.9 %collective-permute-start.37 = (bf16[128,1792]{1,0:T(8,128)(2,1)S(1)}, bf16[128,1792]{1,0:T(8,128)(2,1)S(1)}, u32[]{:S(2)}, u32[]{:S(2)}) collective-permute-start(bf16[128,1792]{1,0:T(8,128)(2,1)S(1)} %join.10.near_ref), channel_id=1, source_target_pairs={{0,16},{1,17},{2,18},{3,19},{4,20},{5,21},{6,22},{7,23},{8,24},{9,... | collective-permute-start | bytes 1376264 | tf_op jit(solution)/shard_map/ppermute | solution.py:531
  130.3 8.5 %collective-permute-start.15 = (bf16[64,1792]{1,0:T(8,128)(2,1)S(1)}, bf16[64,1792]{1,0:T(8,128)(2,1)S(1)}, u32[]{:S(2)}, u32[]{:S(2)}) collective-permute-start(bf16[64,1792]{1,0:T(8,128)(2,1)S(1)} %activate.5.near_ref), channel_id=1, source_target_pairs={{0,8},{1,9},{2,10},{3,11},{4,12},{5,13},{6,14},{7,15},{8,0},{9,1},... | collective-permute-start | bytes 688136 | tf_op jit(solution)/shard_map/ppermute | solution.py:531
  136.3 18.5 %collective-permute-start.33 = (bf16[128,1792]{1,0:T(8,128)(2,1)S(1)}, bf16[128,1792]{1,0:T(8,128)(2,1)S(1)}, u32[]{:S(2)}, u32[]{:S(2)}) collective-permute-start(bf16[128,1792]{1,0:T(8,128)(2,1)S(1)} %join.9.near_ref), channel_id=1, source_target_pairs={{0,8},{1,9},{2,10},{3,11},{4,12},{5,13},{6,14},{7,15},{8,0},{9,1},... | collective-permute-start | bytes 1376264 | tf_op jit(solution)/shard_map/ppermute | solution.py:531
  137.3 13.4 %collective-permute-start.11 = (bf16[64,1792]{1,0:T(8,128)(2,1)S(1)}, bf16[64,1792]{1,0:T(8,128)(2,1)S(1)}, u32[]{:S(2)}, u32[]{:S(2)}) collective-permute-start(bf16[64,1792]{1,0:T(8,128)(2,1)S(1)} %activate.4.near_ref), channel_id=1, source_target_pairs={{0,16},{1,17},{2,18},{3,19},{4,20},{5,21},{6,22},{7,23},{8,24},{9,... | collective-permute-start | bytes 688136 | tf_op jit(solution)/shard_map/ppermute | solution.py:531
  138.9 19.7 %collective-permute-start.16 = (bf16[128,1792]{1,0:T(8,128)(2,1)S(1)}, bf16[128,1792]{1,0:T(8,128)(2,1)S(1)}, u32[]{:S(2)}, u32[]{:S(2)}) collective-permute-start(bf16[128,1792]{1,0:T(8,128)(2,1)S(1)} %join.8.near_ref), channel_id=1, source_target_pairs={{0,16},{1,17},{2,18},{3,19},{4,20},{5,21},{6,22},{7,23},{8,24},{9,... | collective-permute-start | bytes 1376264 | tf_op jit(solution)/shard_map/ppermute | solution.py:531
  150.7 11.5 %collective-permute-start.12 = (bf16[128,1792]{1,0:T(8,128)(2,1)S(1)}, bf16[128,1792]{1,0:T(8,128)(2,1)S(1)}, u32[]{:S(2)}, u32[]{:S(2)}) collective-permute-start(bf16[128,1792]{1,0:T(8,128)(2,1)S(1)} %join.7.near_ref), channel_id=1, source_target_pairs={{0,8},{1,9},{2,10},{3,11},{4,12},{5,13},{6,14},{7,15},{8,0},{9,1},... | collective-permute-start | bytes 1376264 | tf_op jit(solution)/shard_map/ppermute | solution.py:531
  158.5 10.2 %collective-permute-start.38 = (bf16[128,2048]{1,0:T(8,128)(2,1)S(1)}, bf16[128,2048]{1,0:T(8,128)(2,1)S(1)}, u32[]{:S(2)}, u32[]{:S(2)}) collective-permute-start(bf16[128,2048]{1,0:T(8,128)(2,1)S(1)} %get-tuple-element.72), channel_id=1, source_target_pairs={{0,1},{1,0},{2,3},{3,2},{4,5},{5,4},{6,7},{7,6},{8,9},{9,8},{10,11... | collective-permute-start | bytes 1572872 | tf_op jit(solution)/shard_map/ppermute | solution.py:531
  162.1 4.5 %copy-start.1 = (bf16[128,1024]{1,0:T(8,128)(2,1)S(1)}, bf16[128,1024]{1,0:T(8,128)(2,1)}, u32[]{:S(2)}) copy-start(bf16[128,1024]{1,0:T(8,128)(2,1)} %rows_ref.1) | copy-start | bytes 786436
  166.0 8.0 %collective-permute-start.17 = (bf16[128,2048]{1,0:T(8,128)(2,1)S(1)}, bf16[128,2048]{1,0:T(8,128)(2,1)S(1)}, u32[]{:S(2)}, u32[]{:S(2)}) collective-permute-start(bf16[128,2048]{1,0:T(8,128)(2,1)S(1)} %get-tuple-element.56), channel_id=1, source_target_pairs={{0,1},{1,0},{2,3},{3,2},{4,5},{5,4},{6,7},{7,6},{8,9},{9,8},{10,11... | collective-permute-start | bytes 1572872 | tf_op jit(solution)/shard_map/ppermute | solution.py:531
  167.1 8.4 %collective-permute-start.48 = (bf16[64,1024]{1,0:T(8,128)(2,1)S(1)}, bf16[64,1024]{1,0:T(8,128)(2,1)S(1)}, u32[]{:S(2)}, u32[]{:S(2)}) collective-permute-start(bf16[64,1024]{1,0:T(8,128)(2,1)S(1)} %take_rows.1.rows_ref.near_ref), channel_id=1, source_target_pairs={{0,8},{1,9},{2,10},{3,11},{4,12},{5,13},{6,14},{7,15},{8,0},{9,1},... | collective-permute-start | bytes 393224 | tf_op jit(solution)/shard_map/ppermute | solution.py:531
  168.9 9.5 %collective-permute-start.39 = (bf16[32,2048]{1,0:T(8,128)(2,1)S(1)}, bf16[32,2048]{1,0:T(8,128)(2,1)S(1)}, u32[]{:S(2)}, u32[]{:S(2)}) collective-permute-start(bf16[32,2048]{1,0:T(8,128)(2,1)S(1)} %get-tuple-element.74), channel_id=1, source_target_pairs={{0,2},{1,3},{2,0},{3,1},{4,6},{5,7},{6,4},{7,5},{8,10},{9,11},{10,... | collective-permute-start | bytes 393224 | tf_op jit(solution)/shard_map/ppermute | solution.py:531
  172.9 12.9 %collective-permute-start.40 = (bf16[32,2048]{1,0:T(8,128)(2,1)S(1)}, bf16[32,2048]{1,0:T(8,128)(2,1)S(1)}, u32[]{:S(2)}, u32[]{:S(2)}) collective-permute-start(bf16[32,2048]{1,0:T(8,128)(2,1)S(1)} %get-tuple-element.75), channel_id=1, source_target_pairs={{0,4},{1,5},{2,6},{3,7},{4,0},{5,1},{6,2},{7,3},{8,12},{9,13},{10,... | collective-permute-start | bytes 393224 | tf_op jit(solution)/shard_map/ppermute | solution.py:531
  174.0 14.2 %collective-permute-start.41 = (bf16[32,2048]{1,0:T(8,128)(2,1)S(1)}, bf16[32,2048]{1,0:T(8,128)(2,1)S(1)}, u32[]{:S(2)}, u32[]{:S(2)}) collective-permute-start(bf16[32,2048]{1,0:T(8,128)(2,1)S(1)} %get-tuple-element.76), channel_id=1, source_target_pairs={{0,6},{1,7},{2,4},{3,5},{4,2},{5,3},{6,0},{7,1},{8,14},{9,15},{10,... | collective-permute-start | bytes 393224 | tf_op jit(solution)/shard_map/ppermute | solution.py:531
  175.5 14.4 %collective-permute-start.18 = (bf16[32,2048]{1,0:T(8,128)(2,1)S(1)}, bf16[32,2048]{1,0:T(8,128)(2,1)S(1)}, u32[]{:S(2)}, u32[]{:S(2)}) collective-permute-start(bf16[32,2048]{1,0:T(8,128)(2,1)S(1)} %get-tuple-element.58), channel_id=1, source_target_pairs={{0,2},{1,3},{2,0},{3,1},{4,6},{5,7},{6,4},{7,5},{8,10},{9,11},{10,... | collective-permute-start | bytes 393224 | tf_op jit(solution)/shard_map/ppermute | solution.py:531
  178.3 21.5 %collective-permute-start.19 = (bf16[32,2048]{1,0:T(8,128)(2,1)S(1)}, bf16[32,2048]{1,0:T(8,128)(2,1)S(1)}, u32[]{:S(2)}, u32[]{:S(2)}) collective-permute-start(bf16[32,2048]{1,0:T(8,128)(2,1)S(1)} %get-tuple-element.59), channel_id=1, source_target_pairs={{0,4},{1,5},{2,6},{3,7},{4,0},{5,1},{6,2},{7,3},{8,12},{9,13},{10,... | collective-permute-start | bytes 393224 | tf_op jit(solution)/shard_map/ppermute | solution.py:531
  185.8 14.0 %collective-permute-start.20 = (bf16[32,2048]{1,0:T(8,128)(2,1)S(1)}, bf16[32,2048]{1,0:T(8,128)(2,1)S(1)}, u32[]{:S(2)}, u32[]{:S(2)}) collective-permute-start(bf16[32,2048]{1,0:T(8,128)(2,1)S(1)} %get-tuple-element.60), channel_id=1, source_target_pairs={{0,6},{1,7},{2,4},{3,5},{4,2},{5,3},{6,0},{7,1},{8,14},{9,15},{10,... | collective-permute-start | bytes 393224 | tf_op jit(solution)/shard_map/ppermute | solution.py:531
  188.3 15.1 %collective-permute-start.49 = (bf16[128,1024]{1,0:T(8,128)(2,1)S(1)}, bf16[128,1024]{1,0:T(8,128)(2,1)S(1)}, u32[]{:S(2)}, u32[]{:S(2)}) collective-permute-start(bf16[128,1024]{1,0:T(8,128)(2,1)S(1)} %join.11.near_ref), channel_id=1, source_target_pairs={{0,16},{1,17},{2,18},{3,19},{4,20},{5,21},{6,22},{7,23},{8,24},{9,... | collective-permute-start | bytes 786440 | tf_op jit(solution)/shard_map/ppermute | solution.py:531
  189.9 12.7 %collective-permute-start.43 = (bf16[32,2048]{1,0:T(8,128)(2,1)S(1)}, bf16[32,2048]{1,0:T(8,128)(2,1)S(1)}, u32[]{:S(2)}, u32[]{:S(2)}) collective-permute-start(bf16[32,2048]{1,0:T(8,128)(2,1)S(1)} %sum_rows.4.refs_3_), channel_id=1, source_target_pairs={{0,0},{1,1},{2,8},{3,9},{4,16},{5,17},{6,24},{7,25},{8,2},{9,3},{1... | collective-permute-start | bytes 393224 | tf_op jit(solution)/shard_map/ppermute | solution.py:531
  200.6 2.0 collective-permute-start.44
  203.3 13.8 %collective-permute-start.53 = (bf16[64,1024]{1,0:T(8,128)(2,1)S(1)}, bf16[64,1024]{1,0:T(8,128)(2,1)S(1)}, u32[]{:S(2)}, u32[]{:S(2)}) collective-permute-start(bf16[64,1024]{1,0:T(8,128)(2,1)S(1)} %get-tuple-element.82.other_ref), channel_id=1, source_target_pairs={{0,1},{1,0},{2,3},{3,2},{4,5},{5,4},{6,7},{7,6},{8,9},{9,8},{10,11... | collective-permute-start | bytes 393224 | tf_op jit(solution)/shard_map/ppermute | solution.py:531
  203.6 27.9 %collective-permute-start.50 = (bf16[1024,256]{1,0:T(8,128)(2,1)S(1)}, bf16[1024,256]{1,0:T(8,128)(2,1)S(1)}, u32[]{:S(2)}, u32[]{:S(2)}) collective-permute-start(bf16[1024,256]{1,0:T(8,128)(2,1)S(1)} %turn.1.own_ref), channel_id=1, source_target_pairs={{0,1},{1,0},{2,3},{3,2},{4,5},{5,4},{6,7},{7,6},{8,9},{9,8},{10,11... | collective-permute-start | bytes 1572872 | tf_op jit(solution)/shard_map/ppermute | solution.py:531
  205.7 14.3 %collective-permute-start.45 = (bf16[64,1024]{1,0:T(8,128)(2,1)S(1)}, bf16[64,1024]{1,0:T(8,128)(2,1)S(1)}, u32[]{:S(2)}, u32[]{:S(2)}) collective-permute-start(bf16[64,1024]{1,0:T(8,128)(2,1)S(1)} %student_term.1.own_ref), channel_id=1, source_target_pairs={{0,2},{1,3},{2,0},{3,1},{4,6},{5,7},{6,4},{7,5},{8,10},{9,11},{10,... | collective-permute-start | bytes 393224 | tf_op jit(solution)/shard_map/ppermute | solution.py:531
  216.2 5.4 %collective-permute-start.51 = (bf16[64,1024]{1,0:T(8,128)(2,1)S(1)}, bf16[64,1024]{1,0:T(8,128)(2,1)S(1)}, u32[]{:S(2)}, u32[]{:S(2)}) collective-permute-start(bf16[64,1024]{1,0:T(8,128)(2,1)S(1)} %get-tuple-element.81.own_ref.near_ref), channel_id=1, source_target_pairs={{0,8},{1,9},{2,10},{3,11},{4,12},{5,13},{6,14},{7,15},{8,0},{9,1},... | collective-permute-start | bytes 393224 | tf_op jit(solution)/shard_map/ppermute | solution.py:531
  217.1 6.9 %collective-permute-start.54 = (bf16[64,1024]{1,0:T(8,128)(2,1)S(1)}, bf16[64,1024]{1,0:T(8,128)(2,1)S(1)}, u32[]{:S(2)}, u32[]{:S(2)}) collective-permute-start(bf16[64,1024]{1,0:T(8,128)(2,1)S(1)} %collective-permute-done.53.near_ref), channel_id=1, source_target_pairs={{0,16},{1,17},{2,18},{3,19},{4,20},{5,21},{6,22},{7,23},{8,24},{9,... | collective-permute-start | bytes 393224 | tf_op jit(solution)/shard_map/ppermute | solution.py:531
  220.0 8.6 %collective-permute-start.46 = (bf16[64,1024]{1,0:T(8,128)(2,1)S(1)}, bf16[64,1024]{1,0:T(8,128)(2,1)S(1)}, u32[]{:S(2)}, u32[]{:S(2)}) collective-permute-start(bf16[64,1024]{1,0:T(8,128)(2,1)S(1)} %sum_rows.6.own_ref), channel_id=1, source_target_pairs={{0,4},{1,5},{2,6},{3,7},{4,0},{5,1},{6,2},{7,3},{8,12},{9,13},{10,... | collective-permute-start | bytes 393224 | tf_op jit(solution)/shard_map/ppermute | solution.py:531
  221.6 9.8 %collective-permute-start.52 = (bf16[128,1024]{1,0:T(8,128)(2,1)S(1)}, bf16[128,1024]{1,0:T(8,128)(2,1)S(1)}, u32[]{:S(2)}, u32[]{:S(2)}) collective-permute-start(bf16[128,1024]{1,0:T(8,128)(2,1)S(1)} %join.12.refs_0_), channel_id=1, source_target_pairs={{0,16},{1,17},{2,18},{3,19},{4,20},{5,21},{6,22},{7,23},{8,24},{9,... | collective-permute-start | bytes 786440 | tf_op jit(solution)/shard_map/ppermute | solution.py:531
  224.0 7.4 %collective-permute-start.55 = (bf16[128,1024]{1,0:T(8,128)(2,1)S(1)}, bf16[128,1024]{1,0:T(8,128)(2,1)S(1)}, u32[]{:S(2)}, u32[]{:S(2)}) collective-permute-start(bf16[128,1024]{1,0:T(8,128)(2,1)S(1)} %join.13.refs_2_), channel_id=1, source_target_pairs={{0,8},{1,9},{2,10},{3,11},{4,12},{5,13},{6,14},{7,15},{8,0},{9,1},... | collective-permute-start | bytes 786440 | tf_op jit(solution)/shard_map/ppermute | solution.py:531
  228.6 1.4 collective-permute-start.47

commit v3 on v2

--- a/solution.py
+++ b/solution.py
@@ -201,7 +201,8 @@
     )(near, far)
 
 
-def down_kernel(block, step, blocks, parts, first, last, at_ref, near_ref, far_ref, *refs):
+def down_kernel(block, step, lists, parts, first, last, at_ref, *refs):
+    pieces, refs = refs[: 2 * len(lists)], refs[2 * len(lists) :]
     w_refs, refs = refs[:parts], refs[parts:]
     if not first:
         before_ref, refs = refs[0], refs[1:]
@@ -212,11 +213,15 @@
 
     @pl.when(pl.program_id(0) == 0)
     def _():
-        half = len(blocks) // 2
-        for slot, at in enumerate(blocks):
-            ref = far_ref if slot >= half else near_ref
-            source = (slot % half) * block
-            lhs_ref[at * block : (at + 1) * block, :] = ref[source : source + block, :]
+        for chunk, blocks in enumerate(lists):
+            half = len(blocks) // 2
+            for slot, at in enumerate(blocks):
+                ref = pieces[2 * chunk + slot // half]
+                source = (slot % half) * block
+                column = chunk * ref.shape[1]
+                lhs_ref[at * block : (at + 1) * block, column : column + ref.shape[1]] = ref[
+                    source : source + block, :
+                ]
 
     part = w_refs[0].shape[0]
     total = 0.0
@@ -238,21 +243,20 @@
                 send_ref[row : row + step, :] = rows.astype(BF16)
 
 
-def down_product(at, near, far, weight, chunk, chunks, step, blocks, before, last):
-    rows = 2 * near.shape[0]
-    depth = weight.shape[0] // chunks
+def down_product(at, pieces, weight, chunk, chunks, step, lists, before, last):
+    rows = 2 * pieces[0].shape[0]
+    depth = len(lists) * (weight.shape[0] // chunks)
     width = weight.shape[1]
-    tile = tile_of(width)
-    whole = pl.BlockSpec(near.shape, lambda n: (0, 0))
+    tile = tile_of(width, 1024 // len(lists))
     full = pl.BlockSpec((rows, tile), lambda n: (0, n))
     half = pl.BlockSpec((rows // 2, tile), lambda n: (0, n))
-    in_specs = [pl.BlockSpec(memory_space=pltpu.SMEM), whole, whole]
-    parts = WEIGHT_PARTS
+    in_specs = [pl.BlockSpec(memory_space=pltpu.SMEM)]
+    in_specs += [whole_block(piece.shape) for piece in pieces]
+    parts = WEIGHT_PARTS * len(lists)
+    start = chunk * WEIGHT_PARTS
     for part in range(parts):
-        in_specs.append(
-            pl.BlockSpec((depth // parts, tile), lambda n, at=chunk * parts + part: (at, n))
-        )
-    operands = [at, near, far] + [weight] * parts
+        in_specs.append(pl.BlockSpec((depth // parts, tile), lambda n, at=start + part: (at, n)))
+    operands = [at, *pieces] + [weight] * parts
     if before is not None:
         in_specs.append(full)
         operands.append(before)
@@ -269,7 +273,7 @@
         out_specs = full
     return pl.pallas_call(
         functools.partial(
-            down_kernel, rows // len(blocks), step, blocks, parts, before is None, last
+            down_kernel, rows // len(lists[0]), step, lists, parts, before is None, last
         ),
         grid=(width // tile,),
         out_shape=out_shape,
@@ -278,7 +282,7 @@
         scratch_shapes=scratch,
         cost_estimate=cost(2 * rows * depth * width, 2 * depth * width + 2 * rows * depth),
         name="down_product",
-        compiler_params=room(14),
+        compiler_params=room(24),
     )(*operands)
 
 
@@ -575,10 +579,16 @@
     target_parts = []
     for r, step in enumerate(steps):
         x, squares = prepare(meta, gather_rows(r), gain)
-        for bit in bits[::-1]:
+        squares = squares.reshape(groups, squares.shape[0] // groups, 128)
+        for bit in bits if r else bits[::-1]:
             half = squares.shape[0] // 2
-            squares = squares[:half] + over_grp(squares[half:], 1 << bit)
+            keep, send = squares[:half], squares[half:]
+            if r:
+                keep, send = squares[::2], squares[1::2]
+            squares = keep + over_grp(send, 1 << bit)
+        squares = squares[0]
         before = None
+        pieces, lists = [], []
         for chunk in range(COL_CHUNKS):
             u = r * COL_CHUNKS + chunk
             order = orders[u % 2]
@@ -590,20 +600,22 @@
                 if stage < len(order) - 1:
                     keep, send = add_halves(keep, arrived)
             hidden = activate(keep, arrived, squares)
-            near, far_rows = gather(hidden, order)
+            pieces.extend(gather(hidden, order))
+            lists.append(gather_list(order))
             last = chunk == COL_CHUNKS - 1
-            before = down_product(
-                meta,
-                near,
-                far_rows,
-                down_weight,
-                chunk,
-                COL_CHUNKS,
-                step,
-                gather_list(order),
-                before,
-                last,
-            )
+            if last or r < len(steps) - 1:
+                before = down_product(
+                    meta,
+                    pieces,
+                    down_weight,
+                    chunk + 1 - len(lists),
+                    COL_CHUNKS,
+                    step,
+                    lists,
+                    before,
+                    last,
+                )
+                pieces, lists = [], []
         keep, send = before
         result, *sends = split(keep, over_inner(send, 1), depth)
         others = [over_inner(sends[far - 1], 2 * far) for far in range(1, depth)]

time: 235 us -> 246 us (1.047)
  waiting for transfers between devices: 100 us -> 110 us
    ppermute x56, waiting for transfers between devices: 100 us -> 110 us  [move(): return lax.ppermute(value, AXES, pairs)]
    pallas_call x4 -> x3, Pallas kernels: 14.6 us -> 14.1 us  [down_product(): pl.pallas_call(functools.partial(down_kernel, rows // len(lists[0]), step...]
  transfers between devices with their start and end apart: 56 -> 56, of which waited for: 17 -> 18; matrix products, arithmetic and copies ran while one was open for 0% -> 0% of each run, Pallas kernels for 24% -> 23%
where the time goes in v3:
time: 246 us
  waiting for transfers between devices  110 us (45%)
  starting transfers between devices  72.6 us (30%)
  Pallas kernels  60 us (24%)
    ppermute x56, waiting for transfers between devices, move(): return lax.ppermute(value, AXES, pairs)  110 us
    ppermute x56, starting transfers between devices, move(): return lax.ppermute(value, AXES, pairs)  72.6 us
    pallas_call x4, Pallas kernels, up_product(): pl.pallas_call(functools.partial(up_kernel, rows // len(blocks), blocks,...  30.9 us
    pallas_call x3, Pallas kernels, down_product(): pl.pallas_call(functools.partial(down_kernel, rows // len(lists[0]), step...  14.1 us
  transfers between devices with their start and end apart: 56, of which 18 were waited for; matrix products, arithmetic and copies ran while one was open for 0% of the time, Pallas kernels for 23%

profile of v3, /device:TPU:0, one launch (start us, length us, event | category | flops | bytes accessed | tf_op | source)
XLA Modules:
  0.0 245.7 jit_solution(15113917496940962450)
XLA Ops:
  0.7 1.0 fusion.2
  2.3 2.6 %collective-permute-start.1 = (bf16[32,2048]{1,0:T(8,128)(2,1)S(1)}, bf16[32,2048]{1,0:T(8,128)(2,1)S(1)}, u32[]{:S(2)}, u32[]{:S(2)}) collective-permute-start(bf16[32,2048]{1,0:T(8,128)(2,1)S(1)} %get-tuple-element.84.refs_0_), channel_id=1, source_target_pairs={{0,2},{1,3},{2,0},{3,1},{4,6},{5,7},{6,4},{7,5},{8,10},{9,11},{10,... | collective-permute-start | bytes 393224 | tf_op jit(solution)/shard_map/ppermute | solution.py:535
  4.9 2.6 %collective-permute-start.3 = (bf16[32,2048]{1,0:T(8,128)(2,1)S(1)}, bf16[32,2048]{1,0:T(8,128)(2,1)S(1)}, u32[]{:S(2)}, u32[]{:S(2)}) collective-permute-start(bf16[32,2048]{1,0:T(8,128)(2,1)S(1)} %get-tuple-element.84.refs_0_), channel_id=1, source_target_pairs={{0,4},{1,5},{2,6},{3,7},{4,0},{5,1},{6,2},{7,3},{8,12},{9,13},{10,... | collective-permute-start | bytes 393224 | tf_op jit(solution)/shard_map/ppermute | solution.py:535
  7.5 0.9 collective-permute-start.22
  8.4 3.5 %collective-permute-start.24 = (bf16[32,2048]{1,0:T(8,128)(2,1)S(1)}, bf16[32,2048]{1,0:T(8,128)(2,1)S(1)}, u32[]{:S(2)}, u32[]{:S(2)}) collective-permute-start(bf16[32,2048]{1,0:T(8,128)(2,1)S(1)} %get-tuple-element.83.refs_0_), channel_id=1, source_target_pairs={{0,4},{1,5},{2,6},{3,7},{4,0},{5,1},{6,2},{7,3},{8,12},{9,13},{10,... | collective-permute-start | bytes 393224 | tf_op jit(solution)/shard_map/ppermute | solution.py:535
  11.9 3.0 %collective-permute-start.26 = (bf16[32,2048]{1,0:T(8,128)(2,1)S(1)}, bf16[32,2048]{1,0:T(8,128)(2,1)S(1)}, u32[]{:S(2)}, u32[]{:S(2)}) collective-permute-start(bf16[32,2048]{1,0:T(8,128)(2,1)S(1)} %get-tuple-element.83.refs_0_), channel_id=1, source_target_pairs={{0,6},{1,7},{2,4},{3,5},{4,2},{5,3},{6,0},{7,1},{8,14},{9,15},{10,... | collective-permute-start | bytes 393224 | tf_op jit(solution)/shard_map/ppermute | solution.py:535
  14.9 3.0 %collective-permute-done.3.refs_4_ = bf16[32,2048]{1,0:T(8,128)(2,1)S(1)} collective-permute-done((bf16[32,2048]{1,0:T(8,128)(2,1)S(1)}, bf16[32,2048]{1,0:T(8,128)(2,1)S(1)}, u32[]{:S(2)}, u32[]{:S(2)}) %collective-permute-start.3) | collective-permute-done | bytes 131104 | tf_op jit(solution)/shard_map/ppermute | solution.py:535
  18.4 0.7 broadcast_in_dim.3.refs_8_
  19.1 10.0 %collective-permute-done.24.refs_4_ = bf16[32,2048]{1,0:T(8,128)(2,1)S(1)} collective-permute-done((bf16[32,2048]{1,0:T(8,128)(2,1)S(1)}, bf16[32,2048]{1,0:T(8,128)(2,1)S(1)}, u32[]{:S(2)}, u32[]{:S(2)}) %collective-permute-start.24) | collective-permute-done | bytes 131104 | tf_op jit(solution)/shard_map/ppermute | solution.py:535
  30.1 1.0 prepare.2
  31.1 7.7 %up_product.4 = (bf16[2,128,1792]{2,1,0:T(8,128)(2,1)S(1)}, bf16[2,128,1792]{2,1,0:T(8,128)(2,1)S(1)}) custom-call(bf16[256,2048]{1,0:T(8,128)(2,1)S(1)} %get-tuple-element.45.x_ref, bf16[2,2048,3584]{2,1,0:T(8,128)(2,1)} %source_ref.7), custom_call_target="tpu_custom_call" | custom-call | flops 3758096384 | bytes 15728640 | tf_op jit(solution)/shard_map/up_product/pallas_call | solution.py:119
  38.8 1.6 collective-permute-start.7
  40.4 1.0 prepare.3
  41.4 7.7 %up_product.7 = (bf16[2,128,1792]{2,1,0:T(8,128)(2,1)S(1)}, bf16[2,128,1792]{2,1,0:T(8,128)(2,1)S(1)}) custom-call(bf16[256,2048]{1,0:T(8,128)(2,1)S(1)} %get-tuple-element.61.x_ref, bf16[2,2048,3584]{2,1,0:T(8,128)(2,1)} %source_ref.7), custom_call_target="tpu_custom_call" | custom-call | flops 3758096384 | bytes 15728640 | tf_op jit(solution)/shard_map/up_product/pallas_call | solution.py:119
  49.7 7.7 %up_product.6 = (bf16[2,128,1792]{2,1,0:T(8,128)(2,1)S(1)}, bf16[2,128,1792]{2,1,0:T(8,128)(2,1)S(1)}) custom-call(bf16[256,2048]{1,0:T(8,128)(2,1)S(1)} %get-tuple-element.61.x_ref, bf16[2,2048,3584]{2,1,0:T(8,128)(2,1)} %source_ref.7), custom_call_target="tpu_custom_call" | custom-call | flops 3758096384 | bytes 15728640 | tf_op jit(solution)/shard_map/up_product/pallas_call | solution.py:119
  57.3 1.6 collective-permute-start.28
  59.0 7.8 %up_product.5 = (bf16[2,128,1792]{2,1,0:T(8,128)(2,1)S(1)}, bf16[2,128,1792]{2,1,0:T(8,128)(2,1)S(1)}) custom-call(bf16[256,2048]{1,0:T(8,128)(2,1)S(1)} %get-tuple-element.45.x_ref, bf16[2,2048,3584]{2,1,0:T(8,128)(2,1)} %source_ref.7), custom_call_target="tpu_custom_call" | custom-call | flops 3758096384 | bytes 15728640 | tf_op jit(solution)/shard_map/up_product/pallas_call | solution.py:119
  67.3 13.5 %collective-permute-done.34.arrived_ref = bf16[2,128,1792]{2,1,0:T(8,128)(2,1)S(1)} collective-permute-done((bf16[2,128,1792]{2,1,0:T(8,128)(2,1)S(1)}, bf16[2,128,1792]{2,1,0:T(8,128)(2,1)S(1)}, u32[]{:S(2)}, u32[]{:S(2)}) %collective-permute-start.34) | collective-permute-done | bytes 917536 | tf_op jit(solution)/shard_map/ppermute | solution.py:535
  81.1 1.6 collective-permute-start.35
  83.3 26.8 %collective-permute-done.30 = f32[2,64,128]{2,1,0:T(8,128)S(1)} collective-permute-done((f32[2,64,128]{2,1,0:T(8,128)S(1)}, f32[2,64,128]{2,1,0:T(8,128)S(1)}, u32[]{:S(2)}, u32[]{:S(2)}) %collective-permute-start.30) | collective-permute-done | bytes 65568 | tf_op jit(solution)/shard_map/ppermute | solution.py:535
  110.1 1.6 collective-permute-start.31
  112.5 1.6 collective-permute-done.31
  114.1 1.5 collective-permute-start.29
  115.9 1.6 collective-permute-start.8
  118.7 1.6 collective-permute-start.36
  120.9 6.6 %collective-permute-done.29.arrived_ref = bf16[2,64,1792]{2,1,0:T(8,128)(2,1)S(1)} collective-permute-done((bf16[2,64,1792]{2,1,0:T(8,128)(2,1)S(1)}, bf16[2,64,1792]{2,1,0:T(8,128)(2,1)S(1)}, u32[]{:S(2)}, u32[]{:S(2)}) %collective-permute-start.29) | collective-permute-done | bytes 458784 | tf_op jit(solution)/shard_map/ppermute | solution.py:535
  127.9 11.5 %collective-permute-done.36.far_ref = bf16[64,1792]{1,0:T(8,128)(2,1)S(1)} collective-permute-done((bf16[64,1792]{1,0:T(8,128)(2,1)S(1)}, bf16[64,1792]{1,0:T(8,128)(2,1)S(1)}, u32[]{:S(2)}, u32[]{:S(2)}) %collective-permute-start.36) | collective-permute-done | bytes 229408 | tf_op jit(solution)/shard_map/ppermute | solution.py:535
  139.4 1.6 collective-permute-start.32
  142.0 1.6 collective-permute-start.11
  144.1 1.6 collective-permute-start.15
  145.6 2.3 collective-permute-done.32.far_ref
  148.0 1.6 collective-permute-start.33
  149.6 1.0 collective-permute-done.11.far_ref
  150.6 1.6 collective-permute-start.12
  152.2 10.4 %collective-permute-done.15.far_ref = bf16[64,1792]{1,0:T(8,128)(2,1)S(1)} collective-permute-done((bf16[64,1792]{1,0:T(8,128)(2,1)S(1)}, bf16[64,1792]{1,0:T(8,128)(2,1)S(1)}, u32[]{:S(2)}, u32[]{:S(2)}) %collective-permute-start.15) | collective-permute-done | bytes 229408 | tf_op jit(solution)/shard_map/ppermute | solution.py:535
  162.7 1.6 collective-permute-start.16
  164.3 3.5 %down_product.4.refs_4_ = f32[256,2048]{1,0:T(8,128)S(1)} custom-call(s32[4]{0:T(128)S(1)} %pad_add_fusion.at_ref.meta_ref, bf16[128,1792]{1,0:T(8,128)(2,1)S(1)} %join.10.refs_0_, bf16[128,1792]{1,0:T(8,128)(2,1)S(1)} %collective-permute-done.37.refs_1_, bf16[3584,2048]{1,0:T(8,128)(2,1)S(1)} %bitcast.12, bf16[3584,2048]{1,0:T(8,128)(2,1)S(1)} %bitcast.12), custom_call_target="tpu_custom_call" | custom-call | flops 1879048192 | bytes 8257536 | tf_op jit(solution)/shard_map/down_product/pallas_call | solution.py:274
  167.9 3.7 %down_product.5 = (f32[128,2048]{1,0:T(8,128)S(1)}, bf16[128,2048]{1,0:T(8,128)(2,1)S(1)}) custom-call(s32[4]{0:T(128)S(1)} %pad_add_fusion.at_ref.meta_ref, bf16[128,1792]{1,0:T(8,128)(2,1)S(1)} %join.9.refs_0_, bf16[128,1792]{1,0:T(8,128)(2,1)S(1)} %collective-permute-done.33.refs_1_, bf16[3584,2048]{1,0:T(8,128)(2,1)S(1)} %bitcast.12, ...), custom_call_target="tpu_custom_call" | custom-call | flops 1879048192 | bytes 8257536 | tf_op jit(solution)/shard_map/down_product/pallas_call | solution.py:274
  171.7 6.9 %down_product.3 = (f32[128,2048]{1,0:T(8,128)S(1)}, bf16[128,2048]{1,0:T(8,128)(2,1)S(1)}) custom-call(s32[4]{0:T(128)S(1)} %pad_add_fusion.at_ref.meta_ref, bf16[128,1792]{1,0:T(8,128)(2,1)S(1)} %join.7.refs_0_, bf16[128,1792]{1,0:T(8,128)(2,1)S(1)} %collective-permute-done.12.refs_1_, bf16[128,1792]{1,0:T(8,128)(2,1)S(1)} %join.8.refs_2_, ...), custom_call_target="tpu_custom_call" | custom-call | flops 3758096384 | bytes 16515072 | tf_op jit(solution)/shard_map/down_product/pallas_call | solution.py:274
  179.7 0.7 collective-permute-start.48
  180.4 2.8 %collective-permute-start.39 = (bf16[32,2048]{1,0:T(8,128)(2,1)S(1)}, bf16[32,2048]{1,0:T(8,128)(2,1)S(1)}, u32[]{:S(2)}, u32[]{:S(2)}) collective-permute-start(bf16[32,2048]{1,0:T(8,128)(2,1)S(1)} %get-tuple-element.74), channel_id=1, source_target_pairs={{0,2},{1,3},{2,0},{3,1},{4,6},{5,7},{6,4},{7,5},{8,10},{9,11},{10,... | collective-permute-start | bytes 393224 | tf_op jit(solution)/shard_map/ppermute | solution.py:535
  183.2 1.1 collective-permute-start.40
  184.4 1.4 collective-permute-start.41
  185.9 1.9 collective-permute-start.18
  187.8 1.5 collective-permute-done.39.refs_0_
  189.3 1.4 collective-permute-start.19
  190.7 5.5 %collective-permute-done.40.refs_1_ = bf16[32,2048]{1,0:T(8,128)(2,1)S(1)} collective-permute-done((bf16[32,2048]{1,0:T(8,128)(2,1)S(1)}, bf16[32,2048]{1,0:T(8,128)(2,1)S(1)}, u32[]{:S(2)}, u32[]{:S(2)}) %collective-permute-start.40) | collective-permute-done | bytes 131104 | tf_op jit(solution)/shard_map/ppermute | solution.py:535
  196.1 2.6 %collective-permute-start.20 = (bf16[32,2048]{1,0:T(8,128)(2,1)S(1)}, bf16[32,2048]{1,0:T(8,128)(2,1)S(1)}, u32[]{:S(2)}, u32[]{:S(2)}) collective-permute-start(bf16[32,2048]{1,0:T(8,128)(2,1)S(1)} %get-tuple-element.60), channel_id=1, source_target_pairs={{0,6},{1,7},{2,4},{3,5},{4,2},{5,3},{6,0},{7,1},{8,14},{9,15},{10,... | collective-permute-start | bytes 393224 | tf_op jit(solution)/shard_map/ppermute | solution.py:535
  198.7 1.6 collective-permute-start.49
  200.4 0.7 collective-permute-start.43
  201.0 9.2 %collective-permute-done.19.refs_1_ = bf16[32,2048]{1,0:T(8,128)(2,1)S(1)} collective-permute-done((bf16[32,2048]{1,0:T(8,128)(2,1)S(1)}, bf16[32,2048]{1,0:T(8,128)(2,1)S(1)}, u32[]{:S(2)}, u32[]{:S(2)}) %collective-permute-start.19) | collective-permute-done | bytes 131104 | tf_op jit(solution)/shard_map/ppermute | solution.py:535
  210.2 0.8 sum_rows.5
  211.7 1.5 predict.1
  214.7 1.5 student_term.1.own_ref
  216.2 9.5 %collective-permute-start.45 = (bf16[64,1024]{1,0:T(8,128)(2,1)S(1)}, bf16[64,1024]{1,0:T(8,128)(2,1)S(1)}, u32[]{:S(2)}, u32[]{:S(2)}) collective-permute-start(bf16[64,1024]{1,0:T(8,128)(2,1)S(1)} %student_term.1.own_ref), channel_id=1, source_target_pairs={{0,2},{1,3},{2,0},{3,1},{4,6},{5,7},{6,4},{7,5},{8,10},{9,11},{10,... | collective-permute-start | bytes 393224 | tf_op jit(solution)/shard_map/ppermute | solution.py:535
  225.8 2.0 collective-permute-start.51
  227.8 1.7 collective-permute-done.45.refs_0_
  229.5 1.8 collective-permute-start.46
  231.5 3.6 %collective-permute-start.52 = (bf16[128,1024]{1,0:T(8,128)(2,1)S(1)}, bf16[128,1024]{1,0:T(8,128)(2,1)S(1)}, u32[]{:S(2)}, u32[]{:S(2)}) collective-permute-start(bf16[128,1024]{1,0:T(8,128)(2,1)S(1)} %join.12.refs_0_), channel_id=1, source_target_pairs={{0,16},{1,17},{2,18},{3,19},{4,20},{5,21},{6,22},{7,23},{8,24},{9,... | collective-permute-start | bytes 786440 | tf_op jit(solution)/shard_map/ppermute | solution.py:535
  235.5 2.7 %collective-permute-done.46.refs_0_ = bf16[64,1024]{1,0:T(8,128)(2,1)S(1)} collective-permute-done((bf16[64,1024]{1,0:T(8,128)(2,1)S(1)}, bf16[64,1024]{1,0:T(8,128)(2,1)S(1)}, u32[]{:S(2)}, u32[]{:S(2)}) %collective-permute-start.46) | collective-permute-done | bytes 131104 | tf_op jit(solution)/shard_map/ppermute | solution.py:535
  238.3 1.3 collective-permute-done.47.other_ref
  239.6 1.4 place.1
  241.0 1.3 collective-permute-done.55.refs_3_
  242.3 3.4 %proj_product.1 = f32[1024,1024]{1,0:T(8,128)} custom-call(bf16[1024,256]{1,0:T(8,128)(2,1)S(1)} %turn.1.own_ref, bf16[1024,256]{1,0:T(8,128)(2,1)S(1)} %collective-permute-done.50.other_ref, bf16[128,1024]{1,0:T(8,128)(2,1)S(1)} %join.12.refs_0_, bf16[128,1024]{1,0:T(8,128)(2,1)S(1)} %collective-permute-done.52.refs_1_, ...), custom_call_target="tpu_custom_call" | custom-call | flops 1073741824 | bytes 5242880 | tf_op jit(solution)/shard_map/proj_product/pallas_call | solution.py:480
  (109 shorter events, 13.3 us)
Async XLA Ops:
  1.7 6.7 %collective-permute-start = (bf16[32,2048]{1,0:T(8,128)(2,1)S(1)}, bf16[32,2048]{1,0:T(8,128)(2,1)S(1)}, u32[]{:S(2)}, u32[]{:S(2)}) collective-permute-start(bf16[32,2048]{1,0:T(8,128)(2,1)S(1)} %get-tuple-element.84.refs_0_), channel_id=1, source_target_pairs={{0,1},{1,0},{2,3},{3,2},{4,5},{5,4},{6,7},{7,6},{8,9},{9,8},{10,11... | collective-permute-start | bytes 393224 | tf_op jit(solution)/shard_map/ppermute | solution.py:535
  2.3 9.6 %collective-permute-start.1 = (bf16[32,2048]{1,0:T(8,128)(2,1)S(1)}, bf16[32,2048]{1,0:T(8,128)(2,1)S(1)}, u32[]{:S(2)}, u32[]{:S(2)}) collective-permute-start(bf16[32,2048]{1,0:T(8,128)(2,1)S(1)} %get-tuple-element.84.refs_0_), channel_id=1, source_target_pairs={{0,2},{1,3},{2,0},{3,1},{4,6},{5,7},{6,4},{7,5},{8,10},{9,11},{10,... | collective-permute-start | bytes 393224 | tf_op jit(solution)/shard_map/ppermute | solution.py:535
  4.9 12.9 %collective-permute-start.3 = (bf16[32,2048]{1,0:T(8,128)(2,1)S(1)}, bf16[32,2048]{1,0:T(8,128)(2,1)S(1)}, u32[]{:S(2)}, u32[]{:S(2)}) collective-permute-start(bf16[32,2048]{1,0:T(8,128)(2,1)S(1)} %get-tuple-element.84.refs_0_), channel_id=1, source_target_pairs={{0,4},{1,5},{2,6},{3,7},{4,0},{5,1},{6,2},{7,3},{8,12},{9,13},{10,... | collective-permute-start | bytes 393224 | tf_op jit(solution)/shard_map/ppermute | solution.py:535
  7.5 10.3 %collective-permute-start.5 = (bf16[32,2048]{1,0:T(8,128)(2,1)S(1)}, bf16[32,2048]{1,0:T(8,128)(2,1)S(1)}, u32[]{:S(2)}, u32[]{:S(2)}) collective-permute-start(bf16[32,2048]{1,0:T(8,128)(2,1)S(1)} %get-tuple-element.84.refs_0_), channel_id=1, source_target_pairs={{0,6},{1,7},{2,4},{3,5},{4,2},{5,3},{6,0},{7,1},{8,14},{9,15},{10,... | collective-permute-start | bytes 393224 | tf_op jit(solution)/shard_map/ppermute | solution.py:535
  7.5 10.9 %collective-permute-start.22 = (bf16[32,2048]{1,0:T(8,128)(2,1)S(1)}, bf16[32,2048]{1,0:T(8,128)(2,1)S(1)}, u32[]{:S(2)}, u32[]{:S(2)}) collective-permute-start(bf16[32,2048]{1,0:T(8,128)(2,1)S(1)} %get-tuple-element.83.refs_0_), channel_id=1, source_target_pairs={{0,2},{1,3},{2,0},{3,1},{4,6},{5,7},{6,4},{7,5},{8,10},{9,11},{10,... | collective-permute-start | bytes 393224 | tf_op jit(solution)/shard_map/ppermute | solution.py:535
  8.4 20.7 %collective-permute-start.24 = (bf16[32,2048]{1,0:T(8,128)(2,1)S(1)}, bf16[32,2048]{1,0:T(8,128)(2,1)S(1)}, u32[]{:S(2)}, u32[]{:S(2)}) collective-permute-start(bf16[32,2048]{1,0:T(8,128)(2,1)S(1)} %get-tuple-element.83.refs_0_), channel_id=1, source_target_pairs={{0,4},{1,5},{2,6},{3,7},{4,0},{5,1},{6,2},{7,3},{8,12},{9,13},{10,... | collective-permute-start | bytes 393224 | tf_op jit(solution)/shard_map/ppermute | solution.py:535
  11.9 17.2 %collective-permute-start.26 = (bf16[32,2048]{1,0:T(8,128)(2,1)S(1)}, bf16[32,2048]{1,0:T(8,128)(2,1)S(1)}, u32[]{:S(2)}, u32[]{:S(2)}) collective-permute-start(bf16[32,2048]{1,0:T(8,128)(2,1)S(1)} %get-tuple-element.83.refs_0_), channel_id=1, source_target_pairs={{0,6},{1,7},{2,4},{3,5},{4,2},{5,3},{6,0},{7,1},{8,14},{9,15},{10,... | collective-permute-start | bytes 393224 | tf_op jit(solution)/shard_map/ppermute | solution.py:535
  17.8 11.8 %collective-permute-start.2 = (bf16[32,2048]{1,0:T(8,128)(2,1)S(1)}, bf16[32,2048]{1,0:T(8,128)(2,1)S(1)}, u32[]{:S(2)}, u32[]{:S(2)}) collective-permute-start(bf16[32,2048]{1,0:T(8,128)(2,1)S(1)} %collective-permute-done.1.refs_2_), channel_id=1, source_target_pairs={{0,1},{1,0},{2,3},{3,2},{4,5},{5,4},{6,7},{7,6},{8,9},{9,8},{10,11... | collective-permute-start | bytes 393224 | tf_op jit(solution)/shard_map/ppermute | solution.py:535
  17.8 11.8 %collective-permute-start.4 = (bf16[32,2048]{1,0:T(8,128)(2,1)S(1)}, bf16[32,2048]{1,0:T(8,128)(2,1)S(1)}, u32[]{:S(2)}, u32[]{:S(2)}) collective-permute-start(bf16[32,2048]{1,0:T(8,128)(2,1)S(1)} %collective-permute-done.3.refs_4_), channel_id=1, source_target_pairs={{0,1},{1,0},{2,3},{3,2},{4,5},{5,4},{6,7},{7,6},{8,9},{9,8},{10,11... | collective-permute-start | bytes 393224 | tf_op jit(solution)/shard_map/ppermute | solution.py:535
  18.4 11.8 %collective-permute-start.6 = (bf16[32,2048]{1,0:T(8,128)(2,1)S(1)}, bf16[32,2048]{1,0:T(8,128)(2,1)S(1)}, u32[]{:S(2)}, u32[]{:S(2)}) collective-permute-start(bf16[32,2048]{1,0:T(8,128)(2,1)S(1)} %collective-permute-done.5.refs_6_), channel_id=1, source_target_pairs={{0,1},{1,0},{2,3},{3,2},{4,5},{5,4},{6,7},{7,6},{8,9},{9,8},{10,11... | collective-permute-start | bytes 393224 | tf_op jit(solution)/shard_map/ppermute | solution.py:535
  29.1 11.3 %collective-permute-start.21 = (bf16[32,2048]{1,0:T(8,128)(2,1)S(1)}, bf16[32,2048]{1,0:T(8,128)(2,1)S(1)}, u32[]{:S(2)}, u32[]{:S(2)}) collective-permute-start(bf16[32,2048]{1,0:T(8,128)(2,1)S(1)} %get-tuple-element.83.refs_0_), channel_id=1, source_target_pairs={{0,1},{1,0},{2,3},{3,2},{4,5},{5,4},{6,7},{7,6},{8,9},{9,8},{10,11... | collective-permute-start | bytes 393224 | tf_op jit(solution)/shard_map/ppermute | solution.py:535
  29.1 11.3 %collective-permute-start.23 = (bf16[32,2048]{1,0:T(8,128)(2,1)S(1)}, bf16[32,2048]{1,0:T(8,128)(2,1)S(1)}, u32[]{:S(2)}, u32[]{:S(2)}) collective-permute-start(bf16[32,2048]{1,0:T(8,128)(2,1)S(1)} %collective-permute-done.22.refs_2_), channel_id=1, source_target_pairs={{0,1},{1,0},{2,3},{3,2},{4,5},{5,4},{6,7},{7,6},{8,9},{9,8},{10,11... | collective-permute-start | bytes 393224 | tf_op jit(solution)/shard_map/ppermute | solution.py:535
  29.6 10.8 %collective-permute-start.25 = (bf16[32,2048]{1,0:T(8,128)(2,1)S(1)}, bf16[32,2048]{1,0:T(8,128)(2,1)S(1)}, u32[]{:S(2)}, u32[]{:S(2)}) collective-permute-start(bf16[32,2048]{1,0:T(8,128)(2,1)S(1)} %collective-permute-done.24.refs_4_), channel_id=1, source_target_pairs={{0,1},{1,0},{2,3},{3,2},{4,5},{5,4},{6,7},{7,6},{8,9},{9,8},{10,11... | collective-permute-start | bytes 393224 | tf_op jit(solution)/shard_map/ppermute | solution.py:535
  29.7 10.7 %collective-permute-start.27 = (bf16[32,2048]{1,0:T(8,128)(2,1)S(1)}, bf16[32,2048]{1,0:T(8,128)(2,1)S(1)}, u32[]{:S(2)}, u32[]{:S(2)}) collective-permute-start(bf16[32,2048]{1,0:T(8,128)(2,1)S(1)} %collective-permute-done.26.refs_6_), channel_id=1, source_target_pairs={{0,1},{1,0},{2,3},{3,2},{4,5},{5,4},{6,7},{7,6},{8,9},{9,8},{10,11... | collective-permute-start | bytes 393224 | tf_op jit(solution)/shard_map/ppermute | solution.py:535
  38.8 76.8 %collective-permute-start.7 = (bf16[2,128,1792]{2,1,0:T(8,128)(2,1)S(1)}, bf16[2,128,1792]{2,1,0:T(8,128)(2,1)S(1)}, u32[]{:S(2)}, u32[]{:S(2)}) collective-permute-start(bf16[2,128,1792]{2,1,0:T(8,128)(2,1)S(1)} %get-tuple-element.47), channel_id=1, source_target_pairs={{0,8},{1,9},{2,10},{3,11},{4,12},{5,13},{6,14},{7,15},{8,0},{9,1},... | collective-permute-start | bytes 2752520 | tf_op jit(solution)/shard_map/ppermute | solution.py:535
  49.1 31.7 %collective-permute-start.34 = (bf16[2,128,1792]{2,1,0:T(8,128)(2,1)S(1)}, bf16[2,128,1792]{2,1,0:T(8,128)(2,1)S(1)}, u32[]{:S(2)}, u32[]{:S(2)}) collective-permute-start(bf16[2,128,1792]{2,1,0:T(8,128)(2,1)S(1)} %get-tuple-element.68), channel_id=1, source_target_pairs={{0,8},{1,9},{2,10},{3,11},{4,12},{5,13},{6,14},{7,15},{8,0},{9,1},... | collective-permute-start | bytes 2752520 | tf_op jit(solution)/shard_map/ppermute | solution.py:535
  57.3 54.4 %collective-permute-start.28 = (bf16[2,128,1792]{2,1,0:T(8,128)(2,1)S(1)}, bf16[2,128,1792]{2,1,0:T(8,128)(2,1)S(1)}, u32[]{:S(2)}, u32[]{:S(2)}) collective-permute-start(bf16[2,128,1792]{2,1,0:T(8,128)(2,1)S(1)} %get-tuple-element.63), channel_id=1, source_target_pairs={{0,16},{1,17},{2,18},{3,19},{4,20},{5,21},{6,22},{7,23},{8,24},{9,... | collective-permute-start | bytes 2752520 | tf_op jit(solution)/shard_map/ppermute | solution.py:535
  59.0 105.3 %slice-start = ((s8[14680064]{0:T(1024)(128)(4,1)}), s8[4194304]{0:T(1024)(128)(4,1)S(1)}, s32[]{:S(2)}) async-start(s8[14680064]{0:T(1024)(128)(4,1)} %bitcast.11), calls=%async_computation | async-start | bytes 8388608
  59.0 105.3 %slice-start.1 = ((s8[14680064]{0:T(1024)(128)(4,1)}), s8[4194304]{0:T(1024)(128)(4,1)S(1)}, s32[]{:S(2)}) async-start(s8[14680064]{0:T(1024)(128)(4,1)} %bitcast.11), calls=%async_computation.1 | async-start | bytes 8388608
  59.0 105.3 %slice-start.2 = ((s8[14680064]{0:T(1024)(128)(4,1)}), s8[4194304]{0:T(1024)(128)(4,1)S(1)}, s32[]{:S(2)}) async-start(s8[14680064]{0:T(1024)(128)(4,1)} %bitcast.11), calls=%async_computation.2 | async-start | bytes 8388608
  66.8 50.6 %collective-permute-start.13 = (bf16[2,128,1792]{2,1,0:T(8,128)(2,1)S(1)}, bf16[2,128,1792]{2,1,0:T(8,128)(2,1)S(1)}, u32[]{:S(2)}, u32[]{:S(2)}) collective-permute-start(bf16[2,128,1792]{2,1,0:T(8,128)(2,1)S(1)} %get-tuple-element.52), channel_id=1, source_target_pairs={{0,16},{1,17},{2,18},{3,19},{4,20},{5,21},{6,22},{7,23},{8,24},{9,... | collective-permute-start | bytes 2752520 | tf_op jit(solution)/shard_map/ppermute | solution.py:535
  81.1 46.4 %copy-start = (bf16[1024,1024]{1,0:T(8,128)(2,1)S(1)}, bf16[1024,1024]{1,0:T(8,128)(2,1)}, u32[]{:S(2)}) copy-start(bf16[1024,1024]{1,0:T(8,128)(2,1)} %proj_ref.3) | copy-start | bytes 6291460
  81.1 37.2 %collective-permute-start.35 = (bf16[2,64,1792]{2,1,0:T(8,128)(2,1)S(1)}, bf16[2,64,1792]{2,1,0:T(8,128)(2,1)S(1)}, u32[]{:S(2)}, u32[]{:S(2)}) collective-permute-start(bf16[2,64,1792]{2,1,0:T(8,128)(2,1)S(1)} %get-tuple-element.70), channel_id=1, source_target_pairs={{0,16},{1,17},{2,18},{3,19},{4,20},{5,21},{6,22},{7,23},{8,24},{9,... | collective-permute-start | bytes 1376264 | tf_op jit(solution)/shard_map/ppermute | solution.py:535
  82.7 27.3 %collective-permute-start.30 = (f32[2,64,128]{2,1,0:T(8,128)S(1)}, f32[2,64,128]{2,1,0:T(8,128)S(1)}, u32[]{:S(2)}, u32[]{:S(2)}) collective-permute-start(f32[2,64,128]{2,1,0:T(8,128)S(1)} %bitcast.16), channel_id=1, source_target_pairs={{0,16},{1,17},{2,18},{3,19},{4,20},{5,21},{6,22},{7,23},{8,24},{9,... | collective-permute-start | bytes 196616 | tf_op jit(solution)/shard_map/ppermute | solution.py:535
  110.1 4.0 %collective-permute-start.31 = (f32[1,64,128]{2,1,0:T(8,128)S(1)}, f32[1,64,128]{2,1,0:T(8,128)S(1)}, u32[]{:S(2)}, u32[]{:S(2)}) collective-permute-start(f32[1,64,128]{2,1,0:T(8,128)S(1)} %slice.53), channel_id=1, source_target_pairs={{0,8},{1,9},{2,10},{3,11},{4,12},{5,13},{6,14},{7,15},{8,0},{9,1},... | collective-permute-start | bytes 98312 | tf_op jit(solution)/shard_map/ppermute | solution.py:535
  111.7 8.6 %collective-permute-start.9 = (f32[2,64,128]{2,1,0:T(8,128)S(1)}, f32[2,64,128]{2,1,0:T(8,128)S(1)}, u32[]{:S(2)}, u32[]{:S(2)}) collective-permute-start(f32[2,64,128]{2,1,0:T(8,128)S(1)} %slice.40), channel_id=1, source_target_pairs={{0,8},{1,9},{2,10},{3,11},{4,12},{5,13},{6,14},{7,15},{8,0},{9,1},... | collective-permute-start | bytes 196616 | tf_op jit(solution)/shard_map/ppermute | solution.py:535
  114.1 13.4 %collective-permute-start.29 = (bf16[2,64,1792]{2,1,0:T(8,128)(2,1)S(1)}, bf16[2,64,1792]{2,1,0:T(8,128)(2,1)S(1)}, u32[]{:S(2)}, u32[]{:S(2)}) collective-permute-start(bf16[2,64,1792]{2,1,0:T(8,128)(2,1)S(1)} %get-tuple-element.65), channel_id=1, source_target_pairs={{0,8},{1,9},{2,10},{3,11},{4,12},{5,13},{6,14},{7,15},{8,0},{9,1},... | collective-permute-start | bytes 1376264 | tf_op jit(solution)/shard_map/ppermute | solution.py:535
  115.9 25.7 %collective-permute-start.8 = (bf16[2,64,1792]{2,1,0:T(8,128)(2,1)S(1)}, bf16[2,64,1792]{2,1,0:T(8,128)(2,1)S(1)}, u32[]{:S(2)}, u32[]{:S(2)}) collective-permute-start(bf16[2,64,1792]{2,1,0:T(8,128)(2,1)S(1)} %get-tuple-element.49), channel_id=1, source_target_pairs={{0,16},{1,17},{2,18},{3,19},{4,20},{5,21},{6,22},{7,23},{8,24},{9,... | collective-permute-start | bytes 1376264 | tf_op jit(solution)/shard_map/ppermute | solution.py:535
  117.5 46.9 %slice-start.3 = ((s8[14680064]{0:T(1024)(128)(4,1)}), s8[2097152]{0:T(1024)(128)(4,1)S(1)}, s32[]{:S(2)}) async-start(s8[14680064]{0:T(1024)(128)(4,1)} %bitcast.11), calls=%async_computation.3 | async-start | bytes 4194304
  117.7 25.9 %collective-permute-start.14 = (bf16[2,64,1792]{2,1,0:T(8,128)(2,1)S(1)}, bf16[2,64,1792]{2,1,0:T(8,128)(2,1)S(1)}, u32[]{:S(2)}, u32[]{:S(2)}) collective-permute-start(bf16[2,64,1792]{2,1,0:T(8,128)(2,1)S(1)} %get-tuple-element.54), channel_id=1, source_target_pairs={{0,8},{1,9},{2,10},{3,11},{4,12},{5,13},{6,14},{7,15},{8,0},{9,1},... | collective-permute-start | bytes 1376264 | tf_op jit(solution)/shard_map/ppermute | solution.py:535
  118.7 20.7 %collective-permute-start.36 = (bf16[64,1792]{1,0:T(8,128)(2,1)S(1)}, bf16[64,1792]{1,0:T(8,128)(2,1)S(1)}, u32[]{:S(2)}, u32[]{:S(2)}) collective-permute-start(bf16[64,1792]{1,0:T(8,128)(2,1)S(1)} %activate.7.near_ref), channel_id=1, source_target_pairs={{0,8},{1,9},{2,10},{3,11},{4,12},{5,13},{6,14},{7,15},{8,0},{9,1},... | collective-permute-start | bytes 688136 | tf_op jit(solution)/shard_map/ppermute | solution.py:535
  120.3 20.7 %collective-permute-start.10 = (f32[1,64,128]{2,1,0:T(8,128)S(1)}, f32[1,64,128]{2,1,0:T(8,128)S(1)}, u32[]{:S(2)}, u32[]{:S(2)}) collective-permute-start(f32[1,64,128]{2,1,0:T(8,128)S(1)} %slice.51), channel_id=1, source_target_pairs={{0,16},{1,17},{2,18},{3,19},{4,20},{5,21},{6,22},{7,23},{8,24},{9,... | collective-permute-start | bytes 98312 | tf_op jit(solution)/shard_map/ppermute | solution.py:535
  127.5 84.2 %collective-permute-start.42 = (bf16[1024,1024]{1,0:T(8,128)(2,1)S(1)}, bf16[1024,1024]{1,0:T(8,128)(2,1)S(1)}, u32[]{:S(2)}, u32[]{:S(2)}) collective-permute-start(bf16[1024,1024]{1,0:T(8,128)(2,1)S(1)} %copy-done), channel_id=1, source_target_pairs={{0,1},{1,0},{2,3},{3,2},{4,5},{5,4},{6,7},{7,6},{8,9},{9,8},{10,11... | collective-permute-start | bytes 6291464 | tf_op jit(solution)/shard_map/ppermute | solution.py:535
  139.4 8.5 %collective-permute-start.32 = (bf16[64,1792]{1,0:T(8,128)(2,1)S(1)}, bf16[64,1792]{1,0:T(8,128)(2,1)S(1)}, u32[]{:S(2)}, u32[]{:S(2)}) collective-permute-start(bf16[64,1792]{1,0:T(8,128)(2,1)S(1)} %activate.6.near_ref), channel_id=1, source_target_pairs={{0,16},{1,17},{2,18},{3,19},{4,20},{5,21},{6,22},{7,23},{8,24},{9,... | collective-permute-start | bytes 688136 | tf_op jit(solution)/shard_map/ppermute | solution.py:535
  141.1 23.2 %collective-permute-start.37 = (bf16[128,1792]{1,0:T(8,128)(2,1)S(1)}, bf16[128,1792]{1,0:T(8,128)(2,1)S(1)}, u32[]{:S(2)}, u32[]{:S(2)}) collective-permute-start(bf16[128,1792]{1,0:T(8,128)(2,1)S(1)} %join.10.refs_0_), channel_id=1, source_target_pairs={{0,16},{1,17},{2,18},{3,19},{4,20},{5,21},{6,22},{7,23},{8,24},{9,... | collective-permute-start | bytes 1376264 | tf_op jit(solution)/shard_map/ppermute | solution.py:535
  142.0 8.5 %collective-permute-start.11 = (bf16[64,1792]{1,0:T(8,128)(2,1)S(1)}, bf16[64,1792]{1,0:T(8,128)(2,1)S(1)}, u32[]{:S(2)}, u32[]{:S(2)}) collective-permute-start(bf16[64,1792]{1,0:T(8,128)(2,1)S(1)} %activate.4.near_ref), channel_id=1, source_target_pairs={{0,8},{1,9},{2,10},{3,11},{4,12},{5,13},{6,14},{7,15},{8,0},{9,1},... | collective-permute-start | bytes 688136 | tf_op jit(solution)/shard_map/ppermute | solution.py:535
  144.1 18.6 %collective-permute-start.15 = (bf16[64,1792]{1,0:T(8,128)(2,1)S(1)}, bf16[64,1792]{1,0:T(8,128)(2,1)S(1)}, u32[]{:S(2)}, u32[]{:S(2)}) collective-permute-start(bf16[64,1792]{1,0:T(8,128)(2,1)S(1)} %activate.5.near_ref), channel_id=1, source_target_pairs={{0,16},{1,17},{2,18},{3,19},{4,20},{5,21},{6,22},{7,23},{8,24},{9,... | collective-permute-start | bytes 688136 | tf_op jit(solution)/shard_map/ppermute | solution.py:535
  148.0 19.9 %collective-permute-start.33 = (bf16[128,1792]{1,0:T(8,128)(2,1)S(1)}, bf16[128,1792]{1,0:T(8,128)(2,1)S(1)}, u32[]{:S(2)}, u32[]{:S(2)}) collective-permute-start(bf16[128,1792]{1,0:T(8,128)(2,1)S(1)} %join.9.refs_0_), channel_id=1, source_target_pairs={{0,8},{1,9},{2,10},{3,11},{4,12},{5,13},{6,14},{7,15},{8,0},{9,1},... | collective-permute-start | bytes 1376264 | tf_op jit(solution)/shard_map/ppermute | solution.py:535
  150.6 21.1 %collective-permute-start.12 = (bf16[128,1792]{1,0:T(8,128)(2,1)S(1)}, bf16[128,1792]{1,0:T(8,128)(2,1)S(1)}, u32[]{:S(2)}, u32[]{:S(2)}) collective-permute-start(bf16[128,1792]{1,0:T(8,128)(2,1)S(1)} %join.7.refs_0_), channel_id=1, source_target_pairs={{0,16},{1,17},{2,18},{3,19},{4,20},{5,21},{6,22},{7,23},{8,24},{9,... | collective-permute-start | bytes 1376264 | tf_op jit(solution)/shard_map/ppermute | solution.py:535
  162.7 9.0 %collective-permute-start.16 = (bf16[128,1792]{1,0:T(8,128)(2,1)S(1)}, bf16[128,1792]{1,0:T(8,128)(2,1)S(1)}, u32[]{:S(2)}, u32[]{:S(2)}) collective-permute-start(bf16[128,1792]{1,0:T(8,128)(2,1)S(1)} %join.8.refs_2_), channel_id=1, source_target_pairs={{0,8},{1,9},{2,10},{3,11},{4,12},{5,13},{6,14},{7,15},{8,0},{9,1},... | collective-permute-start | bytes 1376264 | tf_op jit(solution)/shard_map/ppermute | solution.py:535
  171.6 7.5 %copy-start.1 = (bf16[128,1024]{1,0:T(8,128)(2,1)S(1)}, bf16[128,1024]{1,0:T(8,128)(2,1)}, u32[]{:S(2)}) copy-start(bf16[128,1024]{1,0:T(8,128)(2,1)} %rows_ref.1) | copy-start | bytes 786436
  171.6 8.8 %collective-permute-start.38 = (bf16[128,2048]{1,0:T(8,128)(2,1)S(1)}, bf16[128,2048]{1,0:T(8,128)(2,1)S(1)}, u32[]{:S(2)}, u32[]{:S(2)}) collective-permute-start(bf16[128,2048]{1,0:T(8,128)(2,1)S(1)} %get-tuple-element.72), channel_id=1, source_target_pairs={{0,1},{1,0},{2,3},{3,2},{4,5},{5,4},{6,7},{7,6},{8,9},{9,8},{10,11... | collective-permute-start | bytes 1572872 | tf_op jit(solution)/shard_map/ppermute | solution.py:535
  178.6 5.8 %collective-permute-start.17 = (bf16[128,2048]{1,0:T(8,128)(2,1)S(1)}, bf16[128,2048]{1,0:T(8,128)(2,1)S(1)}, u32[]{:S(2)}, u32[]{:S(2)}) collective-permute-start(bf16[128,2048]{1,0:T(8,128)(2,1)S(1)} %get-tuple-element.56), channel_id=1, source_target_pairs={{0,1},{1,0},{2,3},{3,2},{4,5},{5,4},{6,7},{7,6},{8,9},{9,8},{10,11... | collective-permute-start | bytes 1572872 | tf_op jit(solution)/shard_map/ppermute | solution.py:535
  179.7 6.2 %collective-permute-start.48 = (bf16[64,1024]{1,0:T(8,128)(2,1)S(1)}, bf16[64,1024]{1,0:T(8,128)(2,1)S(1)}, u32[]{:S(2)}, u32[]{:S(2)}) collective-permute-start(bf16[64,1024]{1,0:T(8,128)(2,1)S(1)} %take_rows.1.rows_ref.near_ref), channel_id=1, source_target_pairs={{0,8},{1,9},{2,10},{3,11},{4,12},{5,13},{6,14},{7,15},{8,0},{9,1},... | collective-permute-start | bytes 393224 | tf_op jit(solution)/shard_map/ppermute | solution.py:535
  180.4 8.8 %collective-permute-start.39 = (bf16[32,2048]{1,0:T(8,128)(2,1)S(1)}, bf16[32,2048]{1,0:T(8,128)(2,1)S(1)}, u32[]{:S(2)}, u32[]{:S(2)}) collective-permute-start(bf16[32,2048]{1,0:T(8,128)(2,1)S(1)} %get-tuple-element.74), channel_id=1, source_target_pairs={{0,2},{1,3},{2,0},{3,1},{4,6},{5,7},{6,4},{7,5},{8,10},{9,11},{10,... | collective-permute-start | bytes 393224 | tf_op jit(solution)/shard_map/ppermute | solution.py:535
  183.2 12.9 %collective-permute-start.40 = (bf16[32,2048]{1,0:T(8,128)(2,1)S(1)}, bf16[32,2048]{1,0:T(8,128)(2,1)S(1)}, u32[]{:S(2)}, u32[]{:S(2)}) collective-permute-start(bf16[32,2048]{1,0:T(8,128)(2,1)S(1)} %get-tuple-element.75), channel_id=1, source_target_pairs={{0,4},{1,5},{2,6},{3,7},{4,0},{5,1},{6,2},{7,3},{8,12},{9,13},{10,... | collective-permute-start | bytes 393224 | tf_op jit(solution)/shard_map/ppermute | solution.py:535
  184.4 14.3 %collective-permute-start.41 = (bf16[32,2048]{1,0:T(8,128)(2,1)S(1)}, bf16[32,2048]{1,0:T(8,128)(2,1)S(1)}, u32[]{:S(2)}, u32[]{:S(2)}) collective-permute-start(bf16[32,2048]{1,0:T(8,128)(2,1)S(1)} %get-tuple-element.76), channel_id=1, source_target_pairs={{0,6},{1,7},{2,4},{3,5},{4,2},{5,3},{6,0},{7,1},{8,14},{9,15},{10,... | collective-permute-start | bytes 393224 | tf_op jit(solution)/shard_map/ppermute | solution.py:535
  185.9 14.5 %collective-permute-start.18 = (bf16[32,2048]{1,0:T(8,128)(2,1)S(1)}, bf16[32,2048]{1,0:T(8,128)(2,1)S(1)}, u32[]{:S(2)}, u32[]{:S(2)}) collective-permute-start(bf16[32,2048]{1,0:T(8,128)(2,1)S(1)} %get-tuple-element.58), channel_id=1, source_target_pairs={{0,2},{1,3},{2,0},{3,1},{4,6},{5,7},{6,4},{7,5},{8,10},{9,11},{10,... | collective-permute-start | bytes 393224 | tf_op jit(solution)/shard_map/ppermute | solution.py:535
  189.3 20.9 %collective-permute-start.19 = (bf16[32,2048]{1,0:T(8,128)(2,1)S(1)}, bf16[32,2048]{1,0:T(8,128)(2,1)S(1)}, u32[]{:S(2)}, u32[]{:S(2)}) collective-permute-start(bf16[32,2048]{1,0:T(8,128)(2,1)S(1)} %get-tuple-element.59), channel_id=1, source_target_pairs={{0,4},{1,5},{2,6},{3,7},{4,0},{5,1},{6,2},{7,3},{8,12},{9,13},{10,... | collective-permute-start | bytes 393224 | tf_op jit(solution)/shard_map/ppermute | solution.py:535
  196.1 14.1 %collective-permute-start.20 = (bf16[32,2048]{1,0:T(8,128)(2,1)S(1)}, bf16[32,2048]{1,0:T(8,128)(2,1)S(1)}, u32[]{:S(2)}, u32[]{:S(2)}) collective-permute-start(bf16[32,2048]{1,0:T(8,128)(2,1)S(1)} %get-tuple-element.60), channel_id=1, source_target_pairs={{0,6},{1,7},{2,4},{3,5},{4,2},{5,3},{6,0},{7,1},{8,14},{9,15},{10,... | collective-permute-start | bytes 393224 | tf_op jit(solution)/shard_map/ppermute | solution.py:535
  198.7 15.2 %collective-permute-start.49 = (bf16[128,1024]{1,0:T(8,128)(2,1)S(1)}, bf16[128,1024]{1,0:T(8,128)(2,1)S(1)}, u32[]{:S(2)}, u32[]{:S(2)}) collective-permute-start(bf16[128,1024]{1,0:T(8,128)(2,1)S(1)} %join.11.near_ref), channel_id=1, source_target_pairs={{0,16},{1,17},{2,18},{3,19},{4,20},{5,21},{6,22},{7,23},{8,24},{9,... | collective-permute-start | bytes 786440 | tf_op jit(solution)/shard_map/ppermute | solution.py:535
  200.4 12.8 %collective-permute-start.43 = (bf16[32,2048]{1,0:T(8,128)(2,1)S(1)}, bf16[32,2048]{1,0:T(8,128)(2,1)S(1)}, u32[]{:S(2)}, u32[]{:S(2)}) collective-permute-start(bf16[32,2048]{1,0:T(8,128)(2,1)S(1)} %sum_rows.4.refs_3_), channel_id=1, source_target_pairs={{0,0},{1,1},{2,8},{3,9},{4,16},{5,17},{6,24},{7,25},{8,2},{9,3},{1... | collective-permute-start | bytes 393224 | tf_op jit(solution)/shard_map/ppermute | solution.py:535
  211.0 2.2 collective-permute-start.44
  213.8 13.9 %collective-permute-start.53 = (bf16[64,1024]{1,0:T(8,128)(2,1)S(1)}, bf16[64,1024]{1,0:T(8,128)(2,1)S(1)}, u32[]{:S(2)}, u32[]{:S(2)}) collective-permute-start(bf16[64,1024]{1,0:T(8,128)(2,1)S(1)} %get-tuple-element.82.other_ref), channel_id=1, source_target_pairs={{0,1},{1,0},{2,3},{3,2},{4,5},{5,4},{6,7},{7,6},{8,9},{9,8},{10,11... | collective-permute-start | bytes 393224 | tf_op jit(solution)/shard_map/ppermute | solution.py:535
  214.1 26.8 %collective-permute-start.50 = (bf16[1024,256]{1,0:T(8,128)(2,1)S(1)}, bf16[1024,256]{1,0:T(8,128)(2,1)S(1)}, u32[]{:S(2)}, u32[]{:S(2)}) collective-permute-start(bf16[1024,256]{1,0:T(8,128)(2,1)S(1)} %turn.1.own_ref), channel_id=1, source_target_pairs={{0,1},{1,0},{2,3},{3,2},{4,5},{5,4},{6,7},{7,6},{8,9},{9,8},{10,11... | collective-permute-start | bytes 1572872 | tf_op jit(solution)/shard_map/ppermute | solution.py:535
  216.2 13.2 %collective-permute-start.45 = (bf16[64,1024]{1,0:T(8,128)(2,1)S(1)}, bf16[64,1024]{1,0:T(8,128)(2,1)S(1)}, u32[]{:S(2)}, u32[]{:S(2)}) collective-permute-start(bf16[64,1024]{1,0:T(8,128)(2,1)S(1)} %student_term.1.own_ref), channel_id=1, source_target_pairs={{0,2},{1,3},{2,0},{3,1},{4,6},{5,7},{6,4},{7,5},{8,10},{9,11},{10,... | collective-permute-start | bytes 393224 | tf_op jit(solution)/shard_map/ppermute | solution.py:535
  225.8 5.7 %collective-permute-start.51 = (bf16[64,1024]{1,0:T(8,128)(2,1)S(1)}, bf16[64,1024]{1,0:T(8,128)(2,1)S(1)}, u32[]{:S(2)}, u32[]{:S(2)}) collective-permute-start(bf16[64,1024]{1,0:T(8,128)(2,1)S(1)} %get-tuple-element.81.own_ref.near_ref), channel_id=1, source_target_pairs={{0,8},{1,9},{2,10},{3,11},{4,12},{5,13},{6,14},{7,15},{8,0},{9,1},... | collective-permute-start | bytes 393224 | tf_op jit(solution)/shard_map/ppermute | solution.py:535
  227.8 7.3 %collective-permute-start.54 = (bf16[64,1024]{1,0:T(8,128)(2,1)S(1)}, bf16[64,1024]{1,0:T(8,128)(2,1)S(1)}, u32[]{:S(2)}, u32[]{:S(2)}) collective-permute-start(bf16[64,1024]{1,0:T(8,128)(2,1)S(1)} %collective-permute-done.53.near_ref), channel_id=1, source_target_pairs={{0,16},{1,17},{2,18},{3,19},{4,20},{5,21},{6,22},{7,23},{8,24},{9,... | collective-permute-start | bytes 393224 | tf_op jit(solution)/shard_map/ppermute | solution.py:535
  229.5 8.6 %collective-permute-start.46 = (bf16[64,1024]{1,0:T(8,128)(2,1)S(1)}, bf16[64,1024]{1,0:T(8,128)(2,1)S(1)}, u32[]{:S(2)}, u32[]{:S(2)}) collective-permute-start(bf16[64,1024]{1,0:T(8,128)(2,1)S(1)} %sum_rows.6.own_ref), channel_id=1, source_target_pairs={{0,4},{1,5},{2,6},{3,7},{4,0},{5,1},{6,2},{7,3},{8,12},{9,13},{10,... | collective-permute-start | bytes 393224 | tf_op jit(solution)/shard_map/ppermute | solution.py:535
  231.5 9.5 %collective-permute-start.52 = (bf16[128,1024]{1,0:T(8,128)(2,1)S(1)}, bf16[128,1024]{1,0:T(8,128)(2,1)S(1)}, u32[]{:S(2)}, u32[]{:S(2)}) collective-permute-start(bf16[128,1024]{1,0:T(8,128)(2,1)S(1)} %join.12.refs_0_), channel_id=1, source_target_pairs={{0,16},{1,17},{2,18},{3,19},{4,20},{5,21},{6,22},{7,23},{8,24},{9,... | collective-permute-start | bytes 786440 | tf_op jit(solution)/shard_map/ppermute | solution.py:535
  235.1 7.2 %collective-permute-start.55 = (bf16[128,1024]{1,0:T(8,128)(2,1)S(1)}, bf16[128,1024]{1,0:T(8,128)(2,1)S(1)}, u32[]{:S(2)}, u32[]{:S(2)}) collective-permute-start(bf16[128,1024]{1,0:T(8,128)(2,1)S(1)} %join.13.refs_2_), channel_id=1, source_target_pairs={{0,8},{1,9},{2,10},{3,11},{4,12},{5,13},{6,14},{7,15},{8,0},{9,1},... | collective-permute-start | bytes 786440 | tf_op jit(solution)/shard_map/ppermute | solution.py:535
  238.2 1.4 collective-permute-start.47
